TPU v7x, 128 devices: a whole 4x4x4 slice. The times are simulated.
128 devices in a mesh: req: 32 (over y, z, core), tp: 4 (over x).
Axes of the slice: x: 4, y: 4, z: 4, core: 2. Of those that a mesh axis runs over, the one named last changes fastest.
Arguments:
- states: bfloat16 [64, 512, 1024], P('req', 'tp'), may hold values from -45 to 45
- lengths: int32 [64], P('req'), may hold values from 3 to 512, as said below
- w_qkv: bfloat16 [1024, 3, 1024], P(None, None, 'tp'), may hold values from -0.1875 to 0.1875
- b_qkv: float32 [3, 1024], P(None, 'tp'), may hold values from -3 to 3
- w_out: bfloat16 [1024, 1024], P('tp'), may hold values from -0.1875 to 0.1875
- b_out: float32 [1024], replicated, may hold values from -3 to 3
- ln1_gain: float32 [1024], replicated, may hold values from 0.1 to 1.9
- ln1_shift: float32 [1024], replicated, may hold values from -3 to 3
- w_up: bfloat16 [1024, 4096], P(None, 'tp'), may hold values from -0.1875 to 0.1875
- b_up: float32 [4096], P('tp'), may hold values from -3 to 3
- w_down: bfloat16 [4096, 1024], P('tp'), may hold values from -0.09375 to 0.09375
- b_down: float32 [1024], replicated, may hold values from -3 to 3
- ln2_gain: float32 [1024], replicated, may hold values from 0.1 to 1.9
- ln2_shift: float32 [1024], replicated, may hold values from -3 to 3
- index_rows: bfloat16 [524288, 1024], P(('req', 'tp')), may hold values from -0.1875 to 0.1875
- cand_ids: int32 [64, 64], P('req', 'tp'), may hold values from 0 to 524287
Outputs:
- hidden_out: bfloat16 [64, 512, 1024], P('req', 'tp')
- scores: float32 [64, 64], P('req', 'tp')
Inputs may be any that keep to these rules, and one draw needn't show every extreme that they name: Valid positions are the first lengths ones of a text; in every draw some text has 512.
All inputs are finite; a program needn't handle non-finite values.
Results may differ from a plain program's by a relative error of at most 0.015.
Values may be sent and summed in bfloat16 or wider, within the bound.
A program may use at most 128 MiB of HBM per device.

v0:
```python
import jax
import jax.numpy as jnp
from jax import lax
from jax.sharding import PartitionSpec as P

HEAD_DIM = 64
WINDOW = 512


layer_eps = 1e-05
norm_eps = 1e-06


def layer_norm(values, gain, shift):
    centre = values - jnp.mean(values, axis=-1, keepdims=True)
    spread = jnp.mean(centre * centre, axis=-1, keepdims=True)
    return centre * lax.rsqrt(spread + layer_eps) * gain + shift


def window_attention(queries_h, keys_h, values_h, length):
    seq_len = queries_h.shape[0]
    half_window = WINDOW // 2
    padding = ((half_window, half_window), (0, 0), (0, 0))
    keys_padded = jnp.pad(keys_h, padding)
    values_padded = jnp.pad(values_h, padding)
    scale_factor = HEAD_DIM ** (-0.5)

    def one_block(block_idx):
        blk_start = block_idx * WINDOW
        query_pos = blk_start + jnp.arange(WINDOW, dtype=jnp.int32)
        key_pos = blk_start - half_window + jnp.arange(2 * WINDOW, dtype=jnp.int32)
        keep_mask = (
            (jnp.abs(query_pos[:, None] - key_pos[None, :]) <= half_window)
            & (key_pos[None, :] >= 0)
            & (key_pos[None, :] < length)
        )
        logits = (
            jnp.einsum("qhe,khe->hqk", queries_h, keys_padded, preferred_element_type=jnp.float32)
            * scale_factor
        )
        logits = jnp.where(keep_mask[None], logits, jnp.float32(-1e30))
        top_val = jnp.max(logits, axis=-1, keepdims=True)
        expo = jnp.exp(logits - top_val)
        attn_weights = (expo / jnp.sum(expo, axis=-1, keepdims=True)).astype(jnp.bfloat16)
        context = jnp.einsum(
            "hqk,khe->qhe", attn_weights, values_padded, preferred_element_type=jnp.float32
        )
        context = jnp.where((query_pos < length)[:, None, None], context, jnp.float32(0.0))
        return context.astype(jnp.bfloat16)

    blocks = lax.map(one_block, jnp.arange(seq_len // WINDOW, dtype=jnp.int32))
    return blocks.reshape(seq_len, queries_h.shape[1] * HEAD_DIM)


def per_device(
    states,
    lengths,
    w_qkv,
    b_qkv,
    w_out,
    b_out,
    ln1_gain,
    ln1_shift,
    w_up,
    b_up,
    w_down,
    b_down,
    ln2_gain,
    ln2_shift,
    index_rows,
    cand_ids,
):
    tp_count = lax.axis_size("tp")
    tp_rank = lax.axis_index("tp")
    req_count = lax.axis_size("req")
    text_count, row_share, model_width = states.shape
    full_states = lax.all_gather(states, "tp", axis=1, tiled=True)
    seq_len = full_states.shape[1]
    local_width = w_qkv.shape[2]
    heads_here = local_width // HEAD_DIM
    projected = (
        jnp.einsum("tsd,dce->tsce", full_states, w_qkv, preferred_element_type=jnp.float32) + b_qkv
    ).astype(jnp.bfloat16)
    queries_h = projected[:, :, 0].reshape(text_count, seq_len, heads_here, HEAD_DIM)
    keys_h = projected[:, :, 1].reshape(text_count, seq_len, heads_here, HEAD_DIM)
    values_h = projected[:, :, 2].reshape(text_count, seq_len, heads_here, HEAD_DIM)

    def per_text(bundle):
        return window_attention(bundle[0], bundle[1], bundle[2], bundle[3])

    context = lax.map(per_text, (queries_h, keys_h, values_h, lengths))
    partial_value = jnp.einsum("tsk,kd->tsd", context, w_out, preferred_element_type=jnp.float32)
    attn_sum = lax.psum(partial_value.astype(jnp.bfloat16), "tp").astype(jnp.float32)
    normed_full = layer_norm(
        full_states.astype(jnp.float32) + attn_sum + b_out, ln1_gain, ln1_shift
    ).astype(jnp.bfloat16)
    normed_local = lax.dynamic_slice_in_dim(normed_full, tp_rank * row_share, row_share, 1)
    up_act = jax.nn.gelu(
        jnp.einsum("tsd,df->tsf", normed_full, w_up, preferred_element_type=jnp.float32) + b_up,
        approximate=False,
    ).astype(jnp.bfloat16)
    down_part = jnp.einsum("tsf,fd->tsd", up_act, w_down, preferred_element_type=jnp.float32)
    down_sum = lax.psum_scatter(
        down_part.astype(jnp.bfloat16), "tp", scatter_dimension=1, tiled=True
    ).astype(jnp.float32)
    hidden_out = layer_norm(
        normed_local.astype(jnp.float32) + down_sum + b_down, ln2_gain, ln2_shift
    ).astype(jnp.bfloat16)
    positions = tp_rank * row_share + jnp.arange(row_share, dtype=jnp.int32)
    is_valid = positions[None, :] < lengths[:, None]
    local_pool = jnp.sum(
        jnp.where(is_valid[:, :, None], hidden_out.astype(jnp.float32), jnp.float32(0.0)), axis=1
    )
    pooled = lax.psum(local_pool, "tp") / lengths.astype(jnp.float32)[:, None]
    query_vec = (
        pooled * lax.rsqrt(jnp.mean(pooled * pooled, axis=-1, keepdims=True) + norm_eps)
    ).astype(jnp.bfloat16)
    all_queries = lax.all_gather(query_vec, "req", axis=0, tiled=True)
    quarter = cand_ids.shape[1]
    gathered_ids = lax.all_gather(cand_ids, ("req", "tp"), axis=0, tiled=True)
    all_ids = (
        gathered_ids.reshape(req_count, tp_count, text_count, quarter)
        .transpose(0, 2, 1, 3)
        .reshape(req_count * text_count, tp_count * quarter)
    )
    rows_here = index_rows.shape[0]
    first_row = (lax.axis_index("req") * tp_count + tp_rank) * rows_here
    local_ids = all_ids - first_row
    is_owned = (local_ids >= 0) & (local_ids < rows_here)
    safe_ids = jnp.clip(local_ids, 0, rows_here - 1)
    fetched = jnp.take(index_rows, safe_ids.reshape(-1), axis=0).reshape(
        safe_ids.shape[0], safe_ids.shape[1], model_width
    )
    picked = jnp.einsum("td,tcd->tc", all_queries, fetched, preferred_element_type=jnp.float32)
    owner_terms = jnp.where(is_owned, picked, jnp.float32(0.0))
    owner_terms = (
        owner_terms.reshape(req_count, text_count, tp_count, quarter)
        .transpose(0, 2, 1, 3)
        .reshape(req_count * tp_count * text_count, quarter)
    )
    scores = lax.psum_scatter(owner_terms, ("req", "tp"), scatter_dimension=0, tiled=True)
    return (hidden_out, scores)


def solution(mesh):
    placed = (
        P("req", "tp", None),
        P("req"),
        P(None, None, "tp"),
        P(None, "tp"),
        P("tp", None),
        P(),
        P(),
        P(),
        P(None, "tp"),
        P("tp"),
        P("tp", None),
        P(),
        P(),
        P(),
        P(("req", "tp"), None),
        P("req", "tp"),
    )
    return jax.shard_map(
        per_device,
        mesh=mesh,
        in_specs=placed,
        out_specs=(P("req", "tp", None), P("req", "tp")),
        check_vma=False,
    )
```

profile of v0, /device:TPU:1, one launch (start us, length us, event | category | flops | bytes accessed | tf_op | source)
XLA Modules:
  0.0 362.5 jit_solution(10841223569805811967)
XLA Ops:
  8.0 35.7 %all-gather.4.cloned.1.call-done = bf16[2,512,1024]{2,1,0:T(8,128)(2,1)} async-done(((bf16[2,128,1024]{2,1,0:T(8,128)(2,1)}), bf16[2,512,1024]{2,1,0:T(8,128)(2,1)}) %all-gather.4.cloned.1.call-update) | async-done | bytes 2097168 | tf_op jit(solution)/shard_map/all_gather | solution.py:77
  43.7 3.9 %add_convert_fusion.1 = bf16[2,512,3,256]{1,3,2,0:T(8,128)(2,1)S(1)} fusion(f32[3,256]{1,0:T(4,128)} %param.21, bf16[1024,3,256]{2,0,1:T(8,128)(2,1)} %param.20, bf16[2,512,1024]{2,1,0:T(8,128)(2,1)} %all-gather.4.cloned.1.call-done), kind=kOutput, calls=%fused_computation.68 | convolution fusion | flops 1612185600 | bytes 5245952 | tf_op jit(solution)/shard_map/tsd,dce->tsce/dot_general | solution.py:82
  47.6 1.2 fusion.150
  48.8 33.0 %while.17 = (s32[]{:T(128)}, bf16[2,512,256]{1,2,0:T(8,128)(2,1)}, s32[2]{0:T(128)S(1)}, bf16[2,512,4,64]{1,3,2,0:T(8,128)(2,1)}, bf16[2,512,4,64]{1,3,2,0:T(8,1...) while((s32[]{:T(128)}, bf16[2,512,256]{1,2,0:T(8,128)(2,1)}, s32[2]{0:T(128)S(1)}, ...), condition=%wide.region_3.4_spmd, body=%wide.region_0.3_spmd.sunk | while | flops 552343040 | bytes 24671904 | solution.py:91
  52.0 6.9 %fusion.166 = (f32[4,512]{1,0:T(4,128)S(1)}, f32[4,512,1024]{2,1,0:T(8,128)}) fusion(pred[512,1024]{1,0:T(8,128)(4,1)S(1)} %fusion.165, bf16[512,4,64]{0,2,1:T(8,128)(2,1)S(1)} %get-tuple-element.195, bf16[2,512,4,64]{1,3,2,0:T(8,128)(2,1)} %get-tuple-element.217, s32[]{:T(128)} %get-tuple-element.206), kind=kOutput, calls=%fused_computation.171.clone.1 | convolution fusion | flops 276825088 | bytes 9445888 | tf_op jit(solution)/shard_map/while/body/eval_jaxpr/while/body/eval_jaxpr/sub | solution.py:43
  59.6 4.9 %fusion.167 = bf16[4,64,512]{2,1,0:T(8,128)(2,1)S(1)} fusion(f32[4,512,1024]{2,1,0:T(8,128)} %get-tuple-element.196, f32[4,512]{1,0:T(4,128)S(1)} %get-tuple-element.197, bf16[512,4,64]{0,2,1:T(8,128)(2,1)S(1)} %get-tuple-element.198, pred[512]{0:T(512)(128)(4,1)S(1)} %iota_compare_fusion.2), kind=kOutput, calls=%fused_computation.14.clone.1 | convolution fusion | flops 272891904 | bytes 8921600 | tf_op jit(solution)/shard_map/while/body/eval_jaxpr/while/body/eval_jaxpr/hqk,khe->qhe/dot_general | solution.py:45
  67.4 1.1 dynamic-slice_bitcast_fusion.3
  68.5 6.9 %fusion.166 = (f32[4,512]{1,0:T(4,128)S(1)}, f32[4,512,1024]{2,1,0:T(8,128)}) fusion(pred[512,1024]{1,0:T(8,128)(4,1)S(1)} %fusion.165, bf16[512,4,64]{0,2,1:T(8,128)(2,1)S(1)} %get-tuple-element.195, bf16[2,512,4,64]{1,3,2,0:T(8,128)(2,1)} %get-tuple-element.217, s32[]{:T(128)} %get-tuple-element.206), kind=kOutput, calls=%fused_computation.171.clone.1 | convolution fusion | flops 276825088 | bytes 9445888 | tf_op jit(solution)/shard_map/while/body/eval_jaxpr/while/body/eval_jaxpr/sub | solution.py:43
  76.1 4.9 %fusion.167 = bf16[4,64,512]{2,1,0:T(8,128)(2,1)S(1)} fusion(f32[4,512,1024]{2,1,0:T(8,128)} %get-tuple-element.196, f32[4,512]{1,0:T(4,128)S(1)} %get-tuple-element.197, bf16[512,4,64]{0,2,1:T(8,128)(2,1)S(1)} %get-tuple-element.198, pred[512]{0:T(512)(128)(4,1)S(1)} %iota_compare_fusion.2), kind=kOutput, calls=%fused_computation.14.clone.1 | convolution fusion | flops 272891904 | bytes 8921600 | tf_op jit(solution)/shard_map/while/body/eval_jaxpr/while/body/eval_jaxpr/hqk,khe->qhe/dot_general | solution.py:45
  81.8 3.2 convolution_convert_fusion
  85.3 58.6 %all-reduce.5.cloned.1.call-done = bf16[2,512,1024]{2,1,0:T(8,128)(2,1)} async-done(((bf16[2,512,1024]{2,1,0:T(8,128)(2,1)}), bf16[2,512,1024]{2,1,0:T(8,128)(2,1)}) %all-reduce.5.cloned.1.call-update) | async-done | bytes 2097168 | tf_op jit(solution)/shard_map/psum | solution.py:93
  143.9 3.1 fusion.54
  148.5 1.2 add_convert_fusion
  149.8 3.4 fusion.103
  153.2 12.5 %fusion.92 = bf16[2,512,1024]{2,1,0:T(8,128)(2,1)} fusion(bf16[1024,1024]{1,0:T(8,128)(2,1)S(1)} %copy-done.13, f32[2,512,1024]{2,1,0:T(8,128)S(1)} %get-tuple-element.149, f32[1024]{0:T(1024)S(1)} %copy-done.14, u8[512,1024]{1,0:T(8,128)(4,1)S(1)} %get-tuple-element.123, u8[512,1024]{1,0:T(8,128)(4,1)S(1)} %get-tuple-element.122), kind=kOutput, calls=%fused_computation.105 | convolution fusion | flops 2222981120 | bytes 9441280 | tf_op jit(solution)/shard_map/tsf,fd->tsd/dot_general | solution.py:102
  165.7 55.1 %all-gather = s32[128,2,16]{2,1,0:T(2,128)S(1)} all-gather(s32[1,2,16]{2,1,0:T(2,128)S(1)} %bitcast.89), channel_id=1, replica_groups=mesh['req'=32,'tp'=4] {'req','tp'}, dimensions={0}, use_global_device_ids=true | all-gather | bytes 16512 | tf_op jit(solution)/shard_map/all_gather | solution.py:120
  221.7 25.4 %gather_fusion = bf16[4096,1024]{1,0:T(8,128)(2,1)} fusion(bf16[4096,1024]{1,0:T(8,128)(2,1)} %param.32, s32[4096]{0:T(1024)S(1)} %broadcast_clamp_fusion), kind=kCustom, calls=%fused_computation | custom fusion | bytes 16793600 | tf_op jit(solution)/shard_map/jit(_take)/gather | solution.py:131
  247.2 1.5 fusion.104
  248.6 1.5 multiply_reduce_fusion.1
  250.2 2.4 select_reduce_fusion
  252.6 8.4 %psum.15 = f32[2,1024]{1,0:T(2,128)S(1)} all-reduce(f32[2,1024]{1,0:T(2,128)S(1)} %get-tuple-element.138), channel_id=1, replica_groups=mesh['req'=32,'tp'=4] {'tp'}, use_global_device_ids=true, to_apply=%region_11.12 | all-reduce | flops 2048 | bytes 16384 | tf_op jit(solution)/shard_map/psum | solution.py:114
  261.3 25.0 %all-gather.1 = bf16[32,2,1024]{2,1,0:T(2,128)(2,1)S(1)} all-gather(bf16[1,2,1024]{2,1,0:T(2,128)(2,1)S(1)} %fusion.108), channel_id=1, replica_groups=mesh['req'=32,'tp'=4] {'req'}, dimensions={0}, use_global_device_ids=true | all-gather | bytes 135168 | tf_op jit(solution)/shard_map/all_gather | solution.py:118
  286.4 4.7 %fusion.41 = f32[64,1,64]{2,1,0:T(1,128)S(1)} fusion(bf16[64,1024,1]{1,2,0:T(2,128)(2,1)S(1)} %reshape.275, bf16[64,64,1024]{2,1,0:T(8,128)(2,1)} %bitcast.75, pred[64,64]{1,0:T(8,128)(4,1)S(1)} %compare_and_fusion.1), kind=kOutput, calls=%fused_computation.38 | convolution fusion | flops 12582912 | bytes 8540160 | tf_op jit(solution)/shard_map/td,tcd->tc/dot_general | solution.py:134
  291.4 64.0 %all-reduce.2 = f32[256,16]{1,0:T(8,128)S(1)} all-reduce(f32[256,16]{1,0:T(8,128)S(1)} %bitcast.82), channel_id=3, replica_groups=mesh['req'=32,'tp'=4] {'req','tp'}, use_global_device_ids=true, to_apply=%region_13.14.clone | all-reduce | flops 4096 | bytes 32768
  (83 shorter events, 12.6 us)
Async XLA Ops:
  7.2 142.6 %copy-start = (bf16[1024,1024]{1,0:T(8,128)(2,1)S(1)}, bf16[1024,1024]{1,0:T(8,128)(2,1)}, u32[]{:S(2)}) copy-start(bf16[1024,1024]{1,0:T(8,128)(2,1)} %param.26) | copy-start | bytes 6291460
  7.2 36.5 %all-gather.4.cloned.1.call-start = ((), (), s32[]{:S(2)}) async-start(), calls=%async_computation.1 | async-start | bytes 2621440 | tf_op jit(solution)/shard_map/all_gather | solution.py:77
  7.9 136.0 %all-reduce.5.cloned.1.call-start = ((), (), s32[]{:S(2)}) async-start(), calls=%async_computation.2 | async-start | bytes 4194304 | tf_op jit(solution)/shard_map/psum | solution.py:93
  8.0 40.8 %copy-start.15 = (s32[2]{0:T(128)S(1)}, s32[2]{0:T(128)}, u32[]{:S(2)}) copy-start(s32[2]{0:T(128)} %param.19) | copy-start | bytes 28
  59.6 4.9 %copy-start.4 = (bf16[2,512,256]{1,2,0:T(8,128)(2,1)S(1)}, bf16[2,512,256]{1,2,0:T(8,128)(2,1)}, u32[]{:S(2)}) copy-start(bf16[2,512,256]{1,2,0:T(8,128)(2,1)} %get-tuple-element.207) | copy-start | bytes 1572868 | tf_op jit(solution)/shard_map/while
  64.5 0.8 copy-start.5
  76.0 4.9 %copy-start.4 = (bf16[2,512,256]{1,2,0:T(8,128)(2,1)S(1)}, bf16[2,512,256]{1,2,0:T(8,128)(2,1)}, u32[]{:S(2)}) copy-start(bf16[2,512,256]{1,2,0:T(8,128)(2,1)} %get-tuple-element.207) | copy-start | bytes 1572868 | tf_op jit(solution)/shard_map/while
  81.0 0.8 copy-start.5
  81.8 62.1 %copy-start.7 = (f32[1024]{0:T(1024)S(1)}, f32[1024]{0:T(1024)}, u32[]{:S(2)}) copy-start(f32[1024]{0:T(1024)} %param.23) | copy-start | bytes 12292
  85.1 63.4 %copy-start.10 = (f32[1024]{0:T(1024)S(1)}, f32[1024]{0:T(1024)}, u32[]{:S(2)}) copy-start(f32[1024]{0:T(1024)} %param.25) | copy-start | bytes 12292
  85.1 63.4 %copy-start.11 = (f32[1024]{0:T(1024)S(1)}, f32[1024]{0:T(1024)}, u32[]{:S(2)}) copy-start(f32[1024]{0:T(1024)} %param.24) | copy-start | bytes 12292
  85.1 162.1 %reduce-scatter.2.cloned.1.call-start = ((), (), s32[]{:S(2)}) async-start(), calls=%async_computation.3 | async-start | bytes 2621440 | tf_op jit(solution)/shard_map/reduce_scatter | solution.py:103
  143.9 3.1 copy-start.1
  143.9 3.5 copy-start.2
  148.4 1.3 copy-start.14
  149.8 3.4 copy-start.3
  149.8 3.4 copy-start.13
  153.2 12.5 %copy-start.12 = (s32[2,16]{1,0:T(2,128)S(1)}, s32[2,16]{1,0:T(2,128)}, u32[]{:S(2)}) copy-start(s32[2,16]{1,0:T(2,128)} %param.33) | copy-start | bytes 388
  221.6 25.5 %copy-start.6 = (f32[1024]{0:T(1024)S(1)}, f32[1024]{0:T(1024)}, u32[]{:S(2)}) copy-start(f32[1024]{0:T(1024)} %param.29) | copy-start | bytes 12292
  221.7 28.5 %copy-start.8 = (f32[1024]{0:T(1024)S(1)}, f32[1024]{0:T(1024)}, u32[]{:S(2)}) copy-start(f32[1024]{0:T(1024)} %param.31) | copy-start | bytes 12292
  221.7 28.5 %copy-start.9 = (f32[1024]{0:T(1024)S(1)}, f32[1024]{0:T(1024)}, u32[]{:S(2)}) copy-start(f32[1024]{0:T(1024)} %param.30) | copy-start | bytes 12292
Sparse Core Ops, SparseCore 0:
  9.7 34.0 all-gather.3
  85.2 58.6 all-reduce.4
  165.8 29.5 reduce-scatter.1
where the time goes:
time: 363 us
  blocking collectives  153 us (42%)
  waiting for transfers between devices  95 us (26%)
  matrix products  51.4 us (14%)
  local copies, waits for them, and re-layouts  33.3 us (9%)
  other arithmetic  15.6 us (4%)
  between operations  14.1 us (4%)
    unnamed x1, blocking collectives  64 us
    psum x1, waiting for transfers between devices, per_device(): lax.psum(partial_value.astype(jnp.bfloat16), 'tp').astype(jnp.float32)  58.6 us
    all_gather x1, blocking collectives, per_device(): gathered_ids = lax.all_gather(cand_ids, ('req', 'tp'), axis=0, tiled=True)  55.1 us
    all_gather x1, waiting for transfers between devices, per_device(): full_states = lax.all_gather(states, 'tp', axis=1, tiled=True)  35.7 us
    gather x1, local copies, waits for them, and re-layouts, per_device(): jnp.take(index_rows, safe_ids.reshape(-1), axis=0)  25.4 us
    all_gather x1, blocking collectives, per_device(): all_queries = lax.all_gather(query_vec, 'req', axis=0, tiled=True)  25 us
    sub x2, matrix products, one_block(): expo = jnp.exp(logits - top_val)  13.8 us
    dot_general x1, matrix products, per_device(): jnp.einsum('tsf,fd->tsd', up_act, w_down, preferred_element_type=jnp.floa...  12.5 us
  transfers between devices with their start and end apart: 3, of which 2 were waited for; matrix products, arithmetic and copies ran while one was open for 7% of the time, Pallas kernels for 0%

commit v1 on v0

--- a/solution.py
+++ b/solution.py
@@ -17,39 +17,30 @@
     return centre * lax.rsqrt(spread + layer_eps) * gain + shift
 
 
-def window_attention(queries_h, keys_h, values_h, length):
-    seq_len = queries_h.shape[0]
+def window_attention(queries_h, keys_h, values_h, lengths):
+    seq_len = queries_h.shape[1]
     half_window = WINDOW // 2
-    padding = ((half_window, half_window), (0, 0), (0, 0))
-    keys_padded = jnp.pad(keys_h, padding)
-    values_padded = jnp.pad(values_h, padding)
     scale_factor = HEAD_DIM ** (-0.5)
-
-    def one_block(block_idx):
-        blk_start = block_idx * WINDOW
-        query_pos = blk_start + jnp.arange(WINDOW, dtype=jnp.int32)
-        key_pos = blk_start - half_window + jnp.arange(2 * WINDOW, dtype=jnp.int32)
-        keep_mask = (
-            (jnp.abs(query_pos[:, None] - key_pos[None, :]) <= half_window)
-            & (key_pos[None, :] >= 0)
-            & (key_pos[None, :] < length)
-        )
-        logits = (
-            jnp.einsum("qhe,khe->hqk", queries_h, keys_padded, preferred_element_type=jnp.float32)
-            * scale_factor
-        )
-        logits = jnp.where(keep_mask[None], logits, jnp.float32(-1e30))
-        top_val = jnp.max(logits, axis=-1, keepdims=True)
-        expo = jnp.exp(logits - top_val)
-        attn_weights = (expo / jnp.sum(expo, axis=-1, keepdims=True)).astype(jnp.bfloat16)
-        context = jnp.einsum(
-            "hqk,khe->qhe", attn_weights, values_padded, preferred_element_type=jnp.float32
-        )
-        context = jnp.where((query_pos < length)[:, None, None], context, jnp.float32(0.0))
-        return context.astype(jnp.bfloat16)
-
-    blocks = lax.map(one_block, jnp.arange(seq_len // WINDOW, dtype=jnp.int32))
-    return blocks.reshape(seq_len, queries_h.shape[1] * HEAD_DIM)
+    pos = jnp.arange(seq_len, dtype=jnp.int32)
+    near = jnp.abs(pos[:, None] - pos[None, :]) <= half_window
+    keep_mask = near[None] & (pos[None, None, :] < lengths[:, None, None])
+    logits = (
+        jnp.einsum("tqhe,tkhe->thqk", queries_h, keys_h, preferred_element_type=jnp.float32)
+        * scale_factor
+    )
+    logits = jnp.where(keep_mask[:, None], logits, jnp.float32(-1e30))
+    top_val = jnp.max(logits, axis=-1, keepdims=True)
+    expo = jnp.exp(logits - top_val)
+    attn_weights = (expo / jnp.sum(expo, axis=-1, keepdims=True)).astype(jnp.bfloat16)
+    context = jnp.einsum(
+        "thqk,tkhe->tqhe", attn_weights, values_h, preferred_element_type=jnp.float32
+    )
+    context = jnp.where(
+        (pos[None, :] < lengths[:, None])[:, :, None, None], context, jnp.float32(0.0)
+    )
+    return context.astype(jnp.bfloat16).reshape(
+        queries_h.shape[0], seq_len, queries_h.shape[2] * HEAD_DIM
+    )
 
 
 def per_device(
@@ -73,7 +64,10 @@
     tp_count = lax.axis_size("tp")
     tp_rank = lax.axis_index("tp")
     req_count = lax.axis_size("req")
+    req_rank = lax.axis_index("req")
     text_count, row_share, model_width = states.shape
+    quarter = cand_ids.shape[1]
+    gathered_ids = lax.all_gather(cand_ids, ("req", "tp"), axis=0, tiled=True)
     full_states = lax.all_gather(states, "tp", axis=1, tiled=True)
     seq_len = full_states.shape[1]
     local_width = w_qkv.shape[2]
@@ -85,10 +79,7 @@
     keys_h = projected[:, :, 1].reshape(text_count, seq_len, heads_here, HEAD_DIM)
     values_h = projected[:, :, 2].reshape(text_count, seq_len, heads_here, HEAD_DIM)
 
-    def per_text(bundle):
-        return window_attention(bundle[0], bundle[1], bundle[2], bundle[3])
-
-    context = lax.map(per_text, (queries_h, keys_h, values_h, lengths))
+    context = window_attention(queries_h, keys_h, values_h, lengths)
     partial_value = jnp.einsum("tsk,kd->tsd", context, w_out, preferred_element_type=jnp.float32)
     attn_sum = lax.psum(partial_value.astype(jnp.bfloat16), "tp").astype(jnp.float32)
     normed_full = layer_norm(
@@ -116,22 +107,20 @@
         pooled * lax.rsqrt(jnp.mean(pooled * pooled, axis=-1, keepdims=True) + norm_eps)
     ).astype(jnp.bfloat16)
     all_queries = lax.all_gather(query_vec, "req", axis=0, tiled=True)
-    quarter = cand_ids.shape[1]
-    gathered_ids = lax.all_gather(cand_ids, ("req", "tp"), axis=0, tiled=True)
     all_ids = (
         gathered_ids.reshape(req_count, tp_count, text_count, quarter)
         .transpose(0, 2, 1, 3)
         .reshape(req_count * text_count, tp_count * quarter)
     )
     rows_here = index_rows.shape[0]
-    first_row = (lax.axis_index("req") * tp_count + tp_rank) * rows_here
+    first_row = (req_rank * tp_count + tp_rank) * rows_here
     local_ids = all_ids - first_row
     is_owned = (local_ids >= 0) & (local_ids < rows_here)
     safe_ids = jnp.clip(local_ids, 0, rows_here - 1)
-    fetched = jnp.take(index_rows, safe_ids.reshape(-1), axis=0).reshape(
-        safe_ids.shape[0], safe_ids.shape[1], model_width
+    all_scores = jnp.einsum(
+        "td,rd->tr", all_queries, index_rows, preferred_element_type=jnp.float32
     )
-    picked = jnp.einsum("td,tcd->tc", all_queries, fetched, preferred_element_type=jnp.float32)
+    picked = jnp.take_along_axis(all_scores, safe_ids, axis=1)
     owner_terms = jnp.where(is_owned, picked, jnp.float32(0.0))
     owner_terms = (
         owner_terms.reshape(req_count, text_count, tp_count, quarter)

time: 363 us -> 349 us (0.961)
  matrix products: 51.4 us -> 39.8 us
    gather x1 -> x3, local copies, waits for them, and re-layouts: 25.4 us -> 33 us  [per_device(): picked = jnp.take_along_axis(all_scores, safe_ids, axis=1)]
    sub x2 -> x1, matrix products: 13.8 us -> 7.66 us  [window_attention(): expo = jnp.exp(logits - top_val)]
    dot_general x3 -> x2, matrix products: 14.5 us -> 10.3 us  [the longest x1 6.04 us: per_device(): jnp.einsum('td,rd->tr', all_queries, index_rows, preferred_element_type=j...]
  transfers between devices with their start and end apart: 3 -> 3, of which waited for: 2 -> 2; matrix products, arithmetic and copies ran while one was open for 7% -> 1% of each run, Pallas kernels for 0% -> 0%
where the time goes in v1:
time: 349 us
  blocking collectives  153 us (44%)
  waiting for transfers between devices  93.8 us (27%)
  matrix products  39.8 us (11%)
  local copies, waits for them, and re-layouts  35.7 us (10%)
  between operations  14.1 us (4%)
  other arithmetic  12.5 us (4%)
    unnamed x1, blocking collectives  64 us
    psum x1, waiting for transfers between devices, per_device(): lax.psum(partial_value.astype(jnp.bfloat16), 'tp').astype(jnp.float32)  58.6 us
    all_gather x1, blocking collectives, per_device(): gathered_ids = lax.all_gather(cand_ids, ('req', 'tp'), axis=0, tiled=True)  54.9 us
    all_gather x1, waiting for transfers between devices, per_device(): full_states = lax.all_gather(states, 'tp', axis=1, tiled=True)  34.6 us
    gather x3, local copies, waits for them, and re-layouts, per_device(): picked = jnp.take_along_axis(all_scores, safe_ids, axis=1)  33 us
    all_gather x1, blocking collectives, per_device(): all_queries = lax.all_gather(query_vec, 'req', axis=0, tiled=True)  25.2 us
    dot_general x1, matrix products, per_device(): jnp.einsum('tsf,fd->tsd', up_act, w_down, preferred_element_type=jnp.floa...  12.5 us
    psum x1, blocking collectives, per_device(): pooled = lax.psum(local_pool, 'tp') / lengths.astype(jnp.float32)[:, None]  8.43 us
  transfers between devices with their start and end apart: 3, of which 2 were waited for; matrix products, arithmetic and copies ran while one was open for 1% of the time, Pallas kernels for 0%

profile of v1, /device:TPU:1, one launch (start us, length us, event | category | flops | bytes accessed | tf_op | source)
XLA Modules:
  0.0 348.8 jit_solution(4291036842600969684)
XLA Ops:
  7.2 0.7 all-gather.4.cloned.1.call-update
  8.1 0.7 iota_compare_fusion
  9.2 34.6 %all-gather.4.cloned.1.call-done = bf16[2,512,1024]{2,1,0:T(8,128)(2,1)} async-done(((bf16[2,128,1024]{2,1,0:T(8,128)(2,1)}), bf16[2,512,1024]{2,1,0:T(8,128)(2,1)}) %all-gather.4.cloned.1.call-update) | async-done | bytes 2097168 | tf_op jit(solution)/shard_map/all_gather | solution.py:71
  43.7 3.9 %add_convert_fusion.1 = bf16[2,512,3,256]{1,3,2,0:T(8,128)(2,1)S(1)} fusion(f32[3,256]{1,0:T(4,128)} %param.19, bf16[1024,3,256]{2,0,1:T(8,128)(2,1)} %param.18, bf16[2,512,1024]{2,1,0:T(8,128)(2,1)} %all-gather.4.cloned.1.call-done), kind=kOutput, calls=%fused_computation.36 | convolution fusion | flops 1612185600 | bytes 5245952 | tf_op jit(solution)/shard_map/tsd,dce->tsce/dot_general | solution.py:76
  47.6 1.1 fusion.112
  48.8 7.7 %fusion.113 = (f32[2,4,512]{2,1,0:T(4,128)S(1)}, f32[2,4,512,512]{2,3,1,0:T(8,128)}) fusion(pred[2,512,512]{1,2,0:T(8,128)(4,1)S(1)} %broadcast_and_fusion, bf16[2,512,4,64]{1,3,2,0:T(8,128)(2,1)} %bitcast.59, bf16[2,512,4,64]{1,3,2,0:T(8,128)(2,1)} %bitcast.58), kind=kOutput, calls=%fused_computation.148 | convolution fusion | flops 276824576 | bytes 9977856 | tf_op jit(solution)/shard_map/sub | solution.py:33
  56.4 4.3 %fusion.64 = bf16[2,4,64,512]{3,2,1,0:T(8,128)(2,1)S(1)} fusion(bf16[2,512,4,64]{1,3,2,0:T(8,128)(2,1)S(1)} %bitcast.57, f32[2,4,512,512]{2,3,1,0:T(8,128)} %get-tuple-element.12, f32[2,4,512]{2,1,0:T(4,128)S(1)} %get-tuple-element.11, pred[2,512]{1,0:T(4,128)(4,1)S(1)} %iota_compare_fusion), kind=kOutput, calls=%fused_computation.77 | convolution fusion | flops 273154048 | bytes 9454592 | tf_op jit(solution)/shard_map/thqk,tkhe->tqhe/dot_general | solution.py:35
  60.8 2.0 convolution_convert_fusion
  63.1 58.6 %all-reduce.3.cloned.1.call-done = bf16[2,512,1024]{2,1,0:T(8,128)(2,1)} async-done(((bf16[2,512,1024]{2,1,0:T(8,128)(2,1)}), bf16[2,512,1024]{2,1,0:T(8,128)(2,1)}) %all-reduce.3.cloned.1.call-update) | async-done | bytes 2097168 | tf_op jit(solution)/shard_map/psum | solution.py:84
  121.7 3.1 fusion.15
  125.1 1.1 multiply_reduce_fusion
  126.2 1.2 add_convert_fusion
  127.5 3.4 fusion.66
  131.0 12.5 %fusion.53 = bf16[2,512,1024]{2,1,0:T(8,128)(2,1)} fusion(bf16[1024,1024]{1,0:T(8,128)(2,1)S(1)} %copy-done.13, f32[2,512,1024]{2,1,0:T(8,128)S(1)} %get-tuple-element.13, f32[1024]{0:T(1024)S(1)} %copy-done.14, u8[512,1024]{1,0:T(8,128)(4,1)S(1)} %get-tuple-element.3, u8[512,1024]{1,0:T(8,128)(4,1)S(1)} %get-tuple-element.2), kind=kOutput, calls=%fused_computation.73 | convolution fusion | flops 2222981120 | bytes 9441280 | tf_op jit(solution)/shard_map/tsf,fd->tsd/dot_general | solution.py:93
  143.5 54.9 %all-gather = s32[128,2,16]{2,1,0:T(2,128)S(1)} all-gather(s32[1,2,16]{2,1,0:T(2,128)S(1)} %bitcast.62), channel_id=1, replica_groups=mesh['req'=32,'tp'=4] {'req','tp'}, dimensions={0}, use_global_device_ids=true | all-gather | bytes 16512 | tf_op jit(solution)/shard_map/all_gather | solution.py:70
  199.1 1.5 fusion.69
  200.5 1.5 multiply_reduce_fusion.1
  202.1 2.4 select_reduce_fusion
  204.5 8.4 %psum.15 = f32[2,1024]{1,0:T(2,128)S(1)} all-reduce(f32[2,1024]{1,0:T(2,128)S(1)} %get-tuple-element.6), channel_id=1, replica_groups=mesh['req'=32,'tp'=4] {'tp'}, use_global_device_ids=true, to_apply=%region_9.10 | all-reduce | flops 2048 | bytes 16384 | tf_op jit(solution)/shard_map/psum | solution.py:105
  213.2 25.2 %all-gather.1 = bf16[32,2,1024]{2,1,0:T(2,128)(2,1)S(1)} all-gather(bf16[1,2,1024]{2,1,0:T(2,128)(2,1)S(1)} %fusion.78), channel_id=1, replica_groups=mesh['req'=32,'tp'=4] {'req'}, dimensions={0}, use_global_device_ids=true | all-gather | bytes 135168 | tf_op jit(solution)/shard_map/all_gather | solution.py:109
  238.5 6.0 %fusion.114 = f32[64,4096]{1,0:T(8,128)S(1)} fusion(bf16[64,1024]{1,0:T(8,128)(2,1)S(1)} %reshape.206, bf16[4096,1024]{1,0:T(8,128)(2,1)} %param.30), kind=kOutput, calls=%fused_computation.149 | convolution fusion | flops 536870912 | bytes 9568256 | tf_op jit(solution)/shard_map/td,rd->tr/dot_general | solution.py:120
  244.5 32.8 %gather_fusion = f32[4096]{0:T(1024)S(1)} fusion(f32[64,4096]{1,0:T(8,128)S(1)} %fusion.114, s32[4096]{0:T(1024)S(1)} %reshape.196), kind=kCustom, calls=%fused_computation | custom fusion | bytes 65536 | tf_op jit(solution)/shard_map/jit(take_along_axis)/gather | solution.py:123
  277.7 64.0 %all-reduce = f32[256,16]{1,0:T(8,128)S(1)} all-reduce(f32[256,16]{1,0:T(8,128)S(1)} %bitcast.56), channel_id=3, replica_groups=mesh['req'=32,'tp'=4] {'req','tp'}, use_global_device_ids=true, to_apply=%region_11.12.clone | all-reduce | flops 4096 | bytes 32768
  341.7 0.6 constant_dynamic-slice_fusion
  (61 shorter events, 2.5 us)
Async XLA Ops:
  7.2 120.3 %copy-start = (bf16[1024,1024]{1,0:T(8,128)(2,1)S(1)}, bf16[1024,1024]{1,0:T(8,128)(2,1)}, u32[]{:S(2)}) copy-start(bf16[1024,1024]{1,0:T(8,128)(2,1)} %param.24) | copy-start | bytes 6291460
  7.2 36.5 %all-gather.4.cloned.1.call-start = ((), (), s32[]{:S(2)}) async-start(), calls=%async_computation.1 | async-start | bytes 2621440 | tf_op jit(solution)/shard_map/all_gather | solution.py:71
  7.9 113.7 %all-reduce.3.cloned.1.call-start = ((), (), s32[]{:S(2)}) async-start(), calls=%async_computation.2 | async-start | bytes 4194304 | tf_op jit(solution)/shard_map/psum | solution.py:84
  56.4 4.3 %copy-start.4 = (bf16[256,1024]{1,0:T(8,128)(2,1)S(1)}, bf16[256,1024]{1,0:T(8,128)(2,1)}, u32[]{:S(2)}) copy-start(bf16[256,1024]{1,0:T(8,128)(2,1)} %param.20) | copy-start | bytes 1572868
  60.8 60.9 %copy-start.6 = (f32[1024]{0:T(1024)S(1)}, f32[1024]{0:T(1024)}, u32[]{:S(2)}) copy-start(f32[1024]{0:T(1024)} %param.21) | copy-start | bytes 12292
  62.8 63.4 %copy-start.9 = (f32[1024]{0:T(1024)S(1)}, f32[1024]{0:T(1024)}, u32[]{:S(2)}) copy-start(f32[1024]{0:T(1024)} %param.23) | copy-start | bytes 12292
  62.8 63.4 %copy-start.10 = (f32[1024]{0:T(1024)S(1)}, f32[1024]{0:T(1024)}, u32[]{:S(2)}) copy-start(f32[1024]{0:T(1024)} %param.22) | copy-start | bytes 12292
  62.9 136.2 %reduce-scatter.2.cloned.1.call-start = ((), (), s32[]{:S(2)}) async-start(), calls=%async_computation.3 | async-start | bytes 2621440 | tf_op jit(solution)/shard_map/reduce_scatter | solution.py:94
  121.7 3.1 copy-start.1
  121.7 3.5 copy-start.2
  126.2 1.3 copy-start.14
  127.5 3.4 copy-start.3
  127.5 3.4 copy-start.13
  130.9 12.5 %copy-start.12 = (s32[2]{0:T(128)S(1)}, s32[2]{0:T(128)}, u32[]{:S(2)}) copy-start(s32[2]{0:T(128)} %param.17) | copy-start | bytes 28
  130.9 12.5 %copy-start.11 = (s32[2,16]{1,0:T(2,128)S(1)}, s32[2,16]{1,0:T(2,128)}, u32[]{:S(2)}) copy-start(s32[2,16]{1,0:T(2,128)} %param.31) | copy-start | bytes 388
  130.9 68.1 %copy-start.5 = (f32[1024]{0:T(1024)S(1)}, f32[1024]{0:T(1024)}, u32[]{:S(2)}) copy-start(f32[1024]{0:T(1024)} %param.27) | copy-start | bytes 12292
  143.4 58.7 %copy-start.7 = (f32[1024]{0:T(1024)S(1)}, f32[1024]{0:T(1024)}, u32[]{:S(2)}) copy-start(f32[1024]{0:T(1024)} %param.29) | copy-start | bytes 12292
  143.4 58.7 %copy-start.8 = (f32[1024]{0:T(1024)S(1)}, f32[1024]{0:T(1024)}, u32[]{:S(2)}) copy-start(f32[1024]{0:T(1024)} %param.28) | copy-start | bytes 12292
Sparse Core Ops, SparseCore 0:
  9.7 34.0 all-gather.3
  63.0 58.6 all-reduce.2
  143.6 29.6 reduce-scatter.1

commit v2 on v1

--- a/solution.py
+++ b/solution.py
@@ -67,8 +67,13 @@
     req_rank = lax.axis_index("req")
     text_count, row_share, model_width = states.shape
     quarter = cand_ids.shape[1]
-    gathered_ids = lax.all_gather(cand_ids, ("req", "tp"), axis=0, tiled=True)
     full_states = lax.all_gather(states, "tp", axis=1, tiled=True)
+    device_count = req_count * tp_count
+    gathered_ids = lax.all_to_all(
+        jnp.broadcast_to(cand_ids[None], (device_count,) + cand_ids.shape),
+        ("req", "tp"), 0, 0, tiled=True,
+    )
+    full_states, gathered_ids = lax.optimization_barrier((full_states, gathered_ids))
     seq_len = full_states.shape[1]
     local_width = w_qkv.shape[2]
     heads_here = local_width // HEAD_DIM
@@ -106,7 +111,9 @@
     query_vec = (
         pooled * lax.rsqrt(jnp.mean(pooled * pooled, axis=-1, keepdims=True) + norm_eps)
     ).astype(jnp.bfloat16)
-    all_queries = lax.all_gather(query_vec, "req", axis=0, tiled=True)
+    all_queries = lax.all_to_all(
+        jnp.broadcast_to(query_vec[None], (req_count,) + query_vec.shape), "req", 0, 0, tiled=True
+    ).reshape(req_count * text_count, model_width)
     all_ids = (
         gathered_ids.reshape(req_count, tp_count, text_count, quarter)
         .transpose(0, 2, 1, 3)
@@ -120,14 +127,17 @@
     all_scores = jnp.einsum(
         "td,rd->tr", all_queries, index_rows, preferred_element_type=jnp.float32
     )
-    picked = jnp.take_along_axis(all_scores, safe_ids, axis=1)
+    score_rows = jnp.take(all_scores.T, safe_ids.reshape(-1), axis=0).reshape(
+        safe_ids.shape[0], safe_ids.shape[1], safe_ids.shape[0]
+    )
+    picked = jnp.einsum("tct->tc", score_rows)
     owner_terms = jnp.where(is_owned, picked, jnp.float32(0.0))
     owner_terms = (
         owner_terms.reshape(req_count, text_count, tp_count, quarter)
         .transpose(0, 2, 1, 3)
-        .reshape(req_count * tp_count * text_count, quarter)
+        .reshape(device_count, text_count, quarter)
     )
-    scores = lax.psum_scatter(owner_terms, ("req", "tp"), scatter_dimension=0, tiled=True)
+    scores = jnp.sum(lax.all_to_all(owner_terms, ("req", "tp"), 0, 0, tiled=True), axis=0)
     return (hidden_out, scores)
 
 

time: 349 us -> 251 us (0.72)
  blocking collectives: 153 us -> 20.5 us
  waiting for transfers between devices: 93.8 us -> 117 us
  starting transfers between devices: 0.3 us -> 21.5 us
  local copies, waits for them, and re-layouts: 35.7 us -> 22.2 us
    all_gather x2 -> x0, blocking collectives: 80.2 us -> none  [the longest x1 54.9 us: per_device(): gathered_ids = lax.all_gather(cand_ids, ('req', 'tp'), axis=0, tiled=True)]
    unnamed x1 -> x0, blocking collectives: 64 us -> none
    reduce_scatter x1, waiting for transfers between devices: 0.01 us -> 28.7 us  [per_device(): lax.psum_scatter(down_part.astype(jnp.bfloat16), 'tp', scatter_dimension=...]
    all_gather x1, waiting for transfers between devices: 34.6 us -> 12.9 us  [per_device(): full_states = lax.all_gather(states, 'tp', axis=1, tiled=True)]
    all_to_all x0 -> x2, starting transfers between devices: none -> 21.2 us  [the longest x1 11.5 us: per_device(): lax.all_to_all(jnp.broadcast_to(cand_ids[None], (device_count,) + cand_id...]
    gather x3 -> x1, local copies, waits for them, and re-layouts: 33 us -> 15.7 us  [per_device(): jnp.take(all_scores.T, safe_ids.reshape(-1), axis=0)]
    all_to_all x0 -> x2, waiting for transfers between devices: none -> 16.5 us  [the longest x1 8.8 us: per_device(): lax.all_to_all(jnp.broadcast_to(cand_ids[None], (device_count,) + cand_id...]
    all_to_all x0 -> x1, blocking collectives: none -> 13.9 us  [per_device(): lax.all_to_all(owner_terms, ('req', 'tp'), 0, 0, tiled=True)]
  transfers between devices with their start and end apart: 3 -> 5, of which waited for: 2 -> 5; matrix products, arithmetic and copies ran while one was open for 1% -> 1% of each run, Pallas kernels for 0% -> 0%
where the time goes in v2:
time: 251 us
  waiting for transfers between devices  117 us (47%)
  matrix products  39.8 us (16%)
  local copies, waits for them, and re-layouts  22.2 us (9%)
  starting transfers between devices  21.5 us (9%)
  blocking collectives  20.5 us (8%)
  other arithmetic  15.3 us (6%)
  between operations  14.1 us (6%)
    psum x1, waiting for transfers between devices, per_device(): lax.psum(partial_value.astype(jnp.bfloat16), 'tp').astype(jnp.float32)  58.6 us
    reduce_scatter x1, waiting for transfers between devices, per_device(): lax.psum_scatter(down_part.astype(jnp.bfloat16), 'tp', scatter_dimension=...  28.7 us
    gather x1, local copies, waits for them, and re-layouts, per_device(): jnp.take(all_scores.T, safe_ids.reshape(-1), axis=0)  15.7 us
    all_to_all x1, blocking collectives, per_device(): lax.all_to_all(owner_terms, ('req', 'tp'), 0, 0, tiled=True)  13.9 us
    all_gather x1, waiting for transfers between devices, per_device(): full_states = lax.all_gather(states, 'tp', axis=1, tiled=True)  12.9 us
    dot_general x1, matrix products, per_device(): jnp.einsum('tsf,fd->tsd', up_act, w_down, preferred_element_type=jnp.floa...  12.5 us
    all_to_all x1, starting transfers between devices, per_device(): lax.all_to_all(jnp.broadcast_to(cand_ids[None], (device_count,) + cand_id...  11.5 us
    all_to_all x1, starting transfers between devices, per_device(): lax.all_to_all(jnp.broadcast_to(query_vec[None], (req_count,) + query_vec...  9.67 us
  transfers between devices with their start and end apart: 5, of which 5 were waited for; matrix products, arithmetic and copies ran while one was open for 1% of the time, Pallas kernels for 0%

profile of v2, /device:TPU:1, one launch (start us, length us, event | category | flops | bytes accessed | tf_op | source)
XLA Modules:
  0.0 250.8 jit_solution(11163683712787077177)
XLA Ops:
  7.9 1.4 broadcast_in_dim.50
  9.3 11.5 %all-to-all-start = ((s32[128,2,16]{2,1,0:T(2,128)}), s32[128,2,16]{2,1,0:T(2,128)S(1)}, u32[]{:S(2)}, u32[]{:S(2)}) async-start(s32[128,2,16]{2,1,0:T(2,128)} %broadcast_in_dim.50), calls=%async_computation | async-start | bytes 262144 | tf_op jit(solution)/shard_map/all_to_all | solution.py:72
  22.0 8.8 %all-to-all-done = s32[128,2,16]{2,1,0:T(2,128)S(1)} async-done(((s32[128,2,16]{2,1,0:T(2,128)}), s32[128,2,16]{2,1,0:T(2,128)S(1)}, u32[]{:S(2)}, u32[]{:S(2)}) %all-to-all-start) | async-done | bytes 16416 | tf_op jit(solution)/shard_map/all_to_all | solution.py:72
  30.8 12.9 %all-gather.2.cloned.1.call-done = bf16[2,512,1024]{2,1,0:T(8,128)(2,1)} async-done(((bf16[2,128,1024]{2,1,0:T(8,128)(2,1)}), bf16[2,512,1024]{2,1,0:T(8,128)(2,1)}) %all-gather.2.cloned.1.call-update) | async-done | bytes 2097168 | tf_op jit(solution)/shard_map/all_gather | solution.py:70
  43.7 3.9 %add_convert_fusion.1 = bf16[2,512,3,256]{1,3,2,0:T(8,128)(2,1)S(1)} fusion(f32[3,256]{1,0:T(4,128)} %param.19, bf16[1024,3,256]{2,0,1:T(8,128)(2,1)} %param.18, bf16[2,512,1024]{2,1,0:T(8,128)(2,1)} %all-gather.2.cloned.1.call-done), kind=kOutput, calls=%fused_computation.37 | convolution fusion | flops 1612185600 | bytes 5245952 | tf_op jit(solution)/shard_map/tsd,dce->tsce/dot_general | solution.py:81
  48.8 7.7 %fusion.107 = (f32[2,4,512]{2,1,0:T(4,128)S(1)}, f32[2,4,512,512]{2,3,1,0:T(8,128)}) fusion(pred[2,512,512]{1,2,0:T(8,128)(4,1)S(1)} %broadcast_and_fusion, bf16[2,512,4,64]{1,3,2,0:T(8,128)(2,1)} %bitcast.61, bf16[2,512,4,64]{1,3,2,0:T(8,128)(2,1)} %bitcast.60), kind=kOutput, calls=%fused_computation.147 | convolution fusion | flops 276824576 | bytes 9977856 | tf_op jit(solution)/shard_map/sub | solution.py:33
  56.4 4.3 %fusion.64 = bf16[2,4,64,512]{3,2,1,0:T(8,128)(2,1)S(1)} fusion(bf16[2,512,4,64]{1,3,2,0:T(8,128)(2,1)S(1)} %bitcast.59, f32[2,4,512,512]{2,3,1,0:T(8,128)} %get-tuple-element.16, f32[2,4,512]{2,1,0:T(4,128)S(1)} %get-tuple-element.15, pred[2,512]{1,0:T(4,128)(4,1)S(1)} %iota_compare_fusion.1), kind=kOutput, calls=%fused_computation.79 | convolution fusion | flops 273154048 | bytes 9454592 | tf_op jit(solution)/shard_map/thqk,tkhe->tqhe/dot_general | solution.py:35
  60.8 2.1 convolution_convert_fusion
  63.1 58.6 %all-reduce.2.cloned.1.call-done = bf16[2,512,1024]{2,1,0:T(8,128)(2,1)} async-done(((bf16[2,512,1024]{2,1,0:T(8,128)(2,1)}), bf16[2,512,1024]{2,1,0:T(8,128)(2,1)}) %all-reduce.2.cloned.1.call-update) | async-done | bytes 2097168 | tf_op jit(solution)/shard_map/psum | solution.py:89
  121.7 3.1 %fusion.15 = f32[2,512]{1,0:T(2,128)S(1)} fusion(bf16[2,512,1024]{2,1,0:T(8,128)(2,1)} %all-reduce.2.cloned.1.call-done, bf16[2,512,1024]{2,1,0:T(8,128)(2,1)} %all-gather.2.cloned.1.call-done, f32[1024]{0:T(1024)S(1)} %copy-done.6), kind=kLoop, calls=%fused_computation.36 | loop fusion | flops 5241856 | bytes 4202496 | tf_op jit(solution)/shard_map/reduce_sum | solution.py:15
  127.6 3.4 %fusion.66 = (u8[512,1024]{1,0:T(8,128)(4,1)S(1)}, u8[512,1024]{1,0:T(8,128)(4,1)S(1)}, f32[2,512,1024]{2,1,0:T(8,128)S(1)}) fusion(f32[1024]{0:T(1024)S(1)} %copy-done.13, bf16[2,512,1024]{2,1,0:T(8,128)(2,1)S(1)} %add_convert_fusion, bf16[1024,1024]{1,0:T(8,128)(2,1)S(1)} %copy-done), kind=kOutput, calls=%fused_computation.86 | convolution fusion | flops 2161115136 | bytes 9441280 | tf_op jit(solution)/shard_map/tsd,df->tsf/dot_general | solution.py:95
  131.0 12.5 %fusion.53 = bf16[2,512,1024]{2,1,0:T(8,128)(2,1)} fusion(bf16[1024,1024]{1,0:T(8,128)(2,1)S(1)} %copy-done.12, f32[2,512,1024]{2,1,0:T(8,128)S(1)} %get-tuple-element.17, f32[1024]{0:T(1024)S(1)} %copy-done.13, u8[512,1024]{1,0:T(8,128)(4,1)S(1)} %get-tuple-element.7, u8[512,1024]{1,0:T(8,128)(4,1)S(1)} %get-tuple-element.6), kind=kOutput, calls=%fused_computation.75 | convolution fusion | flops 2222981120 | bytes 9441280 | tf_op jit(solution)/shard_map/tsf,fd->tsd/dot_general | solution.py:98
  144.4 28.7 %reduce-scatter.2.cloned.1.call-done = bf16[2,128,1024]{2,1,0:T(8,128)(2,1)} async-done(((bf16[2,512,1024]{2,1,0:T(8,128)(2,1)}), bf16[2,128,1024]{2,1,0:T(8,128)(2,1)}) %reduce-scatter.2.cloned.1.call-update) | async-done | bytes 524304 | tf_op jit(solution)/shard_map/reduce_scatter | solution.py:99
  173.1 1.4 fusion.69
  174.6 1.5 multiply_reduce_fusion.1
  176.2 2.4 select_reduce_fusion.1
  178.6 6.7 %psum.15 = f32[2,1024]{1,0:T(2,128)S(1)} all-reduce(f32[2,1024]{1,0:T(2,128)S(1)} %get-tuple-element.10), channel_id=1, replica_groups=mesh['req'=32,'tp'=4] {'tp'}, use_global_device_ids=true, to_apply=%region_9.10 | all-reduce | flops 2048 | bytes 16384 | tf_op jit(solution)/shard_map/psum | solution.py:110
  186.2 9.7 %all-to-all-start.1 = ((bf16[32,2,1024]{2,1,0:T(2,128)(2,1)}), bf16[32,2,1024]{2,1,0:T(2,128)(2,1)S(1)}, u32[]{:S(2)}, u32[]{:S(2)}) async-start(bf16[32,2,1024]{2,1,0:T(2,128)(2,1)} %broadcast_in_dim.63), calls=%async_computation.2 | async-start | bytes 262144 | tf_op jit(solution)/shard_map/all_to_all | solution.py:114
  195.9 7.7 %all-to-all-done.1 = bf16[32,2,1024]{2,1,0:T(2,128)(2,1)S(1)} async-done(((bf16[32,2,1024]{2,1,0:T(2,128)(2,1)}), bf16[32,2,1024]{2,1,0:T(2,128)(2,1)S(1)}, u32[]{:S(2)}, u32[]{:S(2)}) %all-to-all-start.1) | async-done | bytes 131104 | tf_op jit(solution)/shard_map/all_to_all | solution.py:114
  203.7 6.0 %convolution_bitcast_fusion = f32[4096,64]{0,1:T(8,128)S(1)} fusion(bf16[64,1024]{1,0:T(8,128)(2,1)S(1)} %reshape.217, bf16[4096,1024]{1,0:T(8,128)(2,1)} %param.30), kind=kOutput, calls=%fused_computation.7 | convolution fusion | flops 536870912 | bytes 9568256 | tf_op jit(solution)/shard_map/td,rd->tr/dot_general | solution.py:127
  209.7 2.0 copy.49
  211.7 15.7 %gather_fusion = f32[4096,64]{1,0:T(8,128)} fusion(f32[4096,64]{1,0:T(8,128)} %copy.49, s32[4096]{0:T(1024)S(1)} %broadcast_clamp_fusion), kind=kCustom, calls=%fused_computation | custom fusion | bytes 2113536 | tf_op jit(solution)/shard_map/jit(_take)/gather | solution.py:130
  227.3 1.9 select_reduce_fusion
  229.6 13.9 %all_to_all.15 = f32[128,2,16]{2,1,0:T(2,128)S(1)} all-to-all(f32[128,2,16]{2,1,0:T(2,128)S(1)} %copy.53), channel_id=1, replica_groups=mesh['req'=32,'tp'=4] {'req','tp'}, dimensions={0} | all-to-all | bytes 32768 | tf_op jit(solution)/shard_map/all_to_all | solution.py:140
  (70 shorter events, 9.0 us)
Async XLA Ops:
  7.2 120.3 %copy-start = (bf16[1024,1024]{1,0:T(8,128)(2,1)S(1)}, bf16[1024,1024]{1,0:T(8,128)(2,1)}, u32[]{:S(2)}) copy-start(bf16[1024,1024]{1,0:T(8,128)(2,1)} %param.24) | copy-start | bytes 6291460
  7.2 36.5 %all-gather.2.cloned.1.call-start = ((), (), s32[]{:S(2)}) async-start(), calls=%async_computation.4 | async-start | bytes 2621440 | tf_op jit(solution)/shard_map/all_gather | solution.py:70
  9.3 21.6 %all-to-all-start = ((s32[128,2,16]{2,1,0:T(2,128)}), s32[128,2,16]{2,1,0:T(2,128)S(1)}, u32[]{:S(2)}, u32[]{:S(2)}) async-start(s32[128,2,16]{2,1,0:T(2,128)} %broadcast_in_dim.50), calls=%async_computation | async-start | bytes 262144 | tf_op jit(solution)/shard_map/all_to_all | solution.py:72
  20.8 100.9 %all-reduce.2.cloned.1.call-start = ((), (), s32[]{:S(2)}) async-start(), calls=%async_computation.5 | async-start | bytes 4194304 | tf_op jit(solution)/shard_map/psum | solution.py:89
  56.4 4.3 %copy-start.4 = (bf16[256,1024]{1,0:T(8,128)(2,1)S(1)}, bf16[256,1024]{1,0:T(8,128)(2,1)}, u32[]{:S(2)}) copy-start(bf16[256,1024]{1,0:T(8,128)(2,1)} %param.20) | copy-start | bytes 1572868
  60.8 60.9 %copy-start.6 = (f32[1024]{0:T(1024)S(1)}, f32[1024]{0:T(1024)}, u32[]{:S(2)}) copy-start(f32[1024]{0:T(1024)} %param.21) | copy-start | bytes 12292
  62.9 63.4 %copy-start.9 = (f32[1024]{0:T(1024)S(1)}, f32[1024]{0:T(1024)}, u32[]{:S(2)}) copy-start(f32[1024]{0:T(1024)} %param.23) | copy-start | bytes 12292
  62.9 63.4 %copy-start.10 = (f32[1024]{0:T(1024)S(1)}, f32[1024]{0:T(1024)}, u32[]{:S(2)}) copy-start(f32[1024]{0:T(1024)} %param.22) | copy-start | bytes 12292
  62.9 110.3 %reduce-scatter.2.cloned.1.call-start = ((), (), s32[]{:S(2)}) async-start(), calls=%async_computation.6 | async-start | bytes 2621440 | tf_op jit(solution)/shard_map/reduce_scatter | solution.py:99
  121.7 3.1 %copy-start.1 = (bf16[2,512,1024]{2,1,0:T(8,128)(2,1)S(1)}, bf16[2,512,1024]{2,1,0:T(8,128)(2,1)}, u32[]{:S(2)}) copy-start(bf16[2,512,1024]{2,1,0:T(8,128)(2,1)} %all-gather.2.cloned.1.call-done) | copy-start | bytes 6291460
  121.7 3.5 %copy-start.2 = (bf16[2,512,1024]{2,1,0:T(8,128)(2,1)S(1)}, bf16[2,512,1024]{2,1,0:T(8,128)(2,1)}, u32[]{:S(2)}) copy-start(bf16[2,512,1024]{2,1,0:T(8,128)(2,1)} %all-reduce.2.cloned.1.call-done) | copy-start | bytes 6291460
  126.2 1.3 copy-start.13
  127.5 3.4 %copy-start.3 = (bf16[2,512,1024]{2,1,0:T(8,128)(2,1)}, bf16[2,512,1024]{2,1,0:T(8,128)(2,1)S(1)}, u32[]{:S(2)}) copy-start(bf16[2,512,1024]{2,1,0:T(8,128)(2,1)S(1)} %add_convert_fusion) | copy-start | bytes 6291460
  127.5 3.4 %copy-start.12 = (bf16[1024,1024]{1,0:T(8,128)(2,1)S(1)}, bf16[1024,1024]{1,0:T(8,128)(2,1)}, u32[]{:S(2)}) copy-start(bf16[1024,1024]{1,0:T(8,128)(2,1)} %param.26) | copy-start | bytes 6291460
  130.9 12.5 %copy-start.11 = (s32[2]{0:T(128)S(1)}, s32[2]{0:T(128)}, u32[]{:S(2)}) copy-start(s32[2]{0:T(128)} %param.17) | copy-start | bytes 28
  131.0 42.2 %copy-start.5 = (f32[1024]{0:T(1024)S(1)}, f32[1024]{0:T(1024)}, u32[]{:S(2)}) copy-start(f32[1024]{0:T(1024)} %param.27) | copy-start | bytes 12292
  143.4 32.7 %copy-start.7 = (f32[1024]{0:T(1024)S(1)}, f32[1024]{0:T(1024)}, u32[]{:S(2)}) copy-start(f32[1024]{0:T(1024)} %param.29) | copy-start | bytes 12292
  143.4 32.7 %copy-start.8 = (f32[1024]{0:T(1024)S(1)}, f32[1024]{0:T(1024)}, u32[]{:S(2)}) copy-start(f32[1024]{0:T(1024)} %param.28) | copy-start | bytes 12292
  186.2 17.4 %all-to-all-start.1 = ((bf16[32,2,1024]{2,1,0:T(2,128)(2,1)}), bf16[32,2,1024]{2,1,0:T(2,128)(2,1)S(1)}, u32[]{:S(2)}, u32[]{:S(2)}) async-start(bf16[32,2,1024]{2,1,0:T(2,128)(2,1)} %broadcast_in_dim.63), calls=%async_computation.2 | async-start | bytes 262144 | tf_op jit(solution)/shard_map/all_to_all | solution.py:114
Sparse Core Ops, SparseCore 0:
  9.7 34.0 all-gather.1
  63.0 58.6 all-reduce.1
  143.6 29.5 reduce-scatter.1

commit v3 on v2

--- a/solution.py
+++ b/solution.py
@@ -1,7 +1,149 @@
+import functools
 import jax
 import jax.numpy as jnp
 from jax import lax
+from jax.experimental import pallas as pl
+from jax.experimental.pallas import tpu as pltpu
 from jax.sharding import PartitionSpec as P
+
+MESH_ID = pl.DeviceIdType.MESH
+
+
+def _ring_peers():
+    n = lax.axis_size("tp")
+    me = lax.axis_index("tp")
+    rq = lax.axis_index("req")
+    core = rq % 2
+    right = (me + 1) % n
+    left = (me + n - 1) % n
+    opp = (me + 2) % n
+    relay_to = (me + 1 + 2 * core) % n
+    relay_from = (me + n - 1 - 2 * core) % n
+    barrier = pltpu.get_barrier_semaphore()
+    for peer in (left, right):
+        pl.semaphore_signal(barrier, inc=1, device_id=(rq, peer), device_id_type=MESH_ID)
+    pl.semaphore_wait(barrier, 2)
+    return me, rq, core, right, left, opp, relay_to, relay_from
+
+
+def _gather_kernel(x_ref, out_ref, send_sem, recv_sem, local_sem):
+    me, rq, core, right, left, opp, relay_to, relay_from = _ring_peers()
+    rows = x_ref.shape[1]
+
+    def slot(src):
+        return out_ref.at[:, pl.ds(src * rows, rows), :]
+
+    local = pltpu.make_async_copy(x_ref, slot(me), local_sem)
+    local.start()
+    to_right = pltpu.make_async_remote_copy(
+        x_ref, slot(me), send_sem.at[0], recv_sem.at[0], device_id=(rq, right), device_id_type=MESH_ID
+    )
+    to_left = pltpu.make_async_remote_copy(
+        x_ref, slot(me), send_sem.at[1], recv_sem.at[1], device_id=(rq, left), device_id_type=MESH_ID
+    )
+    to_right.start()
+    to_left.start()
+    from_relay = pltpu.make_async_remote_copy(
+        x_ref, slot(relay_from), send_sem.at[2], recv_sem.at[core], device_id=(rq, relay_to),
+        device_id_type=MESH_ID,
+    )
+    from_relay.wait_recv()
+    forward = pltpu.make_async_remote_copy(
+        slot(relay_from), slot(relay_from), send_sem.at[2], recv_sem.at[2], device_id=(rq, relay_to),
+        device_id_type=MESH_ID,
+    )
+    forward.start()
+    other_side = (me + 1 + 2 * (1 - core)) % lax.axis_size("tp")
+    from_other = pltpu.make_async_remote_copy(
+        x_ref, slot(other_side), send_sem.at[0], recv_sem.at[1 - core], device_id=(rq, right),
+        device_id_type=MESH_ID,
+    )
+    from_other.wait_recv()
+    from_opp = pltpu.make_async_remote_copy(
+        x_ref, slot(opp), send_sem.at[0], recv_sem.at[2], device_id=(rq, right), device_id_type=MESH_ID
+    )
+    from_opp.wait_recv()
+    to_right.wait_send()
+    to_left.wait_send()
+    forward.wait_send()
+    local.wait()
+
+
+def ring_all_gather(x, collective_id):
+    texts, rows, width = x.shape
+    n = lax.axis_size("tp")
+    return pl.pallas_call(
+        _gather_kernel,
+        out_shape=jax.ShapeDtypeStruct((texts, n * rows, width), x.dtype),
+        in_specs=[pl.BlockSpec(memory_space=pl.ANY)],
+        out_specs=pl.BlockSpec(memory_space=pl.ANY),
+        scratch_shapes=[
+            pltpu.SemaphoreType.DMA((3,)),
+            pltpu.SemaphoreType.DMA((3,)),
+            pltpu.SemaphoreType.DMA,
+        ],
+        compiler_params=pltpu.CompilerParams(collective_id=collective_id, has_side_effects=True),
+    )(x)
+
+
+def _scatter_kernel(p_ref, recv_ref, relay_ref, send_sem, recv_sem, relay_sem):
+    me, rq, core, right, left, opp, relay_to, relay_from = _ring_peers()
+    rows = recv_ref.shape[2]
+
+    def block(dst):
+        return p_ref.at[:, pl.ds(dst * rows, rows), :]
+
+    to_right = pltpu.make_async_remote_copy(
+        block(right), recv_ref.at[0], send_sem.at[0], recv_sem.at[0], device_id=(rq, right),
+        device_id_type=MESH_ID,
+    )
+    to_left = pltpu.make_async_remote_copy(
+        block(left), recv_ref.at[1], send_sem.at[1], recv_sem.at[1], device_id=(rq, left),
+        device_id_type=MESH_ID,
+    )
+    to_relay = pltpu.make_async_remote_copy(
+        block(opp), relay_ref, send_sem.at[2], relay_sem, device_id=(rq, relay_to),
+        device_id_type=MESH_ID,
+    )
+    to_right.start()
+    to_left.start()
+    to_relay.start()
+    to_relay.wait_recv()
+    forward = pltpu.make_async_remote_copy(
+        relay_ref, recv_ref.at[2], send_sem.at[3], recv_sem.at[2], device_id=(rq, relay_to),
+        device_id_type=MESH_ID,
+    )
+    forward.start()
+    to_right.wait_recv()
+    to_left.wait_recv()
+    forward.wait_recv()
+    to_right.wait_send()
+    to_left.wait_send()
+    to_relay.wait_send()
+    forward.wait_send()
+
+
+def ring_reduce_scatter(p, collective_id):
+    texts, all_rows, width = p.shape
+    n = lax.axis_size("tp")
+    rows = all_rows // n
+    recv, _ = pl.pallas_call(
+        _scatter_kernel,
+        out_shape=(
+            jax.ShapeDtypeStruct((n - 1, texts, rows, width), p.dtype),
+            jax.ShapeDtypeStruct((texts, rows, width), p.dtype),
+        ),
+        in_specs=[pl.BlockSpec(memory_space=pl.ANY)],
+        out_specs=(pl.BlockSpec(memory_space=pl.ANY), pl.BlockSpec(memory_space=pl.ANY)),
+        scratch_shapes=[
+            pltpu.SemaphoreType.DMA((4,)),
+            pltpu.SemaphoreType.DMA((3,)),
+            pltpu.SemaphoreType.DMA,
+        ],
+        compiler_params=pltpu.CompilerParams(collective_id=collective_id, has_side_effects=True),
+    )(p)
+    return recv
+
 
 HEAD_DIM = 64
 WINDOW = 512
@@ -67,7 +209,7 @@
     req_rank = lax.axis_index("req")
     text_count, row_share, model_width = states.shape
     quarter = cand_ids.shape[1]
-    full_states = lax.all_gather(states, "tp", axis=1, tiled=True)
+    full_states = ring_all_gather(states, 0)
     device_count = req_count * tp_count
     gathered_ids = lax.all_to_all(
         jnp.broadcast_to(cand_ids[None], (device_count,) + cand_ids.shape),
@@ -86,19 +228,26 @@
 
     context = window_attention(queries_h, keys_h, values_h, lengths)
     partial_value = jnp.einsum("tsk,kd->tsd", context, w_out, preferred_element_type=jnp.float32)
-    attn_sum = lax.psum(partial_value.astype(jnp.bfloat16), "tp").astype(jnp.float32)
-    normed_full = layer_norm(
-        full_states.astype(jnp.float32) + attn_sum + b_out, ln1_gain, ln1_shift
-    ).astype(jnp.bfloat16)
-    normed_local = lax.dynamic_slice_in_dim(normed_full, tp_rank * row_share, row_share, 1)
+    partial_value = partial_value.astype(jnp.bfloat16)
+    attn_recv = ring_reduce_scatter(partial_value, 1)
+    attn_sum = lax.dynamic_slice_in_dim(partial_value, tp_rank * row_share, row_share, 1).astype(
+        jnp.float32
+    ) + jnp.sum(attn_recv.astype(jnp.float32), axis=0)
+    normed_local = layer_norm(
+        states.astype(jnp.float32) + attn_sum + b_out, ln1_gain, ln1_shift
+    ).astype(jnp.bfloat16)
+    normed_full = ring_all_gather(normed_local, 2)
     up_act = jax.nn.gelu(
         jnp.einsum("tsd,df->tsf", normed_full, w_up, preferred_element_type=jnp.float32) + b_up,
         approximate=False,
     ).astype(jnp.bfloat16)
-    down_part = jnp.einsum("tsf,fd->tsd", up_act, w_down, preferred_element_type=jnp.float32)
-    down_sum = lax.psum_scatter(
-        down_part.astype(jnp.bfloat16), "tp", scatter_dimension=1, tiled=True
-    ).astype(jnp.float32)
+    down_part = jnp.einsum(
+        "tsf,fd->tsd", up_act, w_down, preferred_element_type=jnp.float32
+    ).astype(jnp.bfloat16)
+    down_recv = ring_reduce_scatter(down_part, 3)
+    down_sum = lax.dynamic_slice_in_dim(down_part, tp_rank * row_share, row_share, 1).astype(
+        jnp.float32
+    ) + jnp.sum(down_recv.astype(jnp.float32), axis=0)
     hidden_out = layer_norm(
         normed_local.astype(jnp.float32) + down_sum + b_down, ln2_gain, ln2_shift
     ).astype(jnp.bfloat16)

time: 251 us -> 237 us (0.944)
  waiting for transfers between devices: 117 us -> 7.69 us
  Pallas kernels: 0 us -> 101 us
  between operations: 14.1 us -> 1.09 us
    pallas_call x0 -> x4, Pallas kernels: none -> 101 us  [the longest x2 57.2 us: ring_reduce_scatter(): pl.pallas_call(_scatter_kernel, out_shape=(jax.ShapeDtypeStruct((n - 1, t...]
    psum x1 -> x0, waiting for transfers between devices: 58.6 us -> none  [per_device(): lax.psum(partial_value.astype(jnp.bfloat16), 'tp').astype(jnp.float32)]
    reduce_scatter x1 -> x0, waiting for transfers between devices: 28.7 us -> none  [per_device(): lax.psum_scatter(down_part.astype(jnp.bfloat16), 'tp', scatter_dimension=...]
    all_gather x1 -> x0, waiting for transfers between devices: 12.9 us -> none  [per_device(): full_states = lax.all_gather(states, 'tp', axis=1, tiled=True)]
    all_to_all x1, waiting for transfers between devices: 8.8 us -> 0.01 us  [per_device(): lax.all_to_all(jnp.broadcast_to(cand_ids[None], (device_count,) + cand_id...]
    reduce_sum x0 -> x2, other arithmetic: none -> 3.7 us  [the longest x1 1.85 us: per_device(): jnp.sum(down_recv.astype(jnp.float32), axis=0)]
  transfers between devices with their start and end apart: 5 -> 2, of which waited for: 5 -> 1; matrix products, arithmetic and copies ran while one was open for 1% -> 2% of each run, Pallas kernels for 0% -> 10%
where the time goes in v3:
time: 237 us; the launch traced here: 236 us
  Pallas kernels  101 us (43%)
  matrix products  41.8 us (18%)
  local copies, waits for them, and re-layouts  22.9 us (10%)
  blocking collectives  22.2 us (9%)
  starting transfers between devices  21.6 us (9%)
  other arithmetic  17.5 us (7%)
  waiting for transfers between devices  7.69 us (3%)
    pallas_call x2, Pallas kernels, ring_reduce_scatter(): pl.pallas_call(_scatter_kernel, out_shape=(jax.ShapeDtypeStruct((n - 1, t...  57.2 us
    pallas_call x2, Pallas kernels, ring_all_gather(): pl.pallas_call(_gather_kernel, out_shape=jax.ShapeDtypeStruct((texts, n *...  44.3 us
    gather x1, local copies, waits for them, and re-layouts, per_device(): jnp.take(all_scores.T, safe_ids.reshape(-1), axis=0)  15.7 us
    all_to_all x1, blocking collectives, per_device(): lax.all_to_all(owner_terms, ('req', 'tp'), 0, 0, tiled=True)  13.6 us
    dot_general x1, matrix products, per_device(): jnp.einsum('tsf,fd->tsd', up_act, w_down, preferred_element_type=jnp.floa...  12.7 us
    all_to_all x1, starting transfers between devices, per_device(): lax.all_to_all(jnp.broadcast_to(cand_ids[None], (device_count,) + cand_id...  11.5 us
    all_to_all x1, starting transfers between devices, per_device(): lax.all_to_all(jnp.broadcast_to(query_vec[None], (req_count,) + query_vec...  10.1 us
    psum x1, blocking collectives, per_device(): pooled = lax.psum(local_pool, 'tp') / lengths.astype(jnp.float32)[:, None]  8.58 us
  transfers between devices with their start and end apart: 2, of which 1 were waited for; matrix products, arithmetic and copies ran while one was open for 2% of the time, Pallas kernels for 10%

profile of v3, /device:TPU:1, one launch (start us, length us, event | category | flops | bytes accessed | tf_op | source)
XLA Modules:
  0.0 236.2 jit_solution(11370864319238990835)
XLA Ops:
  0.7 1.5 broadcast_in_dim.55
  2.2 11.5 %all-to-all-start = ((s32[128,2,16]{2,1,0:T(2,128)}), s32[128,2,16]{2,1,0:T(2,128)S(1)}, u32[]{:S(2)}, u32[]{:S(2)}) async-start(s32[128,2,16]{2,1,0:T(2,128)} %broadcast_in_dim.55), calls=%async_computation | async-start | bytes 262144 | tf_op jit(solution)/shard_map/all_to_all | solution.py:214
  17.6 22.7 %shard_map.167 = bf16[2,512,1024]{2,1,0:T(8,128)(2,1)} custom-call(bf16[2,128,1024]{2,1,0:T(8,128)(2,1)} %x_ref.1), custom_call_target="tpu_custom_call" | custom-call | tf_op jit(solution)/shard_map/pallas_call | solution.py:75
  41.5 3.9 %add_convert_fusion = bf16[2,512,3,256]{1,3,2,0:T(8,128)(2,1)S(1)} fusion(f32[3,256]{1,0:T(4,128)S(1)} %copy-done.17, bf16[1024,3,256]{2,0,1:T(8,128)(2,1)} %param.18, bf16[2,512,1024]{2,1,0:T(8,128)(2,1)} %shard_map.167), kind=kOutput, calls=%fused_computation.35 | convolution fusion | flops 1612185600 | bytes 5245952 | tf_op jit(solution)/shard_map/tsd,dce->tsce/dot_general | solution.py:223
  48.1 7.7 %fusion.107 = (f32[2,4,512]{2,1,0:T(4,128)S(1)}, f32[2,4,512,512]{2,3,1,0:T(8,128)}) fusion(pred[2,512,512]{1,2,0:T(8,128)(4,1)S(1)} %broadcast_and_fusion, bf16[2,512,4,64]{1,3,2,0:T(8,128)(2,1)} %bitcast.61, bf16[2,512,4,64]{1,3,2,0:T(8,128)(2,1)} %bitcast.60), kind=kOutput, calls=%fused_computation.149 | convolution fusion | flops 276824576 | bytes 9977856 | tf_op jit(solution)/shard_map/sub | solution.py:175
  55.7 4.3 %fusion.63 = bf16[2,4,64,512]{3,2,1,0:T(8,128)(2,1)S(1)} fusion(bf16[2,512,4,64]{1,3,2,0:T(8,128)(2,1)S(1)} %bitcast.59, f32[2,4,512,512]{2,3,1,0:T(8,128)} %get-tuple-element.24, f32[2,4,512]{2,1,0:T(4,128)S(1)} %get-tuple-element.23, pred[2,512]{1,0:T(4,128)(4,1)S(1)} %copy-done.9), kind=kOutput, calls=%fused_computation.77 | convolution fusion | flops 273154048 | bytes 9454592 | tf_op jit(solution)/shard_map/thqk,tkhe->tqhe/dot_general | solution.py:177
  60.1 2.1 convolution_convert_fusion.p_ref
  62.2 28.3 %shard_map.168 = (bf16[3,2,128,1024]{3,2,1,0:T(8,128)(2,1)}, bf16[2,128,1024]{2,1,0:T(8,128)(2,1)}) custom-call(bf16[2,512,1024]{2,1,0:T(8,128)(2,1)} %convolution_convert_fusion.p_ref), custom_call_target="tpu_custom_call" | custom-call | tf_op jit(solution)/shard_map/pallas_call | solution.py:130
  90.5 1.8 convert_reduce_fusion.1
  92.4 1.5 fusion.105
  95.3 21.5 %shard_map.169 = bf16[2,512,1024]{2,1,0:T(8,128)(2,1)} custom-call(bf16[2,128,1024]{2,1,0:T(8,128)(2,1)} %add_convert_fusion.2.x_ref), custom_call_target="tpu_custom_call" | custom-call | tf_op jit(solution)/shard_map/pallas_call | solution.py:75
  116.8 5.2 %fusion.65 = (u8[512,1024]{1,0:T(8,128)(4,1)S(1)}, u8[512,1024]{1,0:T(8,128)(4,1)S(1)}, f32[2,512,1024]{2,1,0:T(8,128)S(1)}) fusion(f32[1024]{0:T(1024)S(1)} %copy-done.18, bf16[2,512,1024]{2,1,0:T(8,128)(2,1)} %shard_map.169, bf16[1024,1024]{1,0:T(8,128)(2,1)S(1)} %copy-done), kind=kOutput, calls=%fused_computation.87 | convolution fusion | flops 2161115136 | bytes 9441280 | tf_op jit(solution)/shard_map/tsd,df->tsf/dot_general | solution.py:241
  122.0 12.7 %fusion.52.p_ref = bf16[2,512,1024]{2,1,0:T(8,128)(2,1)} fusion(bf16[1024,1024]{1,0:T(8,128)(2,1)S(1)} %copy-done.16, f32[2,512,1024]{2,1,0:T(8,128)S(1)} %get-tuple-element.25, f32[1024]{0:T(1024)S(1)} %copy-done.18, u8[512,1024]{1,0:T(8,128)(4,1)S(1)} %get-tuple-element.11, u8[512,1024]{1,0:T(8,128)(4,1)S(1)} %get-tuple-element.10), kind=kOutput, calls=%fused_computation.73 | convolution fusion | flops 2222981120 | bytes 9441280 | tf_op jit(solution)/shard_map/tsf,fd->tsd/dot_general | solution.py:244
  134.7 28.9 %shard_map.170 = (bf16[3,2,128,1024]{3,2,1,0:T(8,128)(2,1)}, bf16[2,128,1024]{2,1,0:T(8,128)(2,1)}) custom-call(bf16[2,512,1024]{2,1,0:T(8,128)(2,1)} %fusion.52.p_ref), custom_call_target="tpu_custom_call" | custom-call | tf_op jit(solution)/shard_map/pallas_call | solution.py:130
  163.6 1.8 convert_reduce_fusion
  165.5 1.5 fusion.104
  168.5 8.6 %psum.7 = f32[2,1024]{1,0:T(2,128)S(1)} all-reduce(f32[2,1024]{1,0:T(2,128)S(1)} %get-tuple-element.14), channel_id=1, replica_groups=mesh['req'=32,'tp'=4] {'tp'}, use_global_device_ids=true, to_apply=%region_9.10 | all-reduce | flops 2048 | bytes 16384 | tf_op jit(solution)/shard_map/psum | solution.py:259
  178.1 10.1 %all-to-all-start.1 = ((bf16[32,2,1024]{2,1,0:T(2,128)(2,1)}), bf16[32,2,1024]{2,1,0:T(2,128)(2,1)S(1)}, u32[]{:S(2)}, u32[]{:S(2)}) async-start(bf16[32,2,1024]{2,1,0:T(2,128)(2,1)} %broadcast_in_dim.63), calls=%async_computation.1 | async-start | bytes 262144 | tf_op jit(solution)/shard_map/all_to_all | solution.py:263
  188.2 7.7 %all-to-all-done.1 = bf16[32,2,1024]{2,1,0:T(2,128)(2,1)S(1)} async-done(((bf16[32,2,1024]{2,1,0:T(2,128)(2,1)}), bf16[32,2,1024]{2,1,0:T(2,128)(2,1)S(1)}, u32[]{:S(2)}, u32[]{:S(2)}) %all-to-all-start.1) | async-done | bytes 131104 | tf_op jit(solution)/shard_map/all_to_all | solution.py:263
  195.9 6.0 %convolution_bitcast_fusion = f32[4096,64]{0,1:T(8,128)S(1)} fusion(bf16[64,1024]{1,0:T(8,128)(2,1)S(1)} %reshape.217, bf16[4096,1024]{1,0:T(8,128)(2,1)} %param.30), kind=kOutput, calls=%fused_computation.7 | convolution fusion | flops 536870912 | bytes 9568256 | tf_op jit(solution)/shard_map/td,rd->tr/dot_general | solution.py:276
  201.9 1.9 copy.49
  203.9 15.7 %gather_fusion = f32[4096,64]{1,0:T(8,128)} fusion(f32[4096,64]{1,0:T(8,128)} %copy.49, s32[4096]{0:T(1024)S(1)} %broadcast_clamp_fusion), kind=kCustom, calls=%fused_computation | custom fusion | bytes 2113536 | tf_op jit(solution)/shard_map/jit(_take)/gather | solution.py:279
  219.6 1.9 select_reduce_fusion
  221.9 13.6 %all_to_all.15 = f32[128,2,16]{2,1,0:T(2,128)S(1)} all-to-all(f32[128,2,16]{2,1,0:T(2,128)S(1)} %copy.53), channel_id=1, replica_groups=mesh['req'=32,'tp'=4] {'req','tp'}, dimensions={0} | all-to-all | bytes 32768 | tf_op jit(solution)/shard_map/all_to_all | solution.py:289
  (77 shorter events, 12.5 us)
Async XLA Ops:
  0.6 116.2 %copy-start = (bf16[1024,1024]{1,0:T(8,128)(2,1)S(1)}, bf16[1024,1024]{1,0:T(8,128)(2,1)}, u32[]{:S(2)}) copy-start(bf16[1024,1024]{1,0:T(8,128)(2,1)} %param.24) | copy-start | bytes 6291460
  0.6 40.9 %copy-start.17 = (f32[3,256]{1,0:T(4,128)S(1)}, f32[3,256]{1,0:T(4,128)}, u32[]{:S(2)}) copy-start(f32[3,256]{1,0:T(4,128)} %param.19) | copy-start | bytes 9220
  2.2 38.2 %all-to-all-start = ((s32[128,2,16]{2,1,0:T(2,128)}), s32[128,2,16]{2,1,0:T(2,128)S(1)}, u32[]{:S(2)}, u32[]{:S(2)}) async-start(s32[128,2,16]{2,1,0:T(2,128)} %broadcast_in_dim.55), calls=%async_computation | async-start | bytes 262144 | tf_op jit(solution)/shard_map/all_to_all | solution.py:214
  14.6 0.6 copy-start.8
  41.5 5.1 %copy-start.2 = (pred[128,2,16]{2,1,0:T(4,128)(4,1)S(1)}, pred[128,2,16]{2,1,0:T(4,128)(4,1)}, u32[]{:S(2)}) copy-start(pred[128,2,16]{2,1,0:T(4,128)(4,1)} %compare_and_fusion) | copy-start | bytes 12292
  48.1 7.7 %copy-start.9 = (pred[2,512]{1,0:T(4,128)(4,1)S(1)}, pred[2,512]{1,0:T(4,128)(4,1)}, u32[]{:S(2)}) copy-start(pred[2,512]{1,0:T(4,128)(4,1)} %copy-done.8) | copy-start | bytes 3076
  55.7 4.3 %copy-start.1 = (bf16[256,1024]{1,0:T(8,128)(2,1)S(1)}, bf16[256,1024]{1,0:T(8,128)(2,1)}, u32[]{:S(2)}) copy-start(bf16[256,1024]{1,0:T(8,128)(2,1)} %param.20) | copy-start | bytes 1572868
  60.1 32.3 %copy-start.10 = (f32[1024]{0:T(1024)S(1)}, f32[1024]{0:T(1024)}, u32[]{:S(2)}) copy-start(f32[1024]{0:T(1024)} %param.21) | copy-start | bytes 12292
  62.2 32.0 %copy-start.6 = (f32[1024]{0:T(1024)S(1)}, f32[1024]{0:T(1024)}, u32[]{:S(2)}) copy-start(f32[1024]{0:T(1024)} %param.23) | copy-start | bytes 12292
  62.2 32.0 %copy-start.7 = (f32[1024]{0:T(1024)S(1)}, f32[1024]{0:T(1024)}, u32[]{:S(2)}) copy-start(f32[1024]{0:T(1024)} %param.22) | copy-start | bytes 12292
  92.4 24.4 %copy-start.18 = (f32[1024]{0:T(1024)S(1)}, f32[1024]{0:T(1024)}, u32[]{:S(2)}) copy-start(f32[1024]{0:T(1024)} %param.25) | copy-start | bytes 12292
  116.8 5.2 %copy-start.16 = (bf16[1024,1024]{1,0:T(8,128)(2,1)S(1)}, bf16[1024,1024]{1,0:T(8,128)(2,1)}, u32[]{:S(2)}) copy-start(bf16[1024,1024]{1,0:T(8,128)(2,1)} %param.26) | copy-start | bytes 6291460
  134.7 30.8 %copy-start.11 = (f32[1024]{0:T(1024)S(1)}, f32[1024]{0:T(1024)}, u32[]{:S(2)}) copy-start(f32[1024]{0:T(1024)} %param.27) | copy-start | bytes 12292
  163.5 3.7 %copy-start.12 = (f32[1024]{0:T(1024)S(1)}, f32[1024]{0:T(1024)}, u32[]{:S(2)}) copy-start(f32[1024]{0:T(1024)} %param.29) | copy-start | bytes 12292
  163.6 3.7 %copy-start.13 = (f32[1024]{0:T(1024)S(1)}, f32[1024]{0:T(1024)}, u32[]{:S(2)}) copy-start(f32[1024]{0:T(1024)} %param.28) | copy-start | bytes 12292
  163.6 3.7 %copy-start.14 = (pred[2,128]{1,0:T(4,128)(4,1)S(1)}, pred[2,128]{1,0:T(4,128)(4,1)}, u32[]{:S(2)}) copy-start(pred[2,128]{1,0:T(4,128)(4,1)} %broadcast_compare_fusion) | copy-start | bytes 772
  163.6 13.5 %copy-start.15 = (f32[2]{0:T(128)S(1)}, f32[2]{0:T(128)}, u32[]{:S(2)}) copy-start(f32[2]{0:T(128)} %convert_element_type.70) | copy-start | bytes 28
  178.1 17.8 %all-to-all-start.1 = ((bf16[32,2,1024]{2,1,0:T(2,128)(2,1)}), bf16[32,2,1024]{2,1,0:T(2,128)(2,1)S(1)}, u32[]{:S(2)}, u32[]{:S(2)}) async-start(bf16[32,2,1024]{2,1,0:T(2,128)(2,1)} %broadcast_in_dim.63), calls=%async_computation.1 | async-start | bytes 262144 | tf_op jit(solution)/shard_map/all_to_all | solution.py:263
  203.8 15.7 %copy-start.3 = (pred[64,64]{1,0:T(8,128)(4,1)S(1)}, pred[64,64]{1,0:T(8,128)(4,1)}, u32[]{:S(2)}) copy-start(pred[64,64]{1,0:T(8,128)(4,1)} %get-tuple-element.26) | copy-start | bytes 12292
  203.8 15.7 %copy-start.4 = (pred[64,64]{1,0:T(8,128)(4,1)S(1)}, pred[64,64]{1,0:T(8,128)(4,1)}, u32[]{:S(2)}) copy-start(pred[64,64]{1,0:T(8,128)(4,1)} %get-tuple-element.27) | copy-start | bytes 12292
  203.9 17.7 %copy-start.5 = (pred[64,64]{0,1:T(8,128)(4,1)S(1)}, pred[64,64]{0,1:T(8,128)(4,1)}, u32[]{:S(2)}) copy-start(pred[64,64]{0,1:T(8,128)(4,1)} %copy.50) | copy-start | bytes 12292

commit v4 on v3

--- a/solution.py
+++ b/solution.py
@@ -211,11 +211,7 @@
     quarter = cand_ids.shape[1]
     full_states = ring_all_gather(states, 0)
     device_count = req_count * tp_count
-    gathered_ids = lax.all_to_all(
-        jnp.broadcast_to(cand_ids[None], (device_count,) + cand_ids.shape),
-        ("req", "tp"), 0, 0, tiled=True,
-    )
-    full_states, gathered_ids = lax.optimization_barrier((full_states, gathered_ids))
+    text_ids = ring_all_gather(cand_ids[:, None, :], 4)
     seq_len = full_states.shape[1]
     local_width = w_qkv.shape[2]
     heads_here = local_width // HEAD_DIM
@@ -256,18 +252,20 @@
     local_pool = jnp.sum(
         jnp.where(is_valid[:, :, None], hidden_out.astype(jnp.float32), jnp.float32(0.0)), axis=1
     )
-    pooled = lax.psum(local_pool, "tp") / lengths.astype(jnp.float32)[:, None]
+    pooled = jnp.sum(ring_all_gather(local_pool[:, None, :], 5), axis=1) / lengths.astype(
+        jnp.float32
+    )[:, None]
     query_vec = (
         pooled * lax.rsqrt(jnp.mean(pooled * pooled, axis=-1, keepdims=True) + norm_eps)
     ).astype(jnp.bfloat16)
-    all_queries = lax.all_to_all(
-        jnp.broadcast_to(query_vec[None], (req_count,) + query_vec.shape), "req", 0, 0, tiled=True
-    ).reshape(req_count * text_count, model_width)
-    all_ids = (
-        gathered_ids.reshape(req_count, tp_count, text_count, quarter)
-        .transpose(0, 2, 1, 3)
-        .reshape(req_count * text_count, tp_count * quarter)
-    )
+    bundle = jnp.concatenate(
+        [query_vec.astype(jnp.float32), text_ids.reshape(text_count, -1).astype(jnp.float32)], axis=1
+    )
+    bundle = lax.all_to_all(
+        jnp.broadcast_to(bundle[None], (req_count,) + bundle.shape), "req", 0, 0, tiled=True
+    ).reshape(req_count * text_count, bundle.shape[1])
+    all_queries = bundle[:, :model_width].astype(jnp.bfloat16)
+    all_ids = bundle[:, model_width:].astype(jnp.int32)
     rows_here = index_rows.shape[0]
     first_row = (req_rank * tp_count + tp_rank) * rows_here
     local_ids = all_ids - first_row

time: 237 us -> 233 us (0.983)
  Pallas kernels: 101 us -> 114 us
  blocking collectives: 22.2 us -> 14.3 us
  starting transfers between devices: 21.6 us -> 13.9 us
    pallas_call x2 -> x4, Pallas kernels: 44.3 us -> 56.3 us  [ring_all_gather(): pl.pallas_call(_gather_kernel, out_shape=jax.ShapeDtypeStruct((texts, n *...]
    psum x1 -> x0, blocking collectives: 8.58 us -> none  [per_device(): pooled = lax.psum(local_pool, 'tp') / lengths.astype(jnp.float32)[:, None]]
    all_to_all x2 -> x1, starting transfers between devices: 21.6 us -> 13.9 us  [per_device(): lax.all_to_all(jnp.broadcast_to(bundle[None], (req_count,) + bundle.shape...]
    all_to_all x2 -> x1, waiting for transfers between devices: 7.69 us -> 9.29 us  [per_device(): lax.all_to_all(jnp.broadcast_to(bundle[None], (req_count,) + bundle.shape...]
  transfers between devices with their start and end apart: 2 -> 1, of which waited for: 1 -> 1; matrix products, arithmetic and copies ran while one was open for 2% -> 0% of each run, Pallas kernels for 10% -> 0%
where the time goes in v4:
time: 233 us; the launch traced here: 232 us
  Pallas kernels  114 us (49%)
  matrix products  41.8 us (18%)
  local copies, waits for them, and re-layouts  21.2 us (9%)
  other arithmetic  17.2 us (7%)
  blocking collectives  14.3 us (6%)
  starting transfers between devices  13.9 us (6%)
  waiting for transfers between devices  9.29 us (4%)
    pallas_call x2, Pallas kernels, ring_reduce_scatter(): pl.pallas_call(_scatter_kernel, out_shape=(jax.ShapeDtypeStruct((n - 1, t...  57.2 us
    pallas_call x4, Pallas kernels, ring_all_gather(): pl.pallas_call(_gather_kernel, out_shape=jax.ShapeDtypeStruct((texts, n *...  56.3 us
    gather x1, local copies, waits for them, and re-layouts, per_device(): jnp.take(all_scores.T, safe_ids.reshape(-1), axis=0)  15.7 us
    all_to_all x1, blocking collectives, per_device(): lax.all_to_all(owner_terms, ('req', 'tp'), 0, 0, tiled=True)  14.3 us
    all_to_all x1, starting transfers between devices, per_device(): lax.all_to_all(jnp.broadcast_to(bundle[None], (req_count,) + bundle.shape...  13.9 us
    dot_general x1, matrix products, per_device(): jnp.einsum('tsf,fd->tsd', up_act, w_down, preferred_element_type=jnp.floa...  12.6 us
    all_to_all x1, waiting for transfers between devices, per_device(): lax.all_to_all(jnp.broadcast_to(bundle[None], (req_count,) + bundle.shape...  9.29 us
    sub x1, matrix products, window_attention(): expo = jnp.exp(logits - top_val)  7.67 us
  transfers between devices with their start and end apart: 1, of which 1 were waited for; matrix products, arithmetic and copies ran while one was open for 0% of the time, Pallas kernels for 0%

profile of v4, /device:TPU:1, one launch (start us, length us, event | category | flops | bytes accessed | tf_op | source)
XLA Modules:
  0.0 232.2 jit_solution(17022655340833877583)
XLA Ops:
  2.3 23.1 %shard_map.167 = bf16[2,512,1024]{2,1,0:T(8,128)(2,1)} custom-call(bf16[2,128,1024]{2,1,0:T(8,128)(2,1)} %x_ref.1), custom_call_target="tpu_custom_call" | custom-call | tf_op jit(solution)/shard_map/pallas_call | solution.py:75
  25.4 3.9 %add_convert_fusion = bf16[2,512,3,256]{1,3,2,0:T(8,128)(2,1)S(1)} fusion(f32[3,256]{1,0:T(4,128)} %param.19, bf16[1024,3,256]{2,0,1:T(8,128)(2,1)} %param.18, bf16[2,512,1024]{2,1,0:T(8,128)(2,1)} %shard_map.167), kind=kOutput, calls=%fused_computation.35 | convolution fusion | flops 1612185600 | bytes 5245952 | tf_op jit(solution)/shard_map/tsd,dce->tsce/dot_general | solution.py:219
  30.8 7.7 %fusion.110 = (f32[2,4,512]{2,1,0:T(4,128)S(1)}, f32[2,4,512,512]{2,3,1,0:T(8,128)}) fusion(pred[2,512,512]{1,2,0:T(8,128)(4,1)S(1)} %broadcast_and_fusion, bf16[2,512,4,64]{1,3,2,0:T(8,128)(2,1)} %bitcast.55, bf16[2,512,4,64]{1,3,2,0:T(8,128)(2,1)} %bitcast.54), kind=kOutput, calls=%fused_computation.151 | convolution fusion | flops 276824576 | bytes 9977856 | tf_op jit(solution)/shard_map/sub | solution.py:175
  38.5 4.3 %fusion.63 = bf16[2,4,64,512]{3,2,1,0:T(8,128)(2,1)S(1)} fusion(bf16[2,512,4,64]{1,3,2,0:T(8,128)(2,1)S(1)} %bitcast.53, f32[2,4,512,512]{2,3,1,0:T(8,128)} %get-tuple-element.22, f32[2,4,512]{2,1,0:T(4,128)S(1)} %get-tuple-element.21, pred[2,512]{1,0:T(4,128)(4,1)S(1)} %iota_compare_fusion.1), kind=kOutput, calls=%fused_computation.77 | convolution fusion | flops 273154048 | bytes 9454592 | tf_op jit(solution)/shard_map/thqk,tkhe->tqhe/dot_general | solution.py:177
  42.8 2.1 convolution_convert_fusion.p_ref
  44.9 28.3 %shard_map.168 = (bf16[3,2,128,1024]{3,2,1,0:T(8,128)(2,1)}, bf16[2,128,1024]{2,1,0:T(8,128)(2,1)}) custom-call(bf16[2,512,1024]{2,1,0:T(8,128)(2,1)} %convolution_convert_fusion.p_ref), custom_call_target="tpu_custom_call" | custom-call | tf_op jit(solution)/shard_map/pallas_call | solution.py:130
  73.2 2.8 %convert_reduce_fusion.1 = f32[2,128,1024]{2,1,0:T(8,128)} fusion(bf16[3,2,128,1024]{3,2,1,0:T(8,128)(2,1)} %get-tuple-element.4), kind=kLoop, calls=%fused_computation.34 | loop fusion | flops 1310720 | bytes 2621440 | tf_op jit(solution)/shard_map/reduce_sum | solution.py:231
  76.0 1.8 fusion.108
  79.2 21.5 %shard_map.169 = bf16[2,512,1024]{2,1,0:T(8,128)(2,1)} custom-call(bf16[2,128,1024]{2,1,0:T(8,128)(2,1)} %add_convert_fusion.2.x_ref), custom_call_target="tpu_custom_call" | custom-call | tf_op jit(solution)/shard_map/pallas_call | solution.py:75
  100.7 5.2 %fusion.65 = (u8[512,1024]{1,0:T(8,128)(4,1)S(1)}, u8[512,1024]{1,0:T(8,128)(4,1)S(1)}, f32[2,512,1024]{2,1,0:T(8,128)S(1)}) fusion(f32[1024]{0:T(1024)S(1)} %copy-done.10, bf16[2,512,1024]{2,1,0:T(8,128)(2,1)} %shard_map.169, bf16[1024,1024]{1,0:T(8,128)(2,1)S(1)} %copy-done), kind=kOutput, calls=%fused_computation.87 | convolution fusion | flops 2161115136 | bytes 9441280 | tf_op jit(solution)/shard_map/tsd,df->tsf/dot_general | solution.py:237
  105.9 12.6 %fusion.52.p_ref = bf16[2,512,1024]{2,1,0:T(8,128)(2,1)} fusion(bf16[1024,1024]{1,0:T(8,128)(2,1)S(1)} %copy-done.9, f32[2,512,1024]{2,1,0:T(8,128)S(1)} %get-tuple-element.23, f32[1024]{0:T(1024)S(1)} %copy-done.10, u8[512,1024]{1,0:T(8,128)(4,1)S(1)} %get-tuple-element.7, u8[512,1024]{1,0:T(8,128)(4,1)S(1)} %get-tuple-element.6), kind=kOutput, calls=%fused_computation.73 | convolution fusion | flops 2222981120 | bytes 9441280 | tf_op jit(solution)/shard_map/tsf,fd->tsd/dot_general | solution.py:240
  118.6 28.9 %shard_map.170 = (bf16[3,2,128,1024]{3,2,1,0:T(8,128)(2,1)}, bf16[2,128,1024]{2,1,0:T(8,128)(2,1)}) custom-call(bf16[2,512,1024]{2,1,0:T(8,128)(2,1)} %fusion.52.p_ref), custom_call_target="tpu_custom_call" | custom-call | tf_op jit(solution)/shard_map/pallas_call | solution.py:130
  147.5 1.8 convert_reduce_fusion
  149.4 1.5 fusion.107
  151.3 1.2 select_reduce_fusion.1
  153.0 6.5 %shard_map.171 = f32[2,4,1024]{2,1,0:T(4,128)} custom-call(f32[2,1,1024]{2,1,0:T(1,128)} %broadcast_in_dim.65.x_ref), custom_call_target="tpu_custom_call" | custom-call | tf_op jit(solution)/shard_map/pallas_call | solution.py:75
  160.5 5.2 %shard_map.172 = s32[2,4,16]{2,1,0:T(4,128)} custom-call(s32[2,1,16]{2,1,0:T(1,128)} %bitcast.58), custom_call_target="tpu_custom_call" | custom-call | tf_op jit(solution)/shard_map/pallas_call | solution.py:75
  167.4 13.9 %all-to-all-start = ((f32[32,2,1088]{2,1,0:T(2,128)}), f32[32,2,1088]{2,1,0:T(2,128)S(1)}, u32[]{:S(2)}, u32[]{:S(2)}) async-start(f32[32,2,1088]{2,1,0:T(2,128)} %broadcast_in_dim.104), calls=%async_computation | async-start | bytes 589824 | tf_op jit(solution)/shard_map/all_to_all | solution.py:264
  181.3 9.3 %all-to-all-done = f32[32,2,1088]{2,1,0:T(2,128)S(1)} async-done(((f32[32,2,1088]{2,1,0:T(2,128)}), f32[32,2,1088]{2,1,0:T(2,128)S(1)}, u32[]{:S(2)}, u32[]{:S(2)}) %all-to-all-start) | async-done | bytes 278560 | tf_op jit(solution)/shard_map/all_to_all | solution.py:264
  190.8 6.0 %convolution_bitcast_fusion = f32[4096,64]{0,1:T(8,128)S(1)} fusion(bf16[4096,1024]{1,0:T(8,128)(2,1)} %param.30, f32[64,1088]{1,0:T(8,128)S(1)} %reshape.193), kind=kOutput, calls=%fused_computation.7 | convolution fusion | flops 536870912 | bytes 9568256 | tf_op jit(solution)/shard_map/td,rd->tr/dot_general | solution.py:274
  196.8 2.0 copy.46
  199.2 15.7 %gather_fusion = f32[4096,64]{1,0:T(8,128)} fusion(f32[4096,64]{1,0:T(8,128)} %copy.46, s32[4096]{0:T(1024)S(1)} %broadcast_clamp_fusion), kind=kCustom, calls=%fused_computation | custom fusion | bytes 2113536 | tf_op jit(solution)/shard_map/jit(_take)/gather | solution.py:277
  214.9 1.9 select_reduce_fusion
  217.2 14.3 %all_to_all.10 = f32[128,2,16]{2,1,0:T(2,128)S(1)} all-to-all(f32[128,2,16]{2,1,0:T(2,128)S(1)} %copy.49), channel_id=1, replica_groups=mesh['req'=32,'tp'=4] {'req','tp'}, dimensions={0} | all-to-all | bytes 32768 | tf_op jit(solution)/shard_map/all_to_all | solution.py:287
  (61 shorter events, 9.7 us)
Async XLA Ops:
  0.6 100.1 %copy-start = (bf16[1024,1024]{1,0:T(8,128)(2,1)S(1)}, bf16[1024,1024]{1,0:T(8,128)(2,1)}, u32[]{:S(2)}) copy-start(bf16[1024,1024]{1,0:T(8,128)(2,1)} %param.24) | copy-start | bytes 6291460
  38.5 4.3 %copy-start.1 = (bf16[256,1024]{1,0:T(8,128)(2,1)S(1)}, bf16[256,1024]{1,0:T(8,128)(2,1)}, u32[]{:S(2)}) copy-start(bf16[256,1024]{1,0:T(8,128)(2,1)} %param.20) | copy-start | bytes 1572868
  42.8 33.2 %copy-start.4 = (f32[1024]{0:T(1024)S(1)}, f32[1024]{0:T(1024)}, u32[]{:S(2)}) copy-start(f32[1024]{0:T(1024)} %param.21) | copy-start | bytes 12292
  44.9 33.2 %copy-start.2 = (f32[1024]{0:T(1024)S(1)}, f32[1024]{0:T(1024)}, u32[]{:S(2)}) copy-start(f32[1024]{0:T(1024)} %param.23) | copy-start | bytes 12292
  44.9 33.2 %copy-start.3 = (f32[1024]{0:T(1024)S(1)}, f32[1024]{0:T(1024)}, u32[]{:S(2)}) copy-start(f32[1024]{0:T(1024)} %param.22) | copy-start | bytes 12292
  76.0 24.7 %copy-start.10 = (f32[1024]{0:T(1024)S(1)}, f32[1024]{0:T(1024)}, u32[]{:S(2)}) copy-start(f32[1024]{0:T(1024)} %param.25) | copy-start | bytes 12292
  100.7 5.2 %copy-start.9 = (bf16[1024,1024]{1,0:T(8,128)(2,1)S(1)}, bf16[1024,1024]{1,0:T(8,128)(2,1)}, u32[]{:S(2)}) copy-start(bf16[1024,1024]{1,0:T(8,128)(2,1)} %param.26) | copy-start | bytes 6291460
  118.6 30.8 %copy-start.5 = (f32[1024]{0:T(1024)S(1)}, f32[1024]{0:T(1024)}, u32[]{:S(2)}) copy-start(f32[1024]{0:T(1024)} %param.27) | copy-start | bytes 12292
  147.5 3.7 %copy-start.8 = (s32[2]{0:T(128)S(1)}, s32[2]{0:T(128)}, u32[]{:S(2)}) copy-start(s32[2]{0:T(128)} %param.17) | copy-start | bytes 28
  147.5 3.8 %copy-start.6 = (f32[1024]{0:T(1024)S(1)}, f32[1024]{0:T(1024)}, u32[]{:S(2)}) copy-start(f32[1024]{0:T(1024)} %param.29) | copy-start | bytes 12292
  147.5 3.8 %copy-start.7 = (f32[1024]{0:T(1024)S(1)}, f32[1024]{0:T(1024)}, u32[]{:S(2)}) copy-start(f32[1024]{0:T(1024)} %param.28) | copy-start | bytes 12292
  167.4 23.2 %all-to-all-start = ((f32[32,2,1088]{2,1,0:T(2,128)}), f32[32,2,1088]{2,1,0:T(2,128)S(1)}, u32[]{:S(2)}, u32[]{:S(2)}) async-start(f32[32,2,1088]{2,1,0:T(2,128)} %broadcast_in_dim.104), calls=%async_computation | async-start | bytes 589824 | tf_op jit(solution)/shard_map/all_to_all | solution.py:264

commit v5 on v4

--- a/solution.py
+++ b/solution.py
@@ -26,109 +26,115 @@
     return me, rq, core, right, left, opp, relay_to, relay_from
 
 
-def _gather_kernel(x_ref, out_ref, send_sem, recv_sem, local_sem):
+def _gather_kernel(chunks, x_ref, out_ref, send_sem, recv_sem, local_sem):
     me, rq, core, right, left, opp, relay_to, relay_from = _ring_peers()
     rows = x_ref.shape[1]
-
-    def slot(src):
-        return out_ref.at[:, pl.ds(src * rows, rows), :]
-
-    local = pltpu.make_async_copy(x_ref, slot(me), local_sem)
+    step = rows // chunks
+
+    def part(ref, k):
+        return ref.at[:, pl.ds(k * step, step), :]
+
+    def slot(src, k):
+        return out_ref.at[:, pl.ds(src * rows + k * step, step), :]
+
+    def copy(src, dst, send, recv, peer):
+        return pltpu.make_async_remote_copy(
+            src, dst, send, recv, device_id=(rq, peer), device_id_type=MESH_ID
+        )
+
+    local = pltpu.make_async_copy(x_ref, out_ref.at[:, pl.ds(me * rows, rows), :], local_sem)
     local.start()
-    to_right = pltpu.make_async_remote_copy(
-        x_ref, slot(me), send_sem.at[0], recv_sem.at[0], device_id=(rq, right), device_id_type=MESH_ID
-    )
-    to_left = pltpu.make_async_remote_copy(
-        x_ref, slot(me), send_sem.at[1], recv_sem.at[1], device_id=(rq, left), device_id_type=MESH_ID
-    )
-    to_right.start()
-    to_left.start()
-    from_relay = pltpu.make_async_remote_copy(
-        x_ref, slot(relay_from), send_sem.at[2], recv_sem.at[core], device_id=(rq, relay_to),
-        device_id_type=MESH_ID,
-    )
-    from_relay.wait_recv()
-    forward = pltpu.make_async_remote_copy(
-        slot(relay_from), slot(relay_from), send_sem.at[2], recv_sem.at[2], device_id=(rq, relay_to),
-        device_id_type=MESH_ID,
-    )
-    forward.start()
+    sends = []
+    for k in range(chunks):
+        to_right = copy(part(x_ref, k), slot(me, k), send_sem.at[0, k], recv_sem.at[0, k], right)
+        to_left = copy(part(x_ref, k), slot(me, k), send_sem.at[1, k], recv_sem.at[1, k], left)
+        to_right.start()
+        to_left.start()
+        sends += [to_right, to_left]
+    for k in range(chunks):
+        copy(part(x_ref, k), slot(relay_from, k), send_sem.at[2, k], recv_sem.at[core, k], right).wait_recv()
+        forward = copy(
+            slot(relay_from, k), slot(relay_from, k), send_sem.at[2, k], recv_sem.at[2, k], relay_to
+        )
+        forward.start()
+        sends.append(forward)
     other_side = (me + 1 + 2 * (1 - core)) % lax.axis_size("tp")
-    from_other = pltpu.make_async_remote_copy(
-        x_ref, slot(other_side), send_sem.at[0], recv_sem.at[1 - core], device_id=(rq, right),
-        device_id_type=MESH_ID,
-    )
-    from_other.wait_recv()
-    from_opp = pltpu.make_async_remote_copy(
-        x_ref, slot(opp), send_sem.at[0], recv_sem.at[2], device_id=(rq, right), device_id_type=MESH_ID
-    )
-    from_opp.wait_recv()
-    to_right.wait_send()
-    to_left.wait_send()
-    forward.wait_send()
+    for k in range(chunks):
+        copy(part(x_ref, k), slot(other_side, k), send_sem.at[0, k], recv_sem.at[1 - core, k], right).wait_recv()
+    for k in range(chunks):
+        copy(part(x_ref, k), slot(opp, k), send_sem.at[0, k], recv_sem.at[2, k], right).wait_recv()
+    for c in sends:
+        c.wait_send()
     local.wait()
 
 
-def ring_all_gather(x, collective_id):
+def ring_all_gather(x, collective_id, chunks=1):
     texts, rows, width = x.shape
     n = lax.axis_size("tp")
     return pl.pallas_call(
-        _gather_kernel,
+        functools.partial(_gather_kernel, chunks),
         out_shape=jax.ShapeDtypeStruct((texts, n * rows, width), x.dtype),
         in_specs=[pl.BlockSpec(memory_space=pl.ANY)],
         out_specs=pl.BlockSpec(memory_space=pl.ANY),
         scratch_shapes=[
-            pltpu.SemaphoreType.DMA((3,)),
-            pltpu.SemaphoreType.DMA((3,)),
+            pltpu.SemaphoreType.DMA((3, chunks)),
+            pltpu.SemaphoreType.DMA((3, chunks)),
             pltpu.SemaphoreType.DMA,
         ],
         compiler_params=pltpu.CompilerParams(collective_id=collective_id, has_side_effects=True),
     )(x)
 
 
-def _scatter_kernel(p_ref, recv_ref, relay_ref, send_sem, recv_sem, relay_sem):
+def _scatter_kernel(chunks, p_ref, recv_ref, relay_ref, send_sem, recv_sem, relay_sem):
     me, rq, core, right, left, opp, relay_to, relay_from = _ring_peers()
     rows = recv_ref.shape[2]
-
-    def block(dst):
-        return p_ref.at[:, pl.ds(dst * rows, rows), :]
-
-    to_right = pltpu.make_async_remote_copy(
-        block(right), recv_ref.at[0], send_sem.at[0], recv_sem.at[0], device_id=(rq, right),
-        device_id_type=MESH_ID,
-    )
-    to_left = pltpu.make_async_remote_copy(
-        block(left), recv_ref.at[1], send_sem.at[1], recv_sem.at[1], device_id=(rq, left),
-        device_id_type=MESH_ID,
-    )
-    to_relay = pltpu.make_async_remote_copy(
-        block(opp), relay_ref, send_sem.at[2], relay_sem, device_id=(rq, relay_to),
-        device_id_type=MESH_ID,
-    )
-    to_right.start()
-    to_left.start()
-    to_relay.start()
-    to_relay.wait_recv()
-    forward = pltpu.make_async_remote_copy(
-        relay_ref, recv_ref.at[2], send_sem.at[3], recv_sem.at[2], device_id=(rq, relay_to),
-        device_id_type=MESH_ID,
-    )
-    forward.start()
-    to_right.wait_recv()
-    to_left.wait_recv()
-    forward.wait_recv()
-    to_right.wait_send()
-    to_left.wait_send()
-    to_relay.wait_send()
-    forward.wait_send()
-
-
-def ring_reduce_scatter(p, collective_id):
+    step = rows // chunks
+
+    def block(dst, k):
+        return p_ref.at[:, pl.ds(dst * rows + k * step, step), :]
+
+    def part(ref, k):
+        return ref.at[:, pl.ds(k * step, step), :]
+
+    def copy(src, dst, send, recv, peer):
+        return pltpu.make_async_remote_copy(
+            src, dst, send, recv, device_id=(rq, peer), device_id_type=MESH_ID
+        )
+
+    sends = []
+    relays = []
+    for k in range(chunks):
+        to_relay = copy(block(opp, k), part(relay_ref, k), send_sem.at[2, k], relay_sem.at[k], relay_to)
+        to_right = copy(block(right, k), part(recv_ref.at[0], k), send_sem.at[0, k], recv_sem.at[0, k], right)
+        to_left = copy(block(left, k), part(recv_ref.at[1], k), send_sem.at[1, k], recv_sem.at[1, k], left)
+        to_relay.start()
+        to_right.start()
+        to_left.start()
+        sends += [to_relay, to_right, to_left]
+        relays.append(to_relay)
+    forwards = []
+    for k in range(chunks):
+        relays[k].wait_recv()
+        forward = copy(
+            part(relay_ref, k), part(recv_ref.at[2], k), send_sem.at[3, k], recv_sem.at[2, k], relay_to
+        )
+        forward.start()
+        sends.append(forward)
+        forwards.append(forward)
+    for k in range(chunks):
+        sends[3 * k + 1].wait_recv()
+        sends[3 * k + 2].wait_recv()
+        forwards[k].wait_recv()
+    for c in sends:
+        c.wait_send()
+
+
+def ring_reduce_scatter(p, collective_id, chunks=1):
     texts, all_rows, width = p.shape
     n = lax.axis_size("tp")
     rows = all_rows // n
     recv, _ = pl.pallas_call(
-        _scatter_kernel,
+        functools.partial(_scatter_kernel, chunks),
         out_shape=(
             jax.ShapeDtypeStruct((n - 1, texts, rows, width), p.dtype),
             jax.ShapeDtypeStruct((texts, rows, width), p.dtype),
@@ -136,9 +142,9 @@
         in_specs=[pl.BlockSpec(memory_space=pl.ANY)],
         out_specs=(pl.BlockSpec(memory_space=pl.ANY), pl.BlockSpec(memory_space=pl.ANY)),
         scratch_shapes=[
-            pltpu.SemaphoreType.DMA((4,)),
-            pltpu.SemaphoreType.DMA((3,)),
-            pltpu.SemaphoreType.DMA,
+            pltpu.SemaphoreType.DMA((4, chunks)),
+            pltpu.SemaphoreType.DMA((3, chunks)),
+            pltpu.SemaphoreType.DMA((chunks,)),
         ],
         compiler_params=pltpu.CompilerParams(collective_id=collective_id, has_side_effects=True),
     )(p)
@@ -146,6 +152,7 @@
 
 
 HEAD_DIM = 64
+RING_CHUNKS = 4
 WINDOW = 512
 
 
@@ -209,7 +216,7 @@
     req_rank = lax.axis_index("req")
     text_count, row_share, model_width = states.shape
     quarter = cand_ids.shape[1]
-    full_states = ring_all_gather(states, 0)
+    full_states = ring_all_gather(states, 0, RING_CHUNKS)
     device_count = req_count * tp_count
     text_ids = ring_all_gather(cand_ids[:, None, :], 4)
     seq_len = full_states.shape[1]
@@ -225,14 +232,14 @@
     context = window_attention(queries_h, keys_h, values_h, lengths)
     partial_value = jnp.einsum("tsk,kd->tsd", context, w_out, preferred_element_type=jnp.float32)
     partial_value = partial_value.astype(jnp.bfloat16)
-    attn_recv = ring_reduce_scatter(partial_value, 1)
+    attn_recv = ring_reduce_scatter(partial_value, 1, RING_CHUNKS)
     attn_sum = lax.dynamic_slice_in_dim(partial_value, tp_rank * row_share, row_share, 1).astype(
         jnp.float32
     ) + jnp.sum(attn_recv.astype(jnp.float32), axis=0)
     normed_local = layer_norm(
         states.astype(jnp.float32) + attn_sum + b_out, ln1_gain, ln1_shift
     ).astype(jnp.bfloat16)
-    normed_full = ring_all_gather(normed_local, 2)
+    normed_full = ring_all_gather(normed_local, 2, RING_CHUNKS)
     up_act = jax.nn.gelu(
         jnp.einsum("tsd,df->tsf", normed_full, w_up, preferred_element_type=jnp.float32) + b_up,
         approximate=False,
@@ -240,7 +247,7 @@
     down_part = jnp.einsum(
         "tsf,fd->tsd", up_act, w_down, preferred_element_type=jnp.float32
     ).astype(jnp.bfloat16)
-    down_recv = ring_reduce_scatter(down_part, 3)
+    down_recv = ring_reduce_scatter(down_part, 3, RING_CHUNKS)
     down_sum = lax.dynamic_slice_in_dim(down_part, tp_rank * row_share, row_share, 1).astype(
         jnp.float32
     ) + jnp.sum(down_recv.astype(jnp.float32), axis=0)

time: 233 us -> 226 us (0.970)
  Pallas kernels: 114 us -> 109 us
    pallas_call x6, Pallas kernels: 114 us -> 109 us  [the longest x4 56.3 us: ring_all_gather(): pl.pallas_call(functools.partial(_gather_kernel, chunks), out_shape=jax.S...]
where the time goes in v5:
time: 226 us; the launch traced here: 225 us
  Pallas kernels  109 us (48%)
  matrix products  41.8 us (18%)
  local copies, waits for them, and re-layouts  21.2 us (9%)
  other arithmetic  17.2 us (8%)
  blocking collectives  14.2 us (6%)
  starting transfers between devices  11.9 us (5%)
  waiting for transfers between devices  9.29 us (4%)
    pallas_call x4, Pallas kernels, ring_all_gather(): pl.pallas_call(functools.partial(_gather_kernel, chunks), out_shape=jax.S...  56.3 us
    pallas_call x2, Pallas kernels, ring_reduce_scatter(): pl.pallas_call(functools.partial(_scatter_kernel, chunks), out_shape=(jax...  52.5 us
    gather x1, local copies, waits for them, and re-layouts, per_device(): jnp.take(all_scores.T, safe_ids.reshape(-1), axis=0)  15.7 us
    all_to_all x1, blocking collectives, per_device(): lax.all_to_all(owner_terms, ('req', 'tp'), 0, 0, tiled=True)  14.2 us
    dot_general x1, matrix products, per_device(): jnp.einsum('tsf,fd->tsd', up_act, w_down, preferred_element_type=jnp.floa...  12.6 us
    all_to_all x1, starting transfers between devices, per_device(): lax.all_to_all(jnp.broadcast_to(bundle[None], (req_count,) + bundle.shape...  11.9 us
    all_to_all x1, waiting for transfers between devices, per_device(): lax.all_to_all(jnp.broadcast_to(bundle[None], (req_count,) + bundle.shape...  9.29 us
    sub x1, matrix products, window_attention(): expo = jnp.exp(logits - top_val)  7.66 us
  transfers between devices with their start and end apart: 1, of which 1 were waited for; matrix products, arithmetic and copies ran while one was open for 0% of the time, Pallas kernels for 0%

profile of v5, /device:TPU:1, one launch (start us, length us, event | category | flops | bytes accessed | tf_op | source)
XLA Modules:
  0.0 225.4 jit_solution(4239652908726639797)
XLA Ops:
  2.3 21.9 %shard_map.167 = bf16[2,512,1024]{2,1,0:T(8,128)(2,1)} custom-call(bf16[2,128,1024]{2,1,0:T(8,128)(2,1)} %x_ref.1), custom_call_target="tpu_custom_call" | custom-call | tf_op jit(solution)/shard_map/pallas_call | solution.py:74
  24.3 3.9 %add_convert_fusion = bf16[2,512,3,256]{1,3,2,0:T(8,128)(2,1)S(1)} fusion(f32[3,256]{1,0:T(4,128)} %param.19, bf16[1024,3,256]{2,0,1:T(8,128)(2,1)} %param.18, bf16[2,512,1024]{2,1,0:T(8,128)(2,1)} %shard_map.167), kind=kOutput, calls=%fused_computation.35 | convolution fusion | flops 1612185600 | bytes 5245952 | tf_op jit(solution)/shard_map/tsd,dce->tsce/dot_general | solution.py:226
  29.7 7.7 %fusion.110 = (f32[2,4,512]{2,1,0:T(4,128)S(1)}, f32[2,4,512,512]{2,3,1,0:T(8,128)}) fusion(pred[2,512,512]{1,2,0:T(8,128)(4,1)S(1)} %broadcast_and_fusion, bf16[2,512,4,64]{1,3,2,0:T(8,128)(2,1)} %bitcast.55, bf16[2,512,4,64]{1,3,2,0:T(8,128)(2,1)} %bitcast.54), kind=kOutput, calls=%fused_computation.151 | convolution fusion | flops 276824576 | bytes 9977856 | tf_op jit(solution)/shard_map/sub | solution.py:182
  37.3 4.3 %fusion.63 = bf16[2,4,64,512]{3,2,1,0:T(8,128)(2,1)S(1)} fusion(bf16[2,512,4,64]{1,3,2,0:T(8,128)(2,1)S(1)} %bitcast.53, f32[2,4,512,512]{2,3,1,0:T(8,128)} %get-tuple-element.22, f32[2,4,512]{2,1,0:T(4,128)S(1)} %get-tuple-element.21, pred[2,512]{1,0:T(4,128)(4,1)S(1)} %iota_compare_fusion.1), kind=kOutput, calls=%fused_computation.77 | convolution fusion | flops 273154048 | bytes 9454592 | tf_op jit(solution)/shard_map/thqk,tkhe->tqhe/dot_general | solution.py:184
  41.6 2.1 convolution_convert_fusion.p_ref
  43.7 25.9 %shard_map.168 = (bf16[3,2,128,1024]{3,2,1,0:T(8,128)(2,1)}, bf16[2,128,1024]{2,1,0:T(8,128)(2,1)}) custom-call(bf16[2,512,1024]{2,1,0:T(8,128)(2,1)} %convolution_convert_fusion.p_ref), custom_call_target="tpu_custom_call" | custom-call | tf_op jit(solution)/shard_map/pallas_call | solution.py:136
  69.7 2.8 %convert_reduce_fusion.1 = f32[2,128,1024]{2,1,0:T(8,128)} fusion(bf16[3,2,128,1024]{3,2,1,0:T(8,128)(2,1)} %get-tuple-element.4), kind=kLoop, calls=%fused_computation.34 | loop fusion | flops 1310720 | bytes 2621440 | tf_op jit(solution)/shard_map/reduce_sum | solution.py:238
  72.5 1.8 fusion.108
  75.6 21.1 %shard_map.169 = bf16[2,512,1024]{2,1,0:T(8,128)(2,1)} custom-call(bf16[2,128,1024]{2,1,0:T(8,128)(2,1)} %add_convert_fusion.2.x_ref), custom_call_target="tpu_custom_call" | custom-call | tf_op jit(solution)/shard_map/pallas_call | solution.py:74
  96.7 5.2 %fusion.65 = (u8[512,1024]{1,0:T(8,128)(4,1)S(1)}, u8[512,1024]{1,0:T(8,128)(4,1)S(1)}, f32[2,512,1024]{2,1,0:T(8,128)S(1)}) fusion(f32[1024]{0:T(1024)S(1)} %copy-done.10, bf16[2,512,1024]{2,1,0:T(8,128)(2,1)} %shard_map.169, bf16[1024,1024]{1,0:T(8,128)(2,1)S(1)} %copy-done), kind=kOutput, calls=%fused_computation.87 | convolution fusion | flops 2161115136 | bytes 9441280 | tf_op jit(solution)/shard_map/tsd,df->tsf/dot_general | solution.py:244
  101.9 12.6 %fusion.52.p_ref = bf16[2,512,1024]{2,1,0:T(8,128)(2,1)} fusion(bf16[1024,1024]{1,0:T(8,128)(2,1)S(1)} %copy-done.9, f32[2,512,1024]{2,1,0:T(8,128)S(1)} %get-tuple-element.23, f32[1024]{0:T(1024)S(1)} %copy-done.10, u8[512,1024]{1,0:T(8,128)(4,1)S(1)} %get-tuple-element.7, u8[512,1024]{1,0:T(8,128)(4,1)S(1)} %get-tuple-element.6), kind=kOutput, calls=%fused_computation.73 | convolution fusion | flops 2222981120 | bytes 9441280 | tf_op jit(solution)/shard_map/tsf,fd->tsd/dot_general | solution.py:247
  114.6 26.6 %shard_map.170 = (bf16[3,2,128,1024]{3,2,1,0:T(8,128)(2,1)}, bf16[2,128,1024]{2,1,0:T(8,128)(2,1)}) custom-call(bf16[2,512,1024]{2,1,0:T(8,128)(2,1)} %fusion.52.p_ref), custom_call_target="tpu_custom_call" | custom-call | tf_op jit(solution)/shard_map/pallas_call | solution.py:136
  141.2 1.8 convert_reduce_fusion
  143.1 1.5 fusion.107
  145.0 1.2 select_reduce_fusion.1
  146.7 6.8 %shard_map.171 = f32[2,4,1024]{2,1,0:T(4,128)} custom-call(f32[2,1,1024]{2,1,0:T(1,128)} %broadcast_in_dim.65.x_ref), custom_call_target="tpu_custom_call" | custom-call | tf_op jit(solution)/shard_map/pallas_call | solution.py:74
  154.6 6.4 %shard_map.172 = s32[2,4,16]{2,1,0:T(4,128)} custom-call(s32[2,1,16]{2,1,0:T(1,128)} %bitcast.58), custom_call_target="tpu_custom_call" | custom-call | tf_op jit(solution)/shard_map/pallas_call | solution.py:74
  162.6 11.9 %all-to-all-start = ((f32[32,2,1088]{2,1,0:T(2,128)}), f32[32,2,1088]{2,1,0:T(2,128)S(1)}, u32[]{:S(2)}, u32[]{:S(2)}) async-start(f32[32,2,1088]{2,1,0:T(2,128)} %broadcast_in_dim.104), calls=%async_computation | async-start | bytes 589824 | tf_op jit(solution)/shard_map/all_to_all | solution.py:271
  174.6 9.3 %all-to-all-done = f32[32,2,1088]{2,1,0:T(2,128)S(1)} async-done(((f32[32,2,1088]{2,1,0:T(2,128)}), f32[32,2,1088]{2,1,0:T(2,128)S(1)}, u32[]{:S(2)}, u32[]{:S(2)}) %all-to-all-start) | async-done | bytes 278560 | tf_op jit(solution)/shard_map/all_to_all | solution.py:271
  184.1 6.0 %convolution_bitcast_fusion = f32[4096,64]{0,1:T(8,128)S(1)} fusion(bf16[4096,1024]{1,0:T(8,128)(2,1)} %param.30, f32[64,1088]{1,0:T(8,128)S(1)} %reshape.193), kind=kOutput, calls=%fused_computation.7 | convolution fusion | flops 536870912 | bytes 9568256 | tf_op jit(solution)/shard_map/td,rd->tr/dot_general | solution.py:281
  190.1 2.0 copy.46
  192.5 15.7 %gather_fusion = f32[4096,64]{1,0:T(8,128)} fusion(f32[4096,64]{1,0:T(8,128)} %copy.46, s32[4096]{0:T(1024)S(1)} %broadcast_clamp_fusion), kind=kCustom, calls=%fused_computation | custom fusion | bytes 2113536 | tf_op jit(solution)/shard_map/jit(_take)/gather | solution.py:284
  208.2 1.9 select_reduce_fusion
  210.5 14.2 %all_to_all.10 = f32[128,2,16]{2,1,0:T(2,128)S(1)} all-to-all(f32[128,2,16]{2,1,0:T(2,128)S(1)} %copy.49), channel_id=1, replica_groups=mesh['req'=32,'tp'=4] {'req','tp'}, dimensions={0} | all-to-all | bytes 32768 | tf_op jit(solution)/shard_map/all_to_all | solution.py:294
  (61 shorter events, 9.7 us)
Async XLA Ops:
  0.6 96.1 %copy-start = (bf16[1024,1024]{1,0:T(8,128)(2,1)S(1)}, bf16[1024,1024]{1,0:T(8,128)(2,1)}, u32[]{:S(2)}) copy-start(bf16[1024,1024]{1,0:T(8,128)(2,1)} %param.24) | copy-start | bytes 6291460
  37.3 4.3 %copy-start.1 = (bf16[256,1024]{1,0:T(8,128)(2,1)S(1)}, bf16[256,1024]{1,0:T(8,128)(2,1)}, u32[]{:S(2)}) copy-start(bf16[256,1024]{1,0:T(8,128)(2,1)} %param.20) | copy-start | bytes 1572868
  41.6 30.8 %copy-start.4 = (f32[1024]{0:T(1024)S(1)}, f32[1024]{0:T(1024)}, u32[]{:S(2)}) copy-start(f32[1024]{0:T(1024)} %param.21) | copy-start | bytes 12292
  43.7 30.8 %copy-start.2 = (f32[1024]{0:T(1024)S(1)}, f32[1024]{0:T(1024)}, u32[]{:S(2)}) copy-start(f32[1024]{0:T(1024)} %param.23) | copy-start | bytes 12292
  43.7 30.8 %copy-start.3 = (f32[1024]{0:T(1024)S(1)}, f32[1024]{0:T(1024)}, u32[]{:S(2)}) copy-start(f32[1024]{0:T(1024)} %param.22) | copy-start | bytes 12292
  72.4 24.3 %copy-start.10 = (f32[1024]{0:T(1024)S(1)}, f32[1024]{0:T(1024)}, u32[]{:S(2)}) copy-start(f32[1024]{0:T(1024)} %param.25) | copy-start | bytes 12292
  96.7 5.2 %copy-start.9 = (bf16[1024,1024]{1,0:T(8,128)(2,1)S(1)}, bf16[1024,1024]{1,0:T(8,128)(2,1)}, u32[]{:S(2)}) copy-start(bf16[1024,1024]{1,0:T(8,128)(2,1)} %param.26) | copy-start | bytes 6291460
  114.6 28.5 %copy-start.5 = (f32[1024]{0:T(1024)S(1)}, f32[1024]{0:T(1024)}, u32[]{:S(2)}) copy-start(f32[1024]{0:T(1024)} %param.27) | copy-start | bytes 12292
  141.2 3.7 %copy-start.8 = (s32[2]{0:T(128)S(1)}, s32[2]{0:T(128)}, u32[]{:S(2)}) copy-start(s32[2]{0:T(128)} %param.17) | copy-start | bytes 28
  141.2 3.8 %copy-start.6 = (f32[1024]{0:T(1024)S(1)}, f32[1024]{0:T(1024)}, u32[]{:S(2)}) copy-start(f32[1024]{0:T(1024)} %param.29) | copy-start | bytes 12292
  141.2 3.8 %copy-start.7 = (f32[1024]{0:T(1024)S(1)}, f32[1024]{0:T(1024)}, u32[]{:S(2)}) copy-start(f32[1024]{0:T(1024)} %param.28) | copy-start | bytes 12292
  162.6 21.2 %all-to-all-start = ((f32[32,2,1088]{2,1,0:T(2,128)}), f32[32,2,1088]{2,1,0:T(2,128)S(1)}, u32[]{:S(2)}, u32[]{:S(2)}) async-start(f32[32,2,1088]{2,1,0:T(2,128)} %broadcast_in_dim.104), calls=%async_computation | async-start | bytes 589824 | tf_op jit(solution)/shard_map/all_to_all | solution.py:271

commit v6 on v5

--- a/solution.py
+++ b/solution.py
@@ -149,6 +149,85 @@
         compiler_params=pltpu.CompilerParams(collective_id=collective_id, has_side_effects=True),
     )(p)
     return recv
+
+
+def _peer_id(axes, peer):
+    if axes == ("tp",):
+        return (lax.axis_index("req"), peer)
+    if axes == ("req",):
+        return (peer, lax.axis_index("tp"))
+    n_tp = lax.axis_size("tp")
+    return (peer // n_tp, peer % n_tp)
+
+
+def _direct_kernel(axes, scatter, x_ref, out_ref, send_sem, recv_sem, local_sem):
+    n = out_ref.shape[0]
+    me = lax.axis_index(axes)
+    barrier = pltpu.get_barrier_semaphore()
+
+    def greet(d, carry):
+        peer = (me + d) % n
+        pl.semaphore_signal(barrier, inc=1, device_id=_peer_id(axes, peer), device_id_type=MESH_ID)
+        return carry
+
+    lax.fori_loop(1, n, greet, 0)
+    pl.semaphore_wait(barrier, n - 1)
+
+    def source(peer):
+        return x_ref.at[peer] if scatter else x_ref
+
+    local = pltpu.make_async_copy(source(me), out_ref.at[me], local_sem)
+    local.start()
+
+    def send(d, carry):
+        peer = (me + d) % n
+        pltpu.make_async_remote_copy(
+            source(peer), out_ref.at[me], send_sem.at[d], recv_sem.at[me],
+            device_id=_peer_id(axes, peer), device_id_type=MESH_ID,
+        ).start()
+        return carry
+
+    lax.fori_loop(1, n, send, 0)
+
+    def receive(d, carry):
+        src = (me + n - d) % n
+        pltpu.make_async_remote_copy(
+            source(src), out_ref.at[src], send_sem.at[d], recv_sem.at[src],
+            device_id=_peer_id(axes, src), device_id_type=MESH_ID,
+        ).wait_recv()
+        return carry
+
+    lax.fori_loop(1, n, receive, 0)
+
+    def sent(d, carry):
+        peer = (me + d) % n
+        pltpu.make_async_remote_copy(
+            source(peer), out_ref.at[me], send_sem.at[d], recv_sem.at[me],
+            device_id=_peer_id(axes, peer), device_id_type=MESH_ID,
+        ).wait_send()
+        return carry
+
+    lax.fori_loop(1, n, sent, 0)
+    local.wait()
+
+
+def direct_exchange(x, axes, collective_id, scatter=False):
+    n = 1
+    for name in axes:
+        n *= lax.axis_size(name)
+    block = x.shape[1:] if scatter else x.shape
+    return pl.pallas_call(
+        functools.partial(_direct_kernel, axes, scatter),
+        out_shape=jax.ShapeDtypeStruct((n,) + block, x.dtype),
+        in_specs=[pl.BlockSpec(memory_space=pl.ANY)],
+        out_specs=pl.BlockSpec(memory_space=pl.ANY),
+        scratch_shapes=[
+            pltpu.SemaphoreType.DMA((n,)),
+            pltpu.SemaphoreType.DMA((n,)),
+            pltpu.SemaphoreType.DMA,
+        ],
+        compiler_params=pltpu.CompilerParams(collective_id=collective_id, has_side_effects=True),
+    )(x)
 
 
 HEAD_DIM = 64
@@ -218,7 +297,7 @@
     quarter = cand_ids.shape[1]
     full_states = ring_all_gather(states, 0, RING_CHUNKS)
     device_count = req_count * tp_count
-    text_ids = ring_all_gather(cand_ids[:, None, :], 4)
+    text_ids = jnp.swapaxes(direct_exchange(cand_ids, ("tp",), 4), 0, 1)
     seq_len = full_states.shape[1]
     local_width = w_qkv.shape[2]
     heads_here = local_width // HEAD_DIM
@@ -259,7 +338,7 @@
     local_pool = jnp.sum(
         jnp.where(is_valid[:, :, None], hidden_out.astype(jnp.float32), jnp.float32(0.0)), axis=1
     )
-    pooled = jnp.sum(ring_all_gather(local_pool[:, None, :], 5), axis=1) / lengths.astype(
+    pooled = jnp.sum(direct_exchange(local_pool, ("tp",), 5), axis=0) / lengths.astype(
         jnp.float32
     )[:, None]
     query_vec = (
@@ -268,9 +347,7 @@
     bundle = jnp.concatenate(
         [query_vec.astype(jnp.float32), text_ids.reshape(text_count, -1).astype(jnp.float32)], axis=1
     )
-    bundle = lax.all_to_all(
-        jnp.broadcast_to(bundle[None], (req_count,) + bundle.shape), "req", 0, 0, tiled=True
-    ).reshape(req_count * text_count, bundle.shape[1])
+    bundle = direct_exchange(bundle, ("req",), 6).reshape(req_count * text_count, bundle.shape[1])
     all_queries = bundle[:, :model_width].astype(jnp.bfloat16)
     all_ids = bundle[:, model_width:].astype(jnp.int32)
     rows_here = index_rows.shape[0]
@@ -291,7 +368,7 @@
         .transpose(0, 2, 1, 3)
         .reshape(device_count, text_count, quarter)
     )
-    scores = jnp.sum(lax.all_to_all(owner_terms, ("req", "tp"), 0, 0, tiled=True), axis=0)
+    scores = jnp.sum(direct_exchange(owner_terms, ("req", "tp"), 7, scatter=True), axis=0)
     return (hidden_out, scores)
 
 

time: 226 us -> 222 us (0.982)
  Pallas kernels: 109 us -> 140 us
  blocking collectives: 14.2 us -> 0 us
  starting transfers between devices: 11.9 us -> 0 us
  waiting for transfers between devices: 9.29 us -> 0 us
    pallas_call x0 -> x4, Pallas kernels: none -> 44 us  [direct_exchange(): pl.pallas_call(functools.partial(_direct_kernel, axes, scatter), out_shap...]
    all_to_all x1 -> x0, blocking collectives: 14.2 us -> none  [per_device(): lax.all_to_all(owner_terms, ('req', 'tp'), 0, 0, tiled=True)]
    pallas_call x4 -> x2, Pallas kernels: 56.3 us -> 43.1 us  [ring_all_gather(): pl.pallas_call(functools.partial(_gather_kernel, chunks), out_shape=jax.S...]
    all_to_all x1 -> x0, starting transfers between devices: 11.9 us -> none  [per_device(): lax.all_to_all(jnp.broadcast_to(bundle[None], (req_count,) + bundle.shape...]
    all_to_all x1 -> x0, waiting for transfers between devices: 9.29 us -> none  [per_device(): lax.all_to_all(jnp.broadcast_to(bundle[None], (req_count,) + bundle.shape...]
  transfers between devices with their start and end apart: 1 -> 0, of which waited for: 1 -> 0; matrix products, arithmetic and copies ran while one was open for 0% -> 0% of each run, Pallas kernels for 0% -> 0%
where the time goes in v6:
time: 222 us
  Pallas kernels  140 us (63%)
  matrix products  41.8 us (19%)
  local copies, waits for them, and re-layouts  21.4 us (10%)
  other arithmetic  17.9 us (8%)
    pallas_call x2, Pallas kernels, ring_reduce_scatter(): pl.pallas_call(functools.partial(_scatter_kernel, chunks), out_shape=(jax...  52.5 us
    pallas_call x4, Pallas kernels, direct_exchange(): pl.pallas_call(functools.partial(_direct_kernel, axes, scatter), out_shap...  44 us
    pallas_call x2, Pallas kernels, ring_all_gather(): pl.pallas_call(functools.partial(_gather_kernel, chunks), out_shape=jax.S...  43.1 us
    gather x1, local copies, waits for them, and re-layouts, per_device(): jnp.take(all_scores.T, safe_ids.reshape(-1), axis=0)  15.7 us
    dot_general x1, matrix products, per_device(): jnp.einsum('tsf,fd->tsd', up_act, w_down, preferred_element_type=jnp.floa...  12.6 us
    sub x1, matrix products, window_attention(): expo = jnp.exp(logits - top_val)  7.66 us
    dot_general x1, matrix products, per_device(): jnp.einsum('td,rd->tr', all_queries, index_rows, preferred_element_type=j...  6.04 us
    dot_general x1, matrix products, per_device(): jnp.einsum('tsd,df->tsf', normed_full, w_up, preferred_element_type=jnp.f...  5.16 us

profile of v6, /device:TPU:1, one launch (start us, length us, event | category | flops | bytes accessed | tf_op | source)
XLA Modules:
  0.0 221.7 jit_solution(11384117771172515187)
XLA Ops:
  0.6 22.0 %shard_map.167 = bf16[2,512,1024]{2,1,0:T(8,128)(2,1)} custom-call(bf16[2,128,1024]{2,1,0:T(8,128)(2,1)} %x_ref.2), custom_call_target="tpu_custom_call" | custom-call | tf_op jit(solution)/shard_map/pallas_call | solution.py:74
  22.7 3.9 %add_convert_fusion = bf16[2,512,3,256]{1,3,2,0:T(8,128)(2,1)S(1)} fusion(f32[3,256]{1,0:T(4,128)} %param.19, bf16[1024,3,256]{2,0,1:T(8,128)(2,1)} %param.18, bf16[2,512,1024]{2,1,0:T(8,128)(2,1)} %shard_map.167), kind=kOutput, calls=%fused_computation.35 | convolution fusion | flops 1612185600 | bytes 5245952 | tf_op jit(solution)/shard_map/tsd,dce->tsce/dot_general | solution.py:305
  28.3 7.7 %fusion.110 = (f32[2,4,512]{2,1,0:T(4,128)S(1)}, f32[2,4,512,512]{2,3,1,0:T(8,128)}) fusion(pred[2,512,512]{1,2,0:T(8,128)(4,1)S(1)} %broadcast_and_fusion, bf16[2,512,4,64]{1,3,2,0:T(8,128)(2,1)} %bitcast.54, bf16[2,512,4,64]{1,3,2,0:T(8,128)(2,1)} %bitcast.53), kind=kOutput, calls=%fused_computation.152 | convolution fusion | flops 276824576 | bytes 9977856 | tf_op jit(solution)/shard_map/sub | solution.py:261
  36.0 4.3 %fusion.63 = bf16[2,4,64,512]{3,2,1,0:T(8,128)(2,1)S(1)} fusion(bf16[2,512,4,64]{1,3,2,0:T(8,128)(2,1)S(1)} %bitcast.52, f32[2,4,512,512]{2,3,1,0:T(8,128)} %get-tuple-element.22, f32[2,4,512]{2,1,0:T(4,128)S(1)} %get-tuple-element.21, pred[2,512]{1,0:T(4,128)(4,1)S(1)} %iota_compare_fusion.1), kind=kOutput, calls=%fused_computation.77 | convolution fusion | flops 273154048 | bytes 9454592 | tf_op jit(solution)/shard_map/thqk,tkhe->tqhe/dot_general | solution.py:263
  40.3 2.1 convolution_convert_fusion.p_ref
  42.4 25.9 %shard_map.168 = (bf16[3,2,128,1024]{3,2,1,0:T(8,128)(2,1)}, bf16[2,128,1024]{2,1,0:T(8,128)(2,1)}) custom-call(bf16[2,512,1024]{2,1,0:T(8,128)(2,1)} %convolution_convert_fusion.p_ref), custom_call_target="tpu_custom_call" | custom-call | tf_op jit(solution)/shard_map/pallas_call | solution.py:136
  68.4 2.8 %convert_reduce_fusion.1 = f32[2,128,1024]{2,1,0:T(8,128)} fusion(bf16[3,2,128,1024]{3,2,1,0:T(8,128)(2,1)} %get-tuple-element.4), kind=kLoop, calls=%fused_computation.34 | loop fusion | flops 1310720 | bytes 2621440 | tf_op jit(solution)/shard_map/reduce_sum | solution.py:317
  71.1 1.8 fusion.108
  74.3 21.1 %shard_map.169 = bf16[2,512,1024]{2,1,0:T(8,128)(2,1)} custom-call(bf16[2,128,1024]{2,1,0:T(8,128)(2,1)} %add_convert_fusion.2.x_ref), custom_call_target="tpu_custom_call" | custom-call | tf_op jit(solution)/shard_map/pallas_call | solution.py:74
  95.4 5.2 %fusion.65 = (u8[512,1024]{1,0:T(8,128)(4,1)S(1)}, u8[512,1024]{1,0:T(8,128)(4,1)S(1)}, f32[2,512,1024]{2,1,0:T(8,128)S(1)}) fusion(f32[1024]{0:T(1024)S(1)} %copy-done.10, bf16[2,512,1024]{2,1,0:T(8,128)(2,1)} %shard_map.169, bf16[1024,1024]{1,0:T(8,128)(2,1)S(1)} %copy-done), kind=kOutput, calls=%fused_computation.87 | convolution fusion | flops 2161115136 | bytes 9441280 | tf_op jit(solution)/shard_map/tsd,df->tsf/dot_general | solution.py:323
  100.6 12.6 %fusion.52.p_ref = bf16[2,512,1024]{2,1,0:T(8,128)(2,1)} fusion(bf16[1024,1024]{1,0:T(8,128)(2,1)S(1)} %copy-done.9, f32[2,512,1024]{2,1,0:T(8,128)S(1)} %get-tuple-element.23, f32[1024]{0:T(1024)S(1)} %copy-done.10, u8[512,1024]{1,0:T(8,128)(4,1)S(1)} %get-tuple-element.7, u8[512,1024]{1,0:T(8,128)(4,1)S(1)} %get-tuple-element.6), kind=kOutput, calls=%fused_computation.73 | convolution fusion | flops 2222981120 | bytes 9441280 | tf_op jit(solution)/shard_map/tsf,fd->tsd/dot_general | solution.py:326
  113.2 26.6 %shard_map.170 = (bf16[3,2,128,1024]{3,2,1,0:T(8,128)(2,1)}, bf16[2,128,1024]{2,1,0:T(8,128)(2,1)}) custom-call(bf16[2,512,1024]{2,1,0:T(8,128)(2,1)} %fusion.52.p_ref), custom_call_target="tpu_custom_call" | custom-call | tf_op jit(solution)/shard_map/pallas_call | solution.py:136
  139.9 1.8 convert_reduce_fusion
  141.8 1.5 fusion.107
  143.7 1.7 select_reduce_fusion.1
  145.4 5.9 %shard_map.171 = f32[4,2,1024]{2,1,0:T(2,128)} custom-call(f32[2,1024]{1,0:T(2,128)} %get-tuple-element.12.x_ref), custom_call_target="tpu_custom_call" | custom-call | tf_op jit(solution)/shard_map/pallas_call | solution.py:219
  152.4 4.8 %shard_map.172 = s32[4,2,16]{2,1,0:T(2,128)} custom-call(s32[2,16]{1,0:T(2,128)} %x_ref.3), custom_call_target="tpu_custom_call" | custom-call | tf_op jit(solution)/shard_map/pallas_call | solution.py:219
  158.5 15.7 %shard_map.173 = f32[32,2,1088]{2,1,0:T(2,128)} custom-call(f32[2,1088]{1,0:T(2,128)} %pad_maximum_fusion.x_ref), custom_call_target="tpu_custom_call" | custom-call | tf_op jit(solution)/shard_map/pallas_call | solution.py:219
  175.4 6.0 %convolution_bitcast_fusion = f32[4096,64]{0,1:T(8,128)S(1)} fusion(bf16[4096,1024]{1,0:T(8,128)(2,1)} %param.30, f32[64,1088]{1,0:T(8,128)S(1)} %reshape.192), kind=kOutput, calls=%fused_computation.7 | convolution fusion | flops 536870912 | bytes 9568256 | tf_op jit(solution)/shard_map/td,rd->tr/dot_general | solution.py:358
  181.5 2.0 copy.45
  183.8 15.7 %gather_fusion = f32[4096,64]{1,0:T(8,128)} fusion(f32[4096,64]{1,0:T(8,128)} %copy.45, s32[4096]{0:T(1024)S(1)} %broadcast_clamp_fusion), kind=kCustom, calls=%fused_computation | custom fusion | bytes 2113536 | tf_op jit(solution)/shard_map/jit(_take)/gather | solution.py:361
  199.6 1.9 select_reduce_fusion
  202.5 17.6 %shard_map.174 = f32[128,2,16]{2,1,0:T(2,128)} custom-call(f32[128,2,16]{2,1,0:T(2,128)} %bitcast.51), custom_call_target="tpu_custom_call" | custom-call | tf_op jit(solution)/shard_map/pallas_call | solution.py:219
  220.0 1.6 reduce_sum.119
  (58 shorter events, 8.3 us)
Async XLA Ops:
  0.6 94.7 %copy-start = (bf16[1024,1024]{1,0:T(8,128)(2,1)S(1)}, bf16[1024,1024]{1,0:T(8,128)(2,1)}, u32[]{:S(2)}) copy-start(bf16[1024,1024]{1,0:T(8,128)(2,1)} %param.24) | copy-start | bytes 6291460
  22.7 5.1 %copy-start.8 = (s32[2]{0:T(128)S(1)}, s32[2]{0:T(128)}, u32[]{:S(2)}) copy-start(s32[2]{0:T(128)} %param.17) | copy-start | bytes 28
  36.0 4.3 %copy-start.1 = (bf16[256,1024]{1,0:T(8,128)(2,1)S(1)}, bf16[256,1024]{1,0:T(8,128)(2,1)}, u32[]{:S(2)}) copy-start(bf16[256,1024]{1,0:T(8,128)(2,1)} %param.20) | copy-start | bytes 1572868
  40.3 30.8 %copy-start.4 = (f32[1024]{0:T(1024)S(1)}, f32[1024]{0:T(1024)}, u32[]{:S(2)}) copy-start(f32[1024]{0:T(1024)} %param.21) | copy-start | bytes 12292
  42.4 30.8 %copy-start.2 = (f32[1024]{0:T(1024)S(1)}, f32[1024]{0:T(1024)}, u32[]{:S(2)}) copy-start(f32[1024]{0:T(1024)} %param.23) | copy-start | bytes 12292
  42.4 30.8 %copy-start.3 = (f32[1024]{0:T(1024)S(1)}, f32[1024]{0:T(1024)}, u32[]{:S(2)}) copy-start(f32[1024]{0:T(1024)} %param.22) | copy-start | bytes 12292
  71.1 24.3 %copy-start.10 = (f32[1024]{0:T(1024)S(1)}, f32[1024]{0:T(1024)}, u32[]{:S(2)}) copy-start(f32[1024]{0:T(1024)} %param.25) | copy-start | bytes 12292
  95.4 5.2 %copy-start.9 = (bf16[1024,1024]{1,0:T(8,128)(2,1)S(1)}, bf16[1024,1024]{1,0:T(8,128)(2,1)}, u32[]{:S(2)}) copy-start(bf16[1024,1024]{1,0:T(8,128)(2,1)} %param.26) | copy-start | bytes 6291460
  113.2 28.5 %copy-start.5 = (f32[1024]{0:T(1024)S(1)}, f32[1024]{0:T(1024)}, u32[]{:S(2)}) copy-start(f32[1024]{0:T(1024)} %param.27) | copy-start | bytes 12292
  139.9 3.8 %copy-start.6 = (f32[1024]{0:T(1024)S(1)}, f32[1024]{0:T(1024)}, u32[]{:S(2)}) copy-start(f32[1024]{0:T(1024)} %param.29) | copy-start | bytes 12292
  139.9 3.8 %copy-start.7 = (f32[1024]{0:T(1024)S(1)}, f32[1024]{0:T(1024)}, u32[]{:S(2)}) copy-start(f32[1024]{0:T(1024)} %param.28) | copy-start | bytes 12292

commit v7 on v6

--- a/solution.py
+++ b/solution.py
@@ -232,6 +232,7 @@
 
 HEAD_DIM = 64
 RING_CHUNKS = 4
+SPARSE_PAIRS = 128
 WINDOW = 512
 
 
@@ -355,20 +356,37 @@
     local_ids = all_ids - first_row
     is_owned = (local_ids >= 0) & (local_ids < rows_here)
     safe_ids = jnp.clip(local_ids, 0, rows_here - 1)
-    all_scores = jnp.einsum(
-        "td,rd->tr", all_queries, index_rows, preferred_element_type=jnp.float32
-    )
-    score_rows = jnp.take(all_scores.T, safe_ids.reshape(-1), axis=0).reshape(
-        safe_ids.shape[0], safe_ids.shape[1], safe_ids.shape[0]
-    )
-    picked = jnp.einsum("tct->tc", score_rows)
-    owner_terms = jnp.where(is_owned, picked, jnp.float32(0.0))
+    owned_count = jnp.sum(is_owned.astype(jnp.int32))
+
+    def few_owned(_):
+        flat_owned = is_owned.reshape(-1)
+        (pair_at,) = jnp.nonzero(flat_owned, size=SPARSE_PAIRS, fill_value=0)
+        valid = jnp.arange(SPARSE_PAIRS) < owned_count
+        rows = jnp.take(index_rows, safe_ids.reshape(-1)[pair_at], axis=0)
+        queries = jnp.take(all_queries, pair_at // all_ids.shape[1], axis=0)
+        values = jnp.sum(rows.astype(jnp.float32) * queries.astype(jnp.float32), axis=-1)
+        values = jnp.where(valid, values, jnp.float32(0.0))
+        return (
+            jnp.zeros(flat_owned.shape, jnp.float32).at[pair_at].add(values).reshape(all_ids.shape)
+        )
+
+    def many_owned(_):
+        all_scores = jnp.einsum(
+            "td,rd->tr", all_queries, index_rows, preferred_element_type=jnp.float32
+        )
+        score_rows = jnp.take(all_scores.T, safe_ids.reshape(-1), axis=0).reshape(
+            safe_ids.shape[0], safe_ids.shape[1], safe_ids.shape[0]
+        )
+        picked = jnp.einsum("tct->tc", score_rows)
+        return jnp.where(is_owned, picked, jnp.float32(0.0))
+
+    owner_terms = lax.cond(owned_count <= SPARSE_PAIRS, few_owned, many_owned, None)
     owner_terms = (
         owner_terms.reshape(req_count, text_count, tp_count, quarter)
         .transpose(0, 2, 1, 3)
         .reshape(device_count, text_count, quarter)
     )
-    scores = jnp.sum(direct_exchange(owner_terms, ("req", "tp"), 7, scatter=True), axis=0)
+    scores = jnp.sum(lax.all_to_all(owner_terms, ("req", "tp"), 0, 0, tiled=True), axis=0)
     return (hidden_out, scores)
 
 

time: 222 us -> 239 us (1.077)
  other arithmetic: 17.9 us -> 51.2 us
  Pallas kernels: 140 us -> 122 us
  blocking collectives: 0 us -> 16.9 us
  local copies, waits for them, and re-layouts: 21.4 us -> 10.9 us
  matrix products: 41.8 us -> 35.8 us
    scatter-add x0 -> x2, other arithmetic: none -> 30.2 us  [the longest x1 28.8 us: few_owned(): pair_at, = jnp.nonzero(flat_owned, size=SPARSE_PAIRS, fill_value=0)]
    pallas_call x4 -> x3, Pallas kernels: 44 us -> 26.4 us  [direct_exchange(): pl.pallas_call(functools.partial(_direct_kernel, axes, scatter), out_shap...]
    all_to_all x0 -> x1, blocking collectives: none -> 16.9 us  [per_device(): lax.all_to_all(owner_terms, ('req', 'tp'), 0, 0, tiled=True)]
    gather x1 -> x4, local copies, waits for them, and re-layouts: 15.7 us -> 7.63 us  [the longest x3 6.77 us: few_owned(): rows = jnp.take(index_rows, safe_ids.reshape(-1)[pair_at], axis=0)]
    dot_general x1 -> x0, matrix products: 6.04 us -> none  [per_device(): jnp.einsum('td,rd->tr', all_queries, index_rows, preferred_element_type=j...]
where the time goes in v7:
time: 239 us; the launch traced here: 238 us
  Pallas kernels  122 us (51%)
  other arithmetic  51.2 us (21%)
  matrix products  35.8 us (15%)
  blocking collectives  16.9 us (7%)
  local copies, waits for them, and re-layouts  10.9 us (5%)
    pallas_call x2, Pallas kernels, ring_reduce_scatter(): pl.pallas_call(functools.partial(_scatter_kernel, chunks), out_shape=(jax...  52.5 us
    pallas_call x2, Pallas kernels, ring_all_gather(): pl.pallas_call(functools.partial(_gather_kernel, chunks), out_shape=jax.S...  43 us
    scatter-add x1, other arithmetic, few_owned(): pair_at, = jnp.nonzero(flat_owned, size=SPARSE_PAIRS, fill_value=0)  28.8 us
    pallas_call x3, Pallas kernels, direct_exchange(): pl.pallas_call(functools.partial(_direct_kernel, axes, scatter), out_shap...  26.4 us
    all_to_all x1, blocking collectives, per_device(): lax.all_to_all(owner_terms, ('req', 'tp'), 0, 0, tiled=True)  16.9 us
    dot_general x1, matrix products, per_device(): jnp.einsum('tsf,fd->tsd', up_act, w_down, preferred_element_type=jnp.floa...  12.6 us
    sub x1, matrix products, window_attention(): expo = jnp.exp(logits - top_val)  7.66 us
    gather x3, local copies, waits for them, and re-layouts, few_owned(): rows = jnp.take(index_rows, safe_ids.reshape(-1)[pair_at], axis=0)  6.77 us

profile of v7, /device:TPU:1, one launch (start us, length us, event | category | flops | bytes accessed | tf_op | source)
XLA Modules:
  0.0 238.4 jit_solution(9569078888809493910)
XLA Ops:
  2.3 21.9 %shard_map.167 = bf16[2,512,1024]{2,1,0:T(8,128)(2,1)} custom-call(bf16[2,128,1024]{2,1,0:T(8,128)(2,1)} %x_ref.2), custom_call_target="tpu_custom_call" | custom-call | tf_op jit(solution)/shard_map/pallas_call | solution.py:74
  24.3 3.9 %add_convert_fusion = bf16[2,512,3,256]{1,3,2,0:T(8,128)(2,1)S(1)} fusion(f32[3,256]{1,0:T(4,128)} %param.21, bf16[1024,3,256]{2,0,1:T(8,128)(2,1)} %param.20, bf16[2,512,1024]{2,1,0:T(8,128)(2,1)} %shard_map.167), kind=kOutput, calls=%fused_computation.91 | convolution fusion | flops 1612185600 | bytes 5245952 | tf_op jit(solution)/shard_map/tsd,dce->tsce/dot_general | solution.py:306
  29.7 7.7 %fusion.123 = (f32[2,4,512]{2,1,0:T(4,128)S(1)}, f32[2,4,512,512]{2,3,1,0:T(8,128)}) fusion(pred[2,512,512]{1,2,0:T(8,128)(4,1)S(1)} %broadcast_and_fusion, bf16[2,512,4,64]{1,3,2,0:T(8,128)(2,1)} %bitcast.57, bf16[2,512,4,64]{1,3,2,0:T(8,128)(2,1)} %bitcast.56), kind=kOutput, calls=%fused_computation.205 | convolution fusion | flops 276824576 | bytes 9977856 | tf_op jit(solution)/shard_map/sub | solution.py:262
  37.3 4.3 %fusion.75 = bf16[2,4,64,512]{3,2,1,0:T(8,128)(2,1)S(1)} fusion(bf16[2,512,4,64]{1,3,2,0:T(8,128)(2,1)S(1)} %bitcast.55, f32[2,4,512,512]{2,3,1,0:T(8,128)} %get-tuple-element.64, f32[2,4,512]{2,1,0:T(4,128)S(1)} %get-tuple-element.63, pred[2,512]{1,0:T(4,128)(4,1)S(1)} %iota_compare_fusion.2), kind=kOutput, calls=%fused_computation.132 | convolution fusion | flops 273154048 | bytes 9454592 | tf_op jit(solution)/shard_map/thqk,tkhe->tqhe/dot_general | solution.py:264
  41.6 2.1 convolution_convert_fusion.p_ref
  43.7 25.9 %shard_map.168 = (bf16[3,2,128,1024]{3,2,1,0:T(8,128)(2,1)}, bf16[2,128,1024]{2,1,0:T(8,128)(2,1)}) custom-call(bf16[2,512,1024]{2,1,0:T(8,128)(2,1)} %convolution_convert_fusion.p_ref), custom_call_target="tpu_custom_call" | custom-call | tf_op jit(solution)/shard_map/pallas_call | solution.py:136
  69.7 2.8 %convert_reduce_fusion.2 = f32[2,128,1024]{2,1,0:T(8,128)} fusion(bf16[3,2,128,1024]{3,2,1,0:T(8,128)(2,1)} %get-tuple-element.34), kind=kLoop, calls=%fused_computation.90 | loop fusion | flops 1310720 | bytes 2621440 | tf_op jit(solution)/shard_map/reduce_sum | solution.py:318
  72.5 1.8 fusion.121
  75.6 21.1 %shard_map.169 = bf16[2,512,1024]{2,1,0:T(8,128)(2,1)} custom-call(bf16[2,128,1024]{2,1,0:T(8,128)(2,1)} %add_convert_fusion.2.x_ref), custom_call_target="tpu_custom_call" | custom-call | tf_op jit(solution)/shard_map/pallas_call | solution.py:74
  96.7 5.2 %fusion.77 = (u8[512,1024]{1,0:T(8,128)(4,1)S(1)}, u8[512,1024]{1,0:T(8,128)(4,1)S(1)}, f32[2,512,1024]{2,1,0:T(8,128)S(1)}) fusion(f32[1024]{0:T(1024)S(1)} %copy-done.10, bf16[2,512,1024]{2,1,0:T(8,128)(2,1)} %shard_map.169, bf16[1024,1024]{1,0:T(8,128)(2,1)S(1)} %copy-done), kind=kOutput, calls=%fused_computation.142 | convolution fusion | flops 2161115136 | bytes 9441280 | tf_op jit(solution)/shard_map/tsd,df->tsf/dot_general | solution.py:324
  101.9 12.6 %fusion.64.p_ref = bf16[2,512,1024]{2,1,0:T(8,128)(2,1)} fusion(bf16[1024,1024]{1,0:T(8,128)(2,1)S(1)} %copy-done.9, f32[2,512,1024]{2,1,0:T(8,128)S(1)} %get-tuple-element.65, f32[1024]{0:T(1024)S(1)} %copy-done.10, u8[512,1024]{1,0:T(8,128)(4,1)S(1)} %get-tuple-element.44, u8[512,1024]{1,0:T(8,128)(4,1)S(1)} %get-tuple-element.43), kind=kOutput, calls=%fused_computation.128 | convolution fusion | flops 2222981120 | bytes 9441280 | tf_op jit(solution)/shard_map/tsf,fd->tsd/dot_general | solution.py:327
  114.6 26.6 %shard_map.170 = (bf16[3,2,128,1024]{3,2,1,0:T(8,128)(2,1)}, bf16[2,128,1024]{2,1,0:T(8,128)(2,1)}) custom-call(bf16[2,512,1024]{2,1,0:T(8,128)(2,1)} %fusion.64.p_ref), custom_call_target="tpu_custom_call" | custom-call | tf_op jit(solution)/shard_map/pallas_call | solution.py:136
  141.2 1.8 convert_reduce_fusion.1
  143.1 1.5 fusion.120
  145.0 1.7 select_reduce_fusion.1
  146.7 5.9 %shard_map.171 = f32[4,2,1024]{2,1,0:T(2,128)} custom-call(f32[2,1024]{1,0:T(2,128)} %get-tuple-element.49.x_ref), custom_call_target="tpu_custom_call" | custom-call | tf_op jit(solution)/shard_map/pallas_call | solution.py:219
  153.6 4.8 %shard_map.172 = s32[4,2,16]{2,1,0:T(2,128)} custom-call(s32[2,16]{1,0:T(2,128)} %x_ref.3), custom_call_target="tpu_custom_call" | custom-call | tf_op jit(solution)/shard_map/pallas_call | solution.py:219
  159.9 15.7 %shard_map.173 = f32[32,2,1088]{2,1,0:T(2,128)} custom-call(f32[2,1088]{1,0:T(2,128)} %pad_maximum_fusion.x_ref), custom_call_target="tpu_custom_call" | custom-call | tf_op jit(solution)/shard_map/pallas_call | solution.py:219
  175.6 1.2 reshape.382
  178.1 42.4 %conditional.1 = (f32[64,64]{1,0:T(8,128)S(1)}) conditional(s32[]{:T(128)} %convert_element_type.118, (s32[64,64]{1,0:T(8,128)S(1)}, bf16[4096,1024]{1,0:T(8,128)(2,1)}, bf16[64,1024]{1,0:T(8,128)(2,1)S(1)}, pred[64,64]{1,0:T(8,128)(4,1)S(1)}) %tuple.14, (pred[64,64]{1,0:T(8,128)(4,1)S(1)}, s32[]{:T(128)}, s32[64,64]{1,0:T(8,128)S(1)}, ...), branch_computations={%region_12.14_spmd, %region_14.22_spmd} | conditional | flops 537702400 | bytes 12955656 | solution.py:383
  178.9 28.8 %scatter_custom_fusion = s32[128]{0:T(128)S(1)} fusion(s32[4096]{0:T(1024)S(1)} %bitcast.61, s32[4096]{0:T(1024)S(1)} %broadcast.464, s32[]{:T(128)} %constant.74.clone), kind=kCustom, calls=%fused_computation.56 | custom fusion | flops 4096 | bytes 516 | tf_op jit(solution)/shard_map/cond/branch_1_fun/scatter-add | solution.py:363
  211.0 5.5 %gather_fusion.1 = bf16[128,1024]{1,0:T(8,128)(2,1)S(1)} fusion(bf16[4096,1024]{1,0:T(8,128)(2,1)} %get-tuple-element.28, s32[1024]{0:T(1024)S(1)} %pad_clamp_fusion.1), kind=kCustom, calls=%fused_computation.2 | custom fusion | bytes 524800 | tf_op jit(solution)/shard_map/cond/branch_1_fun/jit(_take)/gather | solution.py:365
  219.0 1.4 scatter_custom_fusion.1
  220.8 16.9 %all_to_all.5 = f32[128,2,16]{2,1,0:T(2,128)S(1)} all-to-all(f32[128,2,16]{2,1,0:T(2,128)S(1)} %copy.49), channel_id=1, replica_groups=mesh['req'=32,'tp'=4] {'req','tp'}, dimensions={0} | all-to-all | bytes 32768 | tf_op jit(solution)/shard_map/all_to_all | solution.py:389
  (75 shorter events, 15.5 us)
Async XLA Ops:
  0.6 96.1 %copy-start = (bf16[1024,1024]{1,0:T(8,128)(2,1)S(1)}, bf16[1024,1024]{1,0:T(8,128)(2,1)}, u32[]{:S(2)}) copy-start(bf16[1024,1024]{1,0:T(8,128)(2,1)} %param.26) | copy-start | bytes 6291460
  37.3 4.3 %copy-start.1 = (bf16[256,1024]{1,0:T(8,128)(2,1)S(1)}, bf16[256,1024]{1,0:T(8,128)(2,1)}, u32[]{:S(2)}) copy-start(bf16[256,1024]{1,0:T(8,128)(2,1)} %param.22) | copy-start | bytes 1572868
  41.6 30.8 %copy-start.4 = (f32[1024]{0:T(1024)S(1)}, f32[1024]{0:T(1024)}, u32[]{:S(2)}) copy-start(f32[1024]{0:T(1024)} %param.23) | copy-start | bytes 12292
  43.7 30.8 %copy-start.2 = (f32[1024]{0:T(1024)S(1)}, f32[1024]{0:T(1024)}, u32[]{:S(2)}) copy-start(f32[1024]{0:T(1024)} %param.25) | copy-start | bytes 12292
  43.7 30.8 %copy-start.3 = (f32[1024]{0:T(1024)S(1)}, f32[1024]{0:T(1024)}, u32[]{:S(2)}) copy-start(f32[1024]{0:T(1024)} %param.24) | copy-start | bytes 12292
  72.4 24.3 %copy-start.10 = (f32[1024]{0:T(1024)S(1)}, f32[1024]{0:T(1024)}, u32[]{:S(2)}) copy-start(f32[1024]{0:T(1024)} %param.27) | copy-start | bytes 12292
  96.7 5.2 %copy-start.9 = (bf16[1024,1024]{1,0:T(8,128)(2,1)S(1)}, bf16[1024,1024]{1,0:T(8,128)(2,1)}, u32[]{:S(2)}) copy-start(bf16[1024,1024]{1,0:T(8,128)(2,1)} %param.28) | copy-start | bytes 6291460
  114.6 28.5 %copy-start.5 = (f32[1024]{0:T(1024)S(1)}, f32[1024]{0:T(1024)}, u32[]{:S(2)}) copy-start(f32[1024]{0:T(1024)} %param.29) | copy-start | bytes 12292
  141.2 3.7 %copy-start.8 = (s32[2]{0:T(128)S(1)}, s32[2]{0:T(128)}, u32[]{:S(2)}) copy-start(s32[2]{0:T(128)} %param.19) | copy-start | bytes 28
  141.2 3.8 %copy-start.6 = (f32[1024]{0:T(1024)S(1)}, f32[1024]{0:T(1024)}, u32[]{:S(2)}) copy-start(f32[1024]{0:T(1024)} %param.31) | copy-start | bytes 12292
  141.2 3.8 %copy-start.7 = (f32[1024]{0:T(1024)S(1)}, f32[1024]{0:T(1024)}, u32[]{:S(2)}) copy-start(f32[1024]{0:T(1024)} %param.30) | copy-start | bytes 12292

commit v8 on v7

--- a/solution.py
+++ b/solution.py
@@ -360,15 +360,20 @@
 
     def few_owned(_):
         flat_owned = is_owned.reshape(-1)
-        (pair_at,) = jnp.nonzero(flat_owned, size=SPARSE_PAIRS, fill_value=0)
-        valid = jnp.arange(SPARSE_PAIRS) < owned_count
+        owned_int = is_owned.astype(jnp.int32)
+        row_counts = jnp.cumsum(owned_int, axis=1)
+        row_totals = row_counts[:, -1]
+        running = (row_counts + (jnp.cumsum(row_totals) - row_totals)[:, None]).reshape(-1)
+        rank = jnp.arange(SPARSE_PAIRS, dtype=jnp.int32)
+        chosen = flat_owned[None, :] & (running[None, :] == rank[:, None] + 1)
+        pair_index = jnp.arange(flat_owned.shape[0], dtype=jnp.int32)
+        pair_at = jnp.sum(jnp.where(chosen, pair_index[None, :], 0), axis=1)
         rows = jnp.take(index_rows, safe_ids.reshape(-1)[pair_at], axis=0)
         queries = jnp.take(all_queries, pair_at // all_ids.shape[1], axis=0)
         values = jnp.sum(rows.astype(jnp.float32) * queries.astype(jnp.float32), axis=-1)
-        values = jnp.where(valid, values, jnp.float32(0.0))
-        return (
-            jnp.zeros(flat_owned.shape, jnp.float32).at[pair_at].add(values).reshape(all_ids.shape)
-        )
+        return jnp.sum(
+            jnp.where(chosen, values[:, None], jnp.float32(0.0)), axis=0
+        ).reshape(all_ids.shape)
 
     def many_owned(_):
         all_scores = jnp.einsum(

time: 239 us -> 207 us (0.87)
  other arithmetic: 51.2 us -> 19.1 us
    scatter-add x2 -> x0, other arithmetic: 30.2 us -> none  [the longest x1 28.8 us: few_owned(): pair_at, = jnp.nonzero(flat_owned, size=SPARSE_PAIRS, fill_value=0)]
    gather x3 -> x2, local copies, waits for them, and re-layouts: 6.77 us -> 6.65 us  [few_owned(): rows = jnp.take(index_rows, safe_ids.reshape(-1)[pair_at], axis=0)]
where the time goes in v8:
time: 207 us; the launch traced here: 206 us
  Pallas kernels  122 us (59%)
  matrix products  35.8 us (17%)
  other arithmetic  19.1 us (9%)
  blocking collectives  16.9 us (8%)
  local copies, waits for them, and re-layouts  10.6 us (5%)
    pallas_call x2, Pallas kernels, ring_reduce_scatter(): pl.pallas_call(functools.partial(_scatter_kernel, chunks), out_shape=(jax...  52.5 us
    pallas_call x2, Pallas kernels, ring_all_gather(): pl.pallas_call(functools.partial(_gather_kernel, chunks), out_shape=jax.S...  43 us
    pallas_call x3, Pallas kernels, direct_exchange(): pl.pallas_call(functools.partial(_direct_kernel, axes, scatter), out_shap...  26.4 us
    all_to_all x1, blocking collectives, per_device(): lax.all_to_all(owner_terms, ('req', 'tp'), 0, 0, tiled=True)  16.9 us
    dot_general x1, matrix products, per_device(): jnp.einsum('tsf,fd->tsd', up_act, w_down, preferred_element_type=jnp.floa...  12.6 us
    sub x1, matrix products, window_attention(): expo = jnp.exp(logits - top_val)  7.66 us
    gather x2, local copies, waits for them, and re-layouts, few_owned(): rows = jnp.take(index_rows, safe_ids.reshape(-1)[pair_at], axis=0)  6.65 us
    dot_general x1, matrix products, per_device(): jnp.einsum('tsd,df->tsf', normed_full, w_up, preferred_element_type=jnp.f...  5.17 us

profile of v8, /device:TPU:1, one launch (start us, length us, event | category | flops | bytes accessed | tf_op | source)
XLA Modules:
  0.0 206.1 jit_solution(8320349982203635700)
XLA Ops:
  2.3 21.9 %shard_map.167 = bf16[2,512,1024]{2,1,0:T(8,128)(2,1)} custom-call(bf16[2,128,1024]{2,1,0:T(8,128)(2,1)} %x_ref.2), custom_call_target="tpu_custom_call" | custom-call | tf_op jit(solution)/shard_map/pallas_call | solution.py:74
  24.3 3.9 %add_convert_fusion = bf16[2,512,3,256]{1,3,2,0:T(8,128)(2,1)S(1)} fusion(f32[3,256]{1,0:T(4,128)} %param.21, bf16[1024,3,256]{2,0,1:T(8,128)(2,1)} %param.20, bf16[2,512,1024]{2,1,0:T(8,128)(2,1)} %shard_map.167), kind=kOutput, calls=%fused_computation.73 | convolution fusion | flops 1612185600 | bytes 5245952 | tf_op jit(solution)/shard_map/tsd,dce->tsce/dot_general | solution.py:306
  28.2 1.2 fusion.112
  29.7 7.7 %fusion.113 = (f32[2,4,512]{2,1,0:T(4,128)S(1)}, f32[2,4,512,512]{2,3,1,0:T(8,128)}) fusion(pred[2,512,512]{1,2,0:T(8,128)(4,1)S(1)} %broadcast_and_fusion, bf16[2,512,4,64]{1,3,2,0:T(8,128)(2,1)} %bitcast.72, bf16[2,512,4,64]{1,3,2,0:T(8,128)(2,1)} %bitcast.71), kind=kOutput, calls=%fused_computation.186 | convolution fusion | flops 276824576 | bytes 9977856 | tf_op jit(solution)/shard_map/sub | solution.py:262
  37.3 4.3 %fusion.66 = bf16[2,4,64,512]{3,2,1,0:T(8,128)(2,1)S(1)} fusion(bf16[2,512,4,64]{1,3,2,0:T(8,128)(2,1)S(1)} %bitcast.70, f32[2,4,512,512]{2,3,1,0:T(8,128)} %get-tuple-element.64, f32[2,4,512]{2,1,0:T(4,128)S(1)} %get-tuple-element.63, pred[2,512]{1,0:T(4,128)(4,1)S(1)} %iota_compare_fusion.1), kind=kOutput, calls=%fused_computation.114 | convolution fusion | flops 273154048 | bytes 9454592 | tf_op jit(solution)/shard_map/thqk,tkhe->tqhe/dot_general | solution.py:264
  41.6 2.1 %convolution_convert_fusion.p_ref = bf16[2,512,1024]{2,1,0:T(8,128)(2,1)} fusion(bf16[2,512,256]{1,2,0:T(8,128)(2,1)S(1)} %bitcast.73, bf16[256,1024]{1,0:T(8,128)(2,1)S(1)} %copy-done.1), kind=kOutput, calls=%fused_computation.111 | convolution fusion | flops 537919488 | bytes 3145728 | tf_op jit(solution)/shard_map/tsk,kd->tsd/dot_general | solution.py:313
  43.7 25.9 %shard_map.168 = (bf16[3,2,128,1024]{3,2,1,0:T(8,128)(2,1)}, bf16[2,128,1024]{2,1,0:T(8,128)(2,1)}) custom-call(bf16[2,512,1024]{2,1,0:T(8,128)(2,1)} %convolution_convert_fusion.p_ref), custom_call_target="tpu_custom_call" | custom-call | tf_op jit(solution)/shard_map/pallas_call | solution.py:136
  69.7 2.8 %convert_reduce_fusion.1 = f32[2,128,1024]{2,1,0:T(8,128)} fusion(bf16[3,2,128,1024]{3,2,1,0:T(8,128)(2,1)} %get-tuple-element.31), kind=kLoop, calls=%fused_computation.72 | loop fusion | flops 1310720 | bytes 2621440 | tf_op jit(solution)/shard_map/reduce_sum | solution.py:318
  72.5 1.8 fusion.111
  75.6 21.1 %shard_map.169 = bf16[2,512,1024]{2,1,0:T(8,128)(2,1)} custom-call(bf16[2,128,1024]{2,1,0:T(8,128)(2,1)} %add_convert_fusion.2.x_ref), custom_call_target="tpu_custom_call" | custom-call | tf_op jit(solution)/shard_map/pallas_call | solution.py:74
  96.7 5.2 %fusion.68 = (u8[512,1024]{1,0:T(8,128)(4,1)S(1)}, u8[512,1024]{1,0:T(8,128)(4,1)S(1)}, f32[2,512,1024]{2,1,0:T(8,128)S(1)}) fusion(f32[1024]{0:T(1024)S(1)} %copy-done.10, bf16[2,512,1024]{2,1,0:T(8,128)(2,1)} %shard_map.169, bf16[1024,1024]{1,0:T(8,128)(2,1)S(1)} %copy-done), kind=kOutput, calls=%fused_computation.124 | convolution fusion | flops 2161115136 | bytes 9441280 | tf_op jit(solution)/shard_map/tsd,df->tsf/dot_general | solution.py:324
  101.9 12.6 %fusion.55.p_ref = bf16[2,512,1024]{2,1,0:T(8,128)(2,1)} fusion(bf16[1024,1024]{1,0:T(8,128)(2,1)S(1)} %copy-done.9, f32[2,512,1024]{2,1,0:T(8,128)S(1)} %get-tuple-element.65, f32[1024]{0:T(1024)S(1)} %copy-done.10, u8[512,1024]{1,0:T(8,128)(4,1)S(1)} %get-tuple-element.42, u8[512,1024]{1,0:T(8,128)(4,1)S(1)} %get-tuple-element.41), kind=kOutput, calls=%fused_computation.110 | convolution fusion | flops 2222981120 | bytes 9441280 | tf_op jit(solution)/shard_map/tsf,fd->tsd/dot_general | solution.py:327
  114.6 26.6 %shard_map.170 = (bf16[3,2,128,1024]{3,2,1,0:T(8,128)(2,1)}, bf16[2,128,1024]{2,1,0:T(8,128)(2,1)}) custom-call(bf16[2,512,1024]{2,1,0:T(8,128)(2,1)} %fusion.55.p_ref), custom_call_target="tpu_custom_call" | custom-call | tf_op jit(solution)/shard_map/pallas_call | solution.py:136
  141.2 1.8 convert_reduce_fusion
  143.1 1.5 fusion.110
  145.0 1.7 select_reduce_fusion.3
  146.7 5.9 %shard_map.171 = f32[4,2,1024]{2,1,0:T(2,128)} custom-call(f32[2,1024]{1,0:T(2,128)} %get-tuple-element.47.x_ref), custom_call_target="tpu_custom_call" | custom-call | tf_op jit(solution)/shard_map/pallas_call | solution.py:219
  153.6 4.8 %shard_map.172 = s32[4,2,16]{2,1,0:T(2,128)} custom-call(s32[2,16]{1,0:T(2,128)} %x_ref.3), custom_call_target="tpu_custom_call" | custom-call | tf_op jit(solution)/shard_map/pallas_call | solution.py:219
  159.9 15.7 %shard_map.173 = f32[32,2,1088]{2,1,0:T(2,128)} custom-call(f32[2,1088]{1,0:T(2,128)} %pad_maximum_fusion.x_ref), custom_call_target="tpu_custom_call" | custom-call | tf_op jit(solution)/shard_map/pallas_call | solution.py:219
  175.6 1.2 reshape.313
  178.1 10.1 %conditional.1 = (f32[64,64]{1,0:T(8,128)S(1)}) conditional(s32[]{:T(128)} %convert_element_type.109, (s32[64,64]{1,0:T(8,128)S(1)}, bf16[4096,1024]{1,0:T(8,128)(2,1)}, bf16[64,1024]{1,0:T(8,128)(2,1)S(1)}, pred[64,64]{1,0:T(8,128)(4,1)S(1)}) %tuple.14, (pred[64,64]{1,0:T(8,128)(4,1)S(1)}, s32[64,64]{1,0:T(8,128)S(1)}, ...), branch_computations={%region_12.14_spmd, %region_14.0_spmd} | conditional | flops 537702400 | bytes 12955656 | solution.py:388
  179.8 1.1 gather_fusion
  181.0 5.5 %gather_fusion.1 = bf16[128,1024]{1,0:T(8,128)(2,1)S(1)} fusion(bf16[4096,1024]{1,0:T(8,128)(2,1)} %get-tuple-element.25, s32[1024]{0:T(1024)S(1)} %pad_clamp_fusion.1), kind=kCustom, calls=%fused_computation.2 | custom fusion | bytes 524800 | tf_op jit(solution)/shard_map/cond/branch_1_fun/jit(_take)/gather | solution.py:371
  188.5 16.9 %all_to_all.5 = f32[128,2,16]{2,1,0:T(2,128)S(1)} all-to-all(f32[128,2,16]{2,1,0:T(2,128)S(1)} %copy.46), channel_id=1, replica_groups=mesh['req'=32,'tp'=4] {'req','tp'}, dimensions={0} | all-to-all | bytes 32768 | tf_op jit(solution)/shard_map/all_to_all | solution.py:394
  (70 shorter events, 11.1 us)
Async XLA Ops:
  0.6 96.1 %copy-start = (bf16[1024,1024]{1,0:T(8,128)(2,1)S(1)}, bf16[1024,1024]{1,0:T(8,128)(2,1)}, u32[]{:S(2)}) copy-start(bf16[1024,1024]{1,0:T(8,128)(2,1)} %param.26) | copy-start | bytes 6291460
  37.3 4.3 %copy-start.1 = (bf16[256,1024]{1,0:T(8,128)(2,1)S(1)}, bf16[256,1024]{1,0:T(8,128)(2,1)}, u32[]{:S(2)}) copy-start(bf16[256,1024]{1,0:T(8,128)(2,1)} %param.22) | copy-start | bytes 1572868
  41.6 30.8 %copy-start.4 = (f32[1024]{0:T(1024)S(1)}, f32[1024]{0:T(1024)}, u32[]{:S(2)}) copy-start(f32[1024]{0:T(1024)} %param.23) | copy-start | bytes 12292
  43.7 30.8 %copy-start.2 = (f32[1024]{0:T(1024)S(1)}, f32[1024]{0:T(1024)}, u32[]{:S(2)}) copy-start(f32[1024]{0:T(1024)} %param.25) | copy-start | bytes 12292
  43.7 30.8 %copy-start.3 = (f32[1024]{0:T(1024)S(1)}, f32[1024]{0:T(1024)}, u32[]{:S(2)}) copy-start(f32[1024]{0:T(1024)} %param.24) | copy-start | bytes 12292
  72.4 24.3 %copy-start.10 = (f32[1024]{0:T(1024)S(1)}, f32[1024]{0:T(1024)}, u32[]{:S(2)}) copy-start(f32[1024]{0:T(1024)} %param.27) | copy-start | bytes 12292
  96.7 5.2 %copy-start.9 = (bf16[1024,1024]{1,0:T(8,128)(2,1)S(1)}, bf16[1024,1024]{1,0:T(8,128)(2,1)}, u32[]{:S(2)}) copy-start(bf16[1024,1024]{1,0:T(8,128)(2,1)} %param.28) | copy-start | bytes 6291460
  114.6 28.5 %copy-start.5 = (f32[1024]{0:T(1024)S(1)}, f32[1024]{0:T(1024)}, u32[]{:S(2)}) copy-start(f32[1024]{0:T(1024)} %param.29) | copy-start | bytes 12292
  141.2 3.7 %copy-start.8 = (s32[2]{0:T(128)S(1)}, s32[2]{0:T(128)}, u32[]{:S(2)}) copy-start(s32[2]{0:T(128)} %param.19) | copy-start | bytes 28
  141.2 3.8 %copy-start.6 = (f32[1024]{0:T(1024)S(1)}, f32[1024]{0:T(1024)}, u32[]{:S(2)}) copy-start(f32[1024]{0:T(1024)} %param.31) | copy-start | bytes 12292
  141.2 3.8 %copy-start.7 = (f32[1024]{0:T(1024)S(1)}, f32[1024]{0:T(1024)}, u32[]{:S(2)}) copy-start(f32[1024]{0:T(1024)} %param.30) | copy-start | bytes 12292

commit v9 on v8

--- a/solution.py
+++ b/solution.py
@@ -298,7 +298,6 @@
     quarter = cand_ids.shape[1]
     full_states = ring_all_gather(states, 0, RING_CHUNKS)
     device_count = req_count * tp_count
-    text_ids = jnp.swapaxes(direct_exchange(cand_ids, ("tp",), 4), 0, 1)
     seq_len = full_states.shape[1]
     local_width = w_qkv.shape[2]
     heads_here = local_width // HEAD_DIM
@@ -339,14 +338,18 @@
     local_pool = jnp.sum(
         jnp.where(is_valid[:, :, None], hidden_out.astype(jnp.float32), jnp.float32(0.0)), axis=1
     )
-    pooled = jnp.sum(direct_exchange(local_pool, ("tp",), 5), axis=0) / lengths.astype(
+    pool_and_ids = direct_exchange(
+        jnp.concatenate([local_pool, cand_ids.astype(jnp.float32)], axis=1), ("tp",), 5
+    )
+    text_ids = jnp.swapaxes(pool_and_ids[:, :, model_width:], 0, 1)
+    pooled = jnp.sum(pool_and_ids[:, :, :model_width], axis=0) / lengths.astype(
         jnp.float32
     )[:, None]
     query_vec = (
         pooled * lax.rsqrt(jnp.mean(pooled * pooled, axis=-1, keepdims=True) + norm_eps)
     ).astype(jnp.bfloat16)
     bundle = jnp.concatenate(
-        [query_vec.astype(jnp.float32), text_ids.reshape(text_count, -1).astype(jnp.float32)], axis=1
+        [query_vec.astype(jnp.float32), text_ids.reshape(text_count, -1)], axis=1
     )
     bundle = direct_exchange(bundle, ("req",), 6).reshape(req_count * text_count, bundle.shape[1])
     all_queries = bundle[:, :model_width].astype(jnp.bfloat16)

time: 207 us -> 201 us (0.971)
  Pallas kernels: 122 us -> 116 us
    pallas_call x3 -> x2, Pallas kernels: 26.4 us -> 20.8 us  [direct_exchange(): pl.pallas_call(functools.partial(_direct_kernel, axes, scatter), out_shap...]
where the time goes in v9:
time: 201 us
  Pallas kernels  116 us (58%)
  matrix products  35.8 us (18%)
  other arithmetic  18.5 us (9%)
  blocking collectives  16.9 us (8%)
  local copies, waits for them, and re-layouts  11.3 us (6%)
    pallas_call x2, Pallas kernels, ring_reduce_scatter(): pl.pallas_call(functools.partial(_scatter_kernel, chunks), out_shape=(jax...  52.5 us
    pallas_call x2, Pallas kernels, ring_all_gather(): pl.pallas_call(functools.partial(_gather_kernel, chunks), out_shape=jax.S...  43 us
    pallas_call x2, Pallas kernels, direct_exchange(): pl.pallas_call(functools.partial(_direct_kernel, axes, scatter), out_shap...  20.8 us
    all_to_all x1, blocking collectives, per_device(): lax.all_to_all(owner_terms, ('req', 'tp'), 0, 0, tiled=True)  16.9 us
    dot_general x1, matrix products, per_device(): jnp.einsum('tsf,fd->tsd', up_act, w_down, preferred_element_type=jnp.floa...  12.6 us
    sub x1, matrix products, window_attention(): expo = jnp.exp(logits - top_val)  7.66 us
    gather x2, local copies, waits for them, and re-layouts, few_owned(): rows = jnp.take(index_rows, safe_ids.reshape(-1)[pair_at], axis=0)  6.65 us
    dot_general x1, matrix products, per_device(): jnp.einsum('tsd,df->tsf', normed_full, w_up, preferred_element_type=jnp.f...  5.17 us

profile of v9, /device:TPU:1, one launch (start us, length us, event | category | flops | bytes accessed | tf_op | source)
XLA Modules:
  0.0 200.5 jit_solution(5088068792438321578)
XLA Ops:
  2.3 21.9 %shard_map.167 = bf16[2,512,1024]{2,1,0:T(8,128)(2,1)} custom-call(bf16[2,128,1024]{2,1,0:T(8,128)(2,1)} %x_ref.1), custom_call_target="tpu_custom_call" | custom-call | tf_op jit(solution)/shard_map/pallas_call | solution.py:74
  24.3 3.9 %add_convert_fusion = bf16[2,512,3,256]{1,3,2,0:T(8,128)(2,1)S(1)} fusion(f32[3,256]{1,0:T(4,128)} %param.21, bf16[1024,3,256]{2,0,1:T(8,128)(2,1)} %param.20, bf16[2,512,1024]{2,1,0:T(8,128)(2,1)} %shard_map.167), kind=kOutput, calls=%fused_computation.73 | convolution fusion | flops 1612185600 | bytes 5245952 | tf_op jit(solution)/shard_map/tsd,dce->tsce/dot_general | solution.py:305
  28.2 1.2 fusion.112
  29.7 7.7 %fusion.113 = (f32[2,4,512]{2,1,0:T(4,128)S(1)}, f32[2,4,512,512]{2,3,1,0:T(8,128)}) fusion(pred[2,512,512]{1,2,0:T(8,128)(4,1)S(1)} %broadcast_and_fusion, bf16[2,512,4,64]{1,3,2,0:T(8,128)(2,1)} %bitcast.72, bf16[2,512,4,64]{1,3,2,0:T(8,128)(2,1)} %bitcast.71), kind=kOutput, calls=%fused_computation.188 | convolution fusion | flops 276824576 | bytes 9977856 | tf_op jit(solution)/shard_map/sub | solution.py:262
  37.3 4.3 %fusion.66 = bf16[2,4,64,512]{3,2,1,0:T(8,128)(2,1)S(1)} fusion(bf16[2,512,4,64]{1,3,2,0:T(8,128)(2,1)S(1)} %bitcast.70, f32[2,4,512,512]{2,3,1,0:T(8,128)} %get-tuple-element.64, f32[2,4,512]{2,1,0:T(4,128)S(1)} %get-tuple-element.63, pred[2,512]{1,0:T(4,128)(4,1)S(1)} %iota_compare_fusion.1), kind=kOutput, calls=%fused_computation.114 | convolution fusion | flops 273154048 | bytes 9454592 | tf_op jit(solution)/shard_map/thqk,tkhe->tqhe/dot_general | solution.py:264
  41.6 2.1 %convolution_convert_fusion.p_ref = bf16[2,512,1024]{2,1,0:T(8,128)(2,1)} fusion(bf16[2,512,256]{1,2,0:T(8,128)(2,1)S(1)} %bitcast.73, bf16[256,1024]{1,0:T(8,128)(2,1)S(1)} %copy-done.1), kind=kOutput, calls=%fused_computation.111 | convolution fusion | flops 537919488 | bytes 3145728 | tf_op jit(solution)/shard_map/tsk,kd->tsd/dot_general | solution.py:312
  43.7 25.9 %shard_map.168 = (bf16[3,2,128,1024]{3,2,1,0:T(8,128)(2,1)}, bf16[2,128,1024]{2,1,0:T(8,128)(2,1)}) custom-call(bf16[2,512,1024]{2,1,0:T(8,128)(2,1)} %convolution_convert_fusion.p_ref), custom_call_target="tpu_custom_call" | custom-call | tf_op jit(solution)/shard_map/pallas_call | solution.py:136
  69.7 2.8 %convert_reduce_fusion.1 = f32[2,128,1024]{2,1,0:T(8,128)} fusion(bf16[3,2,128,1024]{3,2,1,0:T(8,128)(2,1)} %get-tuple-element.31), kind=kLoop, calls=%fused_computation.72 | loop fusion | flops 1310720 | bytes 2621440 | tf_op jit(solution)/shard_map/reduce_sum | solution.py:317
  72.5 1.8 fusion.111
  74.6 1.0 add_convert_fusion.2.x_ref
  75.6 21.1 %shard_map.169 = bf16[2,512,1024]{2,1,0:T(8,128)(2,1)} custom-call(bf16[2,128,1024]{2,1,0:T(8,128)(2,1)} %add_convert_fusion.2.x_ref), custom_call_target="tpu_custom_call" | custom-call | tf_op jit(solution)/shard_map/pallas_call | solution.py:74
  96.7 5.2 %fusion.68 = (u8[512,1024]{1,0:T(8,128)(4,1)S(1)}, u8[512,1024]{1,0:T(8,128)(4,1)S(1)}, f32[2,512,1024]{2,1,0:T(8,128)S(1)}) fusion(f32[1024]{0:T(1024)S(1)} %copy-done.11, bf16[2,512,1024]{2,1,0:T(8,128)(2,1)} %shard_map.169, bf16[1024,1024]{1,0:T(8,128)(2,1)S(1)} %copy-done), kind=kOutput, calls=%fused_computation.124 | convolution fusion | flops 2161115136 | bytes 9441280 | tf_op jit(solution)/shard_map/tsd,df->tsf/dot_general | solution.py:323
  101.9 12.6 %fusion.55.p_ref = bf16[2,512,1024]{2,1,0:T(8,128)(2,1)} fusion(bf16[1024,1024]{1,0:T(8,128)(2,1)S(1)} %copy-done.10, f32[2,512,1024]{2,1,0:T(8,128)S(1)} %get-tuple-element.65, f32[1024]{0:T(1024)S(1)} %copy-done.11, u8[512,1024]{1,0:T(8,128)(4,1)S(1)} %get-tuple-element.42, u8[512,1024]{1,0:T(8,128)(4,1)S(1)} %get-tuple-element.41), kind=kOutput, calls=%fused_computation.110 | convolution fusion | flops 2222981120 | bytes 9441280 | tf_op jit(solution)/shard_map/tsf,fd->tsd/dot_general | solution.py:326
  114.6 26.6 %shard_map.170 = (bf16[3,2,128,1024]{3,2,1,0:T(8,128)(2,1)}, bf16[2,128,1024]{2,1,0:T(8,128)(2,1)}) custom-call(bf16[2,512,1024]{2,1,0:T(8,128)(2,1)} %fusion.55.p_ref), custom_call_target="tpu_custom_call" | custom-call | tf_op jit(solution)/shard_map/pallas_call | solution.py:136
  141.2 1.8 convert_reduce_fusion
  143.1 1.5 fusion.110
  145.0 1.2 select_reduce_fusion.3
  146.8 5.9 %shard_map.171 = f32[4,2,1040]{2,1,0:T(2,128)} custom-call(f32[2,1040]{1,0:T(2,128)} %pad_maximum_fusion.x_ref), custom_call_target="tpu_custom_call" | custom-call | tf_op jit(solution)/shard_map/pallas_call | solution.py:219
  155.1 14.9 %shard_map.172 = f32[32,2,1088]{2,1,0:T(2,128)} custom-call(f32[2,1088]{1,0:T(2,128)} %pad_maximum_fusion.1.x_ref), custom_call_target="tpu_custom_call" | custom-call | tf_op jit(solution)/shard_map/pallas_call | solution.py:219
  170.0 1.2 reshape.315
  172.5 10.1 %conditional.1 = (f32[64,64]{1,0:T(8,128)S(1)}) conditional(s32[]{:T(128)} %convert_element_type.101, (s32[64,64]{1,0:T(8,128)S(1)}, bf16[4096,1024]{1,0:T(8,128)(2,1)}, bf16[64,1024]{1,0:T(8,128)(2,1)S(1)}, pred[64,64]{1,0:T(8,128)(4,1)S(1)}) %tuple.14, (pred[64,64]{1,0:T(8,128)(4,1)S(1)}, s32[64,64]{1,0:T(8,128)S(1)}, ...), branch_computations={%region_12.14_spmd, %region_14.0_spmd} | conditional | flops 537702400 | bytes 12955656 | solution.py:391
  174.2 1.1 gather_fusion
  175.4 5.5 %gather_fusion.1 = bf16[128,1024]{1,0:T(8,128)(2,1)S(1)} fusion(bf16[4096,1024]{1,0:T(8,128)(2,1)} %get-tuple-element.25, s32[1024]{0:T(1024)S(1)} %pad_clamp_fusion.1), kind=kCustom, calls=%fused_computation.2 | custom fusion | bytes 524800 | tf_op jit(solution)/shard_map/cond/branch_1_fun/jit(_take)/gather | solution.py:374
  182.9 16.9 %all_to_all.5 = f32[128,2,16]{2,1,0:T(2,128)S(1)} all-to-all(f32[128,2,16]{2,1,0:T(2,128)S(1)} %copy.46), channel_id=1, replica_groups=mesh['req'=32,'tp'=4] {'req','tp'}, dimensions={0} | all-to-all | bytes 32768 | tf_op jit(solution)/shard_map/all_to_all | solution.py:397
  (73 shorter events, 10.6 us)
Async XLA Ops:
  0.6 96.1 %copy-start = (bf16[1024,1024]{1,0:T(8,128)(2,1)S(1)}, bf16[1024,1024]{1,0:T(8,128)(2,1)}, u32[]{:S(2)}) copy-start(bf16[1024,1024]{1,0:T(8,128)(2,1)} %param.26) | copy-start | bytes 6291460
  37.3 4.3 %copy-start.1 = (bf16[256,1024]{1,0:T(8,128)(2,1)S(1)}, bf16[256,1024]{1,0:T(8,128)(2,1)}, u32[]{:S(2)}) copy-start(bf16[256,1024]{1,0:T(8,128)(2,1)} %param.22) | copy-start | bytes 1572868
  41.6 30.8 %copy-start.4 = (f32[1024]{0:T(1024)S(1)}, f32[1024]{0:T(1024)}, u32[]{:S(2)}) copy-start(f32[1024]{0:T(1024)} %param.23) | copy-start | bytes 12292
  43.7 30.8 %copy-start.2 = (f32[1024]{0:T(1024)S(1)}, f32[1024]{0:T(1024)}, u32[]{:S(2)}) copy-start(f32[1024]{0:T(1024)} %param.25) | copy-start | bytes 12292
  43.7 30.8 %copy-start.3 = (f32[1024]{0:T(1024)S(1)}, f32[1024]{0:T(1024)}, u32[]{:S(2)}) copy-start(f32[1024]{0:T(1024)} %param.24) | copy-start | bytes 12292
  72.4 24.3 %copy-start.11 = (f32[1024]{0:T(1024)S(1)}, f32[1024]{0:T(1024)}, u32[]{:S(2)}) copy-start(f32[1024]{0:T(1024)} %param.27) | copy-start | bytes 12292
  96.7 5.2 %copy-start.10 = (bf16[1024,1024]{1,0:T(8,128)(2,1)S(1)}, bf16[1024,1024]{1,0:T(8,128)(2,1)}, u32[]{:S(2)}) copy-start(bf16[1024,1024]{1,0:T(8,128)(2,1)} %param.28) | copy-start | bytes 6291460
  114.6 28.5 %copy-start.5 = (f32[1024]{0:T(1024)S(1)}, f32[1024]{0:T(1024)}, u32[]{:S(2)}) copy-start(f32[1024]{0:T(1024)} %param.29) | copy-start | bytes 12292
  141.2 3.7 %copy-start.9 = (s32[2]{0:T(128)S(1)}, s32[2]{0:T(128)}, u32[]{:S(2)}) copy-start(s32[2]{0:T(128)} %param.19) | copy-start | bytes 28
  141.2 3.8 %copy-start.8 = (s32[2,16]{1,0:T(2,128)S(1)}, s32[2,16]{1,0:T(2,128)}, u32[]{:S(2)}) copy-start(s32[2,16]{1,0:T(2,128)} %param.33) | copy-start | bytes 388
  141.2 3.8 %copy-start.6 = (f32[1024]{0:T(1024)S(1)}, f32[1024]{0:T(1024)}, u32[]{:S(2)}) copy-start(f32[1024]{0:T(1024)} %param.31) | copy-start | bytes 12292
  141.2 3.8 %copy-start.7 = (f32[1024]{0:T(1024)S(1)}, f32[1024]{0:T(1024)}, u32[]{:S(2)}) copy-start(f32[1024]{0:T(1024)} %param.30) | copy-start | bytes 12292

commit v10 on v9

--- a/solution.py
+++ b/solution.py
@@ -85,7 +85,8 @@
     )(x)
 
 
-def _scatter_kernel(chunks, p_ref, recv_ref, relay_ref, send_sem, recv_sem, relay_sem):
+def _scatter_add_kernel(chunks, p_ref, recv_ref, send_sem, recv_sem, relay_sem, local_sem,
+                        own_buf, relay_buf, sum_buf):
     me, rq, core, right, left, opp, relay_to, relay_from = _ring_peers()
     rows = recv_ref.shape[2]
     step = rows // chunks
@@ -102,53 +103,57 @@
         )
 
     sends = []
-    relays = []
-    for k in range(chunks):
-        to_relay = copy(block(opp, k), part(relay_ref, k), send_sem.at[2, k], relay_sem.at[k], relay_to)
-        to_right = copy(block(right, k), part(recv_ref.at[0], k), send_sem.at[0, k], recv_sem.at[0, k], right)
-        to_left = copy(block(left, k), part(recv_ref.at[1], k), send_sem.at[1, k], recv_sem.at[1, k], left)
+    loads = []
+    for k in range(chunks):
+        to_relay = copy(block(opp, k), relay_buf.at[k], send_sem.at[0, k], relay_sem.at[k], relay_to)
+        to_other = copy(
+            block(relay_from, k), part(recv_ref.at[1], k), send_sem.at[1, k], recv_sem.at[1, k], relay_from
+        )
         to_relay.start()
-        to_right.start()
-        to_left.start()
-        sends += [to_relay, to_right, to_left]
-        relays.append(to_relay)
+        to_other.start()
+        load = pltpu.make_async_copy(block(relay_to, k), own_buf.at[k], local_sem.at[k])
+        load.start()
+        sends += [to_relay, to_other]
+        loads.append(load)
     forwards = []
     for k in range(chunks):
-        relays[k].wait_recv()
-        forward = copy(
-            part(relay_ref, k), part(recv_ref.at[2], k), send_sem.at[3, k], recv_sem.at[2, k], relay_to
-        )
+        sends[2 * k].wait_recv()
+        loads[k].wait()
+        sum_buf[k] = (
+            own_buf[k].astype(jnp.float32) + relay_buf[k].astype(jnp.float32)
+        ).astype(sum_buf.dtype)
+        forward = copy(sum_buf.at[k], part(recv_ref.at[0], k), send_sem.at[2, k], recv_sem.at[0, k], relay_to)
         forward.start()
-        sends.append(forward)
         forwards.append(forward)
     for k in range(chunks):
-        sends[3 * k + 1].wait_recv()
-        sends[3 * k + 2].wait_recv()
+        sends[2 * k + 1].wait_recv()
         forwards[k].wait_recv()
-    for c in sends:
+    for c in sends + forwards:
         c.wait_send()
 
 
-def ring_reduce_scatter(p, collective_id, chunks=1):
+def ring_reduce_scatter_add(p, collective_id, chunks=1):
     texts, all_rows, width = p.shape
     n = lax.axis_size("tp")
     rows = all_rows // n
-    recv, _ = pl.pallas_call(
-        functools.partial(_scatter_kernel, chunks),
-        out_shape=(
-            jax.ShapeDtypeStruct((n - 1, texts, rows, width), p.dtype),
-            jax.ShapeDtypeStruct((texts, rows, width), p.dtype),
-        ),
+    step = rows // chunks
+    buf = pltpu.VMEM((chunks, texts, step, width), p.dtype)
+    return pl.pallas_call(
+        functools.partial(_scatter_add_kernel, chunks),
+        out_shape=jax.ShapeDtypeStruct((2, texts, rows, width), p.dtype),
         in_specs=[pl.BlockSpec(memory_space=pl.ANY)],
-        out_specs=(pl.BlockSpec(memory_space=pl.ANY), pl.BlockSpec(memory_space=pl.ANY)),
+        out_specs=pl.BlockSpec(memory_space=pl.ANY),
         scratch_shapes=[
-            pltpu.SemaphoreType.DMA((4, chunks)),
             pltpu.SemaphoreType.DMA((3, chunks)),
+            pltpu.SemaphoreType.DMA((2, chunks)),
             pltpu.SemaphoreType.DMA((chunks,)),
+            pltpu.SemaphoreType.DMA((chunks,)),
+            buf,
+            buf,
+            buf,
         ],
         compiler_params=pltpu.CompilerParams(collective_id=collective_id, has_side_effects=True),
     )(p)
-    return recv
 
 
 def _peer_id(axes, peer):
@@ -311,7 +316,7 @@
     context = window_attention(queries_h, keys_h, values_h, lengths)
     partial_value = jnp.einsum("tsk,kd->tsd", context, w_out, preferred_element_type=jnp.float32)
     partial_value = partial_value.astype(jnp.bfloat16)
-    attn_recv = ring_reduce_scatter(partial_value, 1, RING_CHUNKS)
+    attn_recv = ring_reduce_scatter_add(partial_value, 1, RING_CHUNKS)
     attn_sum = lax.dynamic_slice_in_dim(partial_value, tp_rank * row_share, row_share, 1).astype(
         jnp.float32
     ) + jnp.sum(attn_recv.astype(jnp.float32), axis=0)
@@ -326,7 +331,7 @@
     down_part = jnp.einsum(
         "tsf,fd->tsd", up_act, w_down, preferred_element_type=jnp.float32
     ).astype(jnp.bfloat16)
-    down_recv = ring_reduce_scatter(down_part, 3, RING_CHUNKS)
+    down_recv = ring_reduce_scatter_add(down_part, 3, RING_CHUNKS)
     down_sum = lax.dynamic_slice_in_dim(down_part, tp_rank * row_share, row_share, 1).astype(
         jnp.float32
     ) + jnp.sum(down_recv.astype(jnp.float32), axis=0)

time: 201 us -> 189 us (0.940)
  Pallas kernels: 116 us -> 105 us
    pallas_call x2, Pallas kernels: 52.5 us -> 41 us  [ring_reduce_scatter_add(): pl.pallas_call(functools.partial(_scatter_add_kernel, chunks), out_shape=...]
where the time goes in v10:
time: 189 us
  Pallas kernels  105 us (56%)
  matrix products  35.8 us (19%)
  other arithmetic  17.9 us (9%)
  blocking collectives  16.9 us (9%)
  local copies, waits for them, and re-layouts  11.3 us (6%)
    pallas_call x2, Pallas kernels, ring_all_gather(): pl.pallas_call(functools.partial(_gather_kernel, chunks), out_shape=jax.S...  43.1 us
    pallas_call x2, Pallas kernels, ring_reduce_scatter_add(): pl.pallas_call(functools.partial(_scatter_add_kernel, chunks), out_shape=...  41 us
    pallas_call x2, Pallas kernels, direct_exchange(): pl.pallas_call(functools.partial(_direct_kernel, axes, scatter), out_shap...  20.9 us
    all_to_all x1, blocking collectives, per_device(): lax.all_to_all(owner_terms, ('req', 'tp'), 0, 0, tiled=True)  16.9 us
    dot_general x1, matrix products, per_device(): jnp.einsum('tsf,fd->tsd', up_act, w_down, preferred_element_type=jnp.floa...  12.6 us
    sub x1, matrix products, window_attention(): expo = jnp.exp(logits - top_val)  7.66 us
    gather x2, local copies, waits for them, and re-layouts, few_owned(): rows = jnp.take(index_rows, safe_ids.reshape(-1)[pair_at], axis=0)  6.65 us
    dot_general x1, matrix products, per_device(): jnp.einsum('tsd,df->tsf', normed_full, w_up, preferred_element_type=jnp.f...  5.17 us

profile of v10, /device:TPU:1, one launch (start us, length us, event | category | flops | bytes accessed | tf_op | source)
XLA Modules:
  0.0 188.7 jit_solution(13932850852377282289)
XLA Ops:
  2.3 21.9 %shard_map.167 = bf16[2,512,1024]{2,1,0:T(8,128)(2,1)} custom-call(bf16[2,128,1024]{2,1,0:T(8,128)(2,1)} %x_ref.1), custom_call_target="tpu_custom_call" | custom-call | tf_op jit(solution)/shard_map/pallas_call | solution.py:74
  24.3 3.9 %add_convert_fusion = bf16[2,512,3,256]{1,3,2,0:T(8,128)(2,1)S(1)} fusion(f32[3,256]{1,0:T(4,128)} %param.21, bf16[1024,3,256]{2,0,1:T(8,128)(2,1)} %param.20, bf16[2,512,1024]{2,1,0:T(8,128)(2,1)} %shard_map.167), kind=kOutput, calls=%fused_computation.71 | convolution fusion | flops 1612185600 | bytes 5245952 | tf_op jit(solution)/shard_map/tsd,dce->tsce/dot_general | solution.py:310
  28.2 1.2 fusion.112
  29.7 7.7 %fusion.113 = (f32[2,4,512]{2,1,0:T(4,128)S(1)}, f32[2,4,512,512]{2,3,1,0:T(8,128)}) fusion(pred[2,512,512]{1,2,0:T(8,128)(4,1)S(1)} %broadcast_and_fusion, bf16[2,512,4,64]{1,3,2,0:T(8,128)(2,1)} %bitcast.72, bf16[2,512,4,64]{1,3,2,0:T(8,128)(2,1)} %bitcast.71), kind=kOutput, calls=%fused_computation.188 | convolution fusion | flops 276824576 | bytes 9977856 | tf_op jit(solution)/shard_map/sub | solution.py:267
  37.3 4.3 %fusion.66 = bf16[2,4,64,512]{3,2,1,0:T(8,128)(2,1)S(1)} fusion(bf16[2,512,4,64]{1,3,2,0:T(8,128)(2,1)S(1)} %bitcast.70, f32[2,4,512,512]{2,3,1,0:T(8,128)} %get-tuple-element.60, f32[2,4,512]{2,1,0:T(4,128)S(1)} %get-tuple-element.59, pred[2,512]{1,0:T(4,128)(4,1)S(1)} %iota_compare_fusion.1), kind=kOutput, calls=%fused_computation.114 | convolution fusion | flops 273154048 | bytes 9454592 | tf_op jit(solution)/shard_map/thqk,tkhe->tqhe/dot_general | solution.py:269
  41.6 2.1 %convolution_convert_fusion.p_ref = bf16[2,512,1024]{2,1,0:T(8,128)(2,1)} fusion(bf16[2,512,256]{1,2,0:T(8,128)(2,1)S(1)} %bitcast.73, bf16[256,1024]{1,0:T(8,128)(2,1)S(1)} %copy-done.1), kind=kOutput, calls=%fused_computation.111 | convolution fusion | flops 537919488 | bytes 3145728 | tf_op jit(solution)/shard_map/tsk,kd->tsd/dot_general | solution.py:317
  43.7 20.2 %shard_map.168 = bf16[2,2,128,1024]{3,2,1,0:T(8,128)(2,1)} custom-call(bf16[2,512,1024]{2,1,0:T(8,128)(2,1)} %convolution_convert_fusion.p_ref), custom_call_target="tpu_custom_call" | custom-call | tf_op jit(solution)/shard_map/pallas_call | solution.py:141
  63.9 2.5 %convert_reduce_fusion.1 = f32[2,128,1024]{2,1,0:T(8,128)} fusion(bf16[2,2,128,1024]{3,2,1,0:T(8,128)(2,1)} %shard_map.168), kind=kLoop, calls=%fused_computation.109 | loop fusion | flops 786432 | bytes 2097152 | tf_op jit(solution)/shard_map/reduce_sum | solution.py:322
  66.4 1.8 fusion.111
  68.5 1.0 add_convert_fusion.2.x_ref
  69.6 21.2 %shard_map.169 = bf16[2,512,1024]{2,1,0:T(8,128)(2,1)} custom-call(bf16[2,128,1024]{2,1,0:T(8,128)(2,1)} %add_convert_fusion.2.x_ref), custom_call_target="tpu_custom_call" | custom-call | tf_op jit(solution)/shard_map/pallas_call | solution.py:74
  90.8 5.2 %fusion.68 = (u8[512,1024]{1,0:T(8,128)(4,1)S(1)}, u8[512,1024]{1,0:T(8,128)(4,1)S(1)}, f32[2,512,1024]{2,1,0:T(8,128)S(1)}) fusion(f32[1024]{0:T(1024)S(1)} %copy-done.11, bf16[2,512,1024]{2,1,0:T(8,128)(2,1)} %shard_map.169, bf16[1024,1024]{1,0:T(8,128)(2,1)S(1)} %copy-done), kind=kOutput, calls=%fused_computation.124 | convolution fusion | flops 2161115136 | bytes 9441280 | tf_op jit(solution)/shard_map/tsd,df->tsf/dot_general | solution.py:328
  96.0 12.6 %fusion.55.p_ref = bf16[2,512,1024]{2,1,0:T(8,128)(2,1)} fusion(bf16[1024,1024]{1,0:T(8,128)(2,1)S(1)} %copy-done.10, f32[2,512,1024]{2,1,0:T(8,128)S(1)} %get-tuple-element.61, f32[1024]{0:T(1024)S(1)} %copy-done.11, u8[512,1024]{1,0:T(8,128)(4,1)S(1)} %get-tuple-element.38, u8[512,1024]{1,0:T(8,128)(4,1)S(1)} %get-tuple-element.37), kind=kOutput, calls=%fused_computation.110 | convolution fusion | flops 2222981120 | bytes 9441280 | tf_op jit(solution)/shard_map/tsf,fd->tsd/dot_general | solution.py:331
  108.6 20.9 %shard_map.170 = bf16[2,2,128,1024]{3,2,1,0:T(8,128)(2,1)} custom-call(bf16[2,512,1024]{2,1,0:T(8,128)(2,1)} %fusion.55.p_ref), custom_call_target="tpu_custom_call" | custom-call | tf_op jit(solution)/shard_map/pallas_call | solution.py:141
  129.5 1.6 convert_reduce_fusion
  131.1 1.5 fusion.110
  133.1 1.2 select_reduce_fusion.3
  134.8 6.0 %shard_map.171 = f32[4,2,1040]{2,1,0:T(2,128)} custom-call(f32[2,1040]{1,0:T(2,128)} %pad_maximum_fusion.x_ref), custom_call_target="tpu_custom_call" | custom-call | tf_op jit(solution)/shard_map/pallas_call | solution.py:224
  143.3 14.9 %shard_map.172 = f32[32,2,1088]{2,1,0:T(2,128)} custom-call(f32[2,1088]{1,0:T(2,128)} %pad_maximum_fusion.1.x_ref), custom_call_target="tpu_custom_call" | custom-call | tf_op jit(solution)/shard_map/pallas_call | solution.py:224
  158.2 1.2 reshape.315
  160.7 10.1 %conditional.1 = (f32[64,64]{1,0:T(8,128)S(1)}) conditional(s32[]{:T(128)} %convert_element_type.101, (s32[64,64]{1,0:T(8,128)S(1)}, bf16[4096,1024]{1,0:T(8,128)(2,1)}, bf16[64,1024]{1,0:T(8,128)(2,1)S(1)}, pred[64,64]{1,0:T(8,128)(4,1)S(1)}) %tuple.14, (pred[64,64]{1,0:T(8,128)(4,1)S(1)}, s32[64,64]{1,0:T(8,128)S(1)}, ...), branch_computations={%region_12.14_spmd, %region_14.0_spmd} | conditional | flops 537702400 | bytes 12955656 | solution.py:396
  162.3 1.1 gather_fusion
  163.5 5.5 %gather_fusion.1 = bf16[128,1024]{1,0:T(8,128)(2,1)S(1)} fusion(bf16[4096,1024]{1,0:T(8,128)(2,1)} %get-tuple-element.25, s32[1024]{0:T(1024)S(1)} %pad_clamp_fusion.1), kind=kCustom, calls=%fused_computation.2 | custom fusion | bytes 524800 | tf_op jit(solution)/shard_map/cond/branch_1_fun/jit(_take)/gather | solution.py:379
  171.0 16.9 %all_to_all.5 = f32[128,2,16]{2,1,0:T(2,128)S(1)} all-to-all(f32[128,2,16]{2,1,0:T(2,128)S(1)} %copy.46), channel_id=1, replica_groups=mesh['req'=32,'tp'=4] {'req','tp'}, dimensions={0} | all-to-all | bytes 32768 | tf_op jit(solution)/shard_map/all_to_all | solution.py:402
  (73 shorter events, 10.6 us)
Async XLA Ops:
  0.6 90.1 %copy-start = (bf16[1024,1024]{1,0:T(8,128)(2,1)S(1)}, bf16[1024,1024]{1,0:T(8,128)(2,1)}, u32[]{:S(2)}) copy-start(bf16[1024,1024]{1,0:T(8,128)(2,1)} %param.26) | copy-start | bytes 6291460
  37.3 4.3 %copy-start.1 = (bf16[256,1024]{1,0:T(8,128)(2,1)S(1)}, bf16[256,1024]{1,0:T(8,128)(2,1)}, u32[]{:S(2)}) copy-start(bf16[256,1024]{1,0:T(8,128)(2,1)} %param.22) | copy-start | bytes 1572868
  41.6 24.8 %copy-start.4 = (f32[1024]{0:T(1024)S(1)}, f32[1024]{0:T(1024)}, u32[]{:S(2)}) copy-start(f32[1024]{0:T(1024)} %param.23) | copy-start | bytes 12292
  43.7 24.8 %copy-start.2 = (f32[1024]{0:T(1024)S(1)}, f32[1024]{0:T(1024)}, u32[]{:S(2)}) copy-start(f32[1024]{0:T(1024)} %param.25) | copy-start | bytes 12292
  43.7 24.8 %copy-start.3 = (f32[1024]{0:T(1024)S(1)}, f32[1024]{0:T(1024)}, u32[]{:S(2)}) copy-start(f32[1024]{0:T(1024)} %param.24) | copy-start | bytes 12292
  66.4 24.4 %copy-start.11 = (f32[1024]{0:T(1024)S(1)}, f32[1024]{0:T(1024)}, u32[]{:S(2)}) copy-start(f32[1024]{0:T(1024)} %param.27) | copy-start | bytes 12292
  90.8 5.2 %copy-start.10 = (bf16[1024,1024]{1,0:T(8,128)(2,1)S(1)}, bf16[1024,1024]{1,0:T(8,128)(2,1)}, u32[]{:S(2)}) copy-start(bf16[1024,1024]{1,0:T(8,128)(2,1)} %param.28) | copy-start | bytes 6291460
  108.6 22.5 %copy-start.5 = (f32[1024]{0:T(1024)S(1)}, f32[1024]{0:T(1024)}, u32[]{:S(2)}) copy-start(f32[1024]{0:T(1024)} %param.29) | copy-start | bytes 12292
  129.5 3.5 %copy-start.9 = (s32[2]{0:T(128)S(1)}, s32[2]{0:T(128)}, u32[]{:S(2)}) copy-start(s32[2]{0:T(128)} %param.19) | copy-start | bytes 28
  129.5 3.5 %copy-start.8 = (s32[2,16]{1,0:T(2,128)S(1)}, s32[2,16]{1,0:T(2,128)}, u32[]{:S(2)}) copy-start(s32[2,16]{1,0:T(2,128)} %param.33) | copy-start | bytes 388
  129.5 3.5 %copy-start.6 = (f32[1024]{0:T(1024)S(1)}, f32[1024]{0:T(1024)}, u32[]{:S(2)}) copy-start(f32[1024]{0:T(1024)} %param.31) | copy-start | bytes 12292
  129.5 3.5 %copy-start.7 = (f32[1024]{0:T(1024)S(1)}, f32[1024]{0:T(1024)}, u32[]{:S(2)}) copy-start(f32[1024]{0:T(1024)} %param.30) | copy-start | bytes 12292

commit v11 on v10

--- a/solution.py
+++ b/solution.py
@@ -328,6 +328,7 @@
         jnp.einsum("tsd,df->tsf", normed_full, w_up, preferred_element_type=jnp.float32) + b_up,
         approximate=False,
     ).astype(jnp.bfloat16)
+    up_act = lax.optimization_barrier(up_act)
     down_part = jnp.einsum(
         "tsf,fd->tsd", up_act, w_down, preferred_element_type=jnp.float32
     ).astype(jnp.bfloat16)

time: 189 us -> 188 us (level)
    dot_general x1, matrix products: 12.6 us -> 3.7 us  [per_device(): jnp.einsum('tsf,fd->tsd', up_act, w_down, preferred_element_type=jnp.floa...]
    dot_general x1, matrix products: 5.17 us -> 12.7 us  [per_device(): jnp.einsum('tsd,df->tsf', normed_full, w_up, preferred_element_type=jnp.f...]
where the time goes in v11:
time: 188 us; the launch traced here: 187 us
  Pallas kernels  105 us (56%)
  matrix products  34.4 us (18%)
  other arithmetic  17.9 us (10%)
  blocking collectives  16.9 us (9%)
  local copies, waits for them, and re-layouts  11.3 us (6%)
    pallas_call x2, Pallas kernels, ring_all_gather(): pl.pallas_call(functools.partial(_gather_kernel, chunks), out_shape=jax.S...  43.1 us
    pallas_call x2, Pallas kernels, ring_reduce_scatter_add(): pl.pallas_call(functools.partial(_scatter_add_kernel, chunks), out_shape=...  41 us
    pallas_call x2, Pallas kernels, direct_exchange(): pl.pallas_call(functools.partial(_direct_kernel, axes, scatter), out_shap...  20.9 us
    all_to_all x1, blocking collectives, per_device(): lax.all_to_all(owner_terms, ('req', 'tp'), 0, 0, tiled=True)  16.9 us
    dot_general x1, matrix products, per_device(): jnp.einsum('tsd,df->tsf', normed_full, w_up, preferred_element_type=jnp.f...  12.7 us
    sub x1, matrix products, window_attention(): expo = jnp.exp(logits - top_val)  7.66 us
    gather x2, local copies, waits for them, and re-layouts, few_owned(): rows = jnp.take(index_rows, safe_ids.reshape(-1)[pair_at], axis=0)  6.65 us
    dot_general x1, matrix products, window_attention(): jnp.einsum('thqk,tkhe->tqhe', attn_weights, values_h, preferred_element_t...  4.29 us

profile of v11, /device:TPU:1, one launch (start us, length us, event | category | flops | bytes accessed | tf_op | source)
XLA Modules:
  0.0 187.5 jit_solution(14560384524841382627)
XLA Ops:
  2.3 21.9 %shard_map.167 = bf16[2,512,1024]{2,1,0:T(8,128)(2,1)} custom-call(bf16[2,128,1024]{2,1,0:T(8,128)(2,1)} %x_ref.1), custom_call_target="tpu_custom_call" | custom-call | tf_op jit(solution)/shard_map/pallas_call | solution.py:74
  24.3 3.9 %add_convert_fusion = bf16[2,512,3,256]{1,3,2,0:T(8,128)(2,1)S(1)} fusion(f32[3,256]{1,0:T(4,128)} %param.21, bf16[1024,3,256]{2,0,1:T(8,128)(2,1)} %param.20, bf16[2,512,1024]{2,1,0:T(8,128)(2,1)} %shard_map.167), kind=kOutput, calls=%fused_computation.68 | convolution fusion | flops 1612185600 | bytes 5245952 | tf_op jit(solution)/shard_map/tsd,dce->tsce/dot_general | solution.py:310
  28.2 1.2 fusion.47
  29.7 7.7 %fusion.48 = (f32[2,4,512]{2,1,0:T(4,128)S(1)}, f32[2,4,512,512]{2,3,1,0:T(8,128)}) fusion(pred[2,512,512]{1,2,0:T(8,128)(4,1)S(1)} %broadcast_and_fusion, bf16[2,512,4,64]{1,3,2,0:T(8,128)(2,1)} %bitcast.73, bf16[2,512,4,64]{1,3,2,0:T(8,128)(2,1)} %bitcast.72), kind=kOutput, calls=%fused_computation.120 | convolution fusion | flops 276824576 | bytes 9977856 | tf_op jit(solution)/shard_map/sub | solution.py:267
  37.3 4.3 %fusion.36 = bf16[2,4,64,512]{3,2,1,0:T(8,128)(2,1)S(1)} fusion(bf16[2,512,4,64]{1,3,2,0:T(8,128)(2,1)S(1)} %bitcast.71, f32[2,4,512,512]{2,3,1,0:T(8,128)} %get-tuple-element.58, f32[2,4,512]{2,1,0:T(4,128)S(1)} %get-tuple-element.57, pred[2,512]{1,0:T(4,128)(4,1)S(1)} %iota_compare_fusion.1), kind=kOutput, calls=%fused_computation.81 | convolution fusion | flops 273154048 | bytes 9454592 | tf_op jit(solution)/shard_map/thqk,tkhe->tqhe/dot_general | solution.py:269
  41.6 2.1 %convolution_convert_fusion.p_ref = bf16[2,512,1024]{2,1,0:T(8,128)(2,1)} fusion(bf16[2,512,256]{1,2,0:T(8,128)(2,1)S(1)} %bitcast.74, bf16[256,1024]{1,0:T(8,128)(2,1)S(1)} %copy-done.1), kind=kOutput, calls=%fused_computation.78 | convolution fusion | flops 537919488 | bytes 3145728 | tf_op jit(solution)/shard_map/tsk,kd->tsd/dot_general | solution.py:317
  43.7 20.2 %shard_map.168 = bf16[2,2,128,1024]{3,2,1,0:T(8,128)(2,1)} custom-call(bf16[2,512,1024]{2,1,0:T(8,128)(2,1)} %convolution_convert_fusion.p_ref), custom_call_target="tpu_custom_call" | custom-call | tf_op jit(solution)/shard_map/pallas_call | solution.py:141
  63.9 2.5 %convert_reduce_fusion.1 = f32[2,128,1024]{2,1,0:T(8,128)} fusion(bf16[2,2,128,1024]{3,2,1,0:T(8,128)(2,1)} %shard_map.168), kind=kLoop, calls=%fused_computation.76 | loop fusion | flops 786432 | bytes 2097152 | tf_op jit(solution)/shard_map/reduce_sum | solution.py:322
  66.4 1.8 fusion.46
  68.5 1.0 add_convert_fusion.2.x_ref
  69.6 21.2 %shard_map.169 = bf16[2,512,1024]{2,1,0:T(8,128)(2,1)} custom-call(bf16[2,128,1024]{2,1,0:T(8,128)(2,1)} %add_convert_fusion.2.x_ref), custom_call_target="tpu_custom_call" | custom-call | tf_op jit(solution)/shard_map/pallas_call | solution.py:74
  90.8 12.7 %fusion.7 = bf16[2,512,1024]{2,1,0:T(8,128)(2,1)S(1)} fusion(f32[1024]{0:T(1024)S(1)} %copy-done.11, bf16[2,512,1024]{2,1,0:T(8,128)(2,1)} %shard_map.169, bf16[1024,1024]{1,0:T(8,128)(2,1)S(1)} %copy-done), kind=kOutput, calls=%fused_computation.48 | convolution fusion | flops 2216689664 | bytes 6295552 | tf_op jit(solution)/shard_map/tsd,df->tsf/dot_general | solution.py:328
  103.5 3.7 %fusion.25.p_ref = bf16[2,512,1024]{2,1,0:T(8,128)(2,1)} fusion(bf16[2,512,1024]{2,1,0:T(8,128)(2,1)S(1)} %fusion.7, bf16[1024,1024]{1,0:T(8,128)(2,1)S(1)} %copy-done.10), kind=kOutput, calls=%fused_computation.77 | convolution fusion | flops 2148532224 | bytes 6291456 | tf_op jit(solution)/shard_map/tsf,fd->tsd/dot_general | solution.py:332
  107.2 20.9 %shard_map.170 = bf16[2,2,128,1024]{3,2,1,0:T(8,128)(2,1)} custom-call(bf16[2,512,1024]{2,1,0:T(8,128)(2,1)} %fusion.25.p_ref), custom_call_target="tpu_custom_call" | custom-call | tf_op jit(solution)/shard_map/pallas_call | solution.py:141
  128.2 1.6 convert_reduce_fusion
  129.7 1.5 fusion.45
  131.7 1.2 select_reduce_fusion.3
  133.4 6.0 %shard_map.171 = f32[4,2,1040]{2,1,0:T(2,128)} custom-call(f32[2,1040]{1,0:T(2,128)} %pad_maximum_fusion.x_ref), custom_call_target="tpu_custom_call" | custom-call | tf_op jit(solution)/shard_map/pallas_call | solution.py:224
  141.9 14.9 %shard_map.172 = f32[32,2,1088]{2,1,0:T(2,128)} custom-call(f32[2,1088]{1,0:T(2,128)} %pad_maximum_fusion.1.x_ref), custom_call_target="tpu_custom_call" | custom-call | tf_op jit(solution)/shard_map/pallas_call | solution.py:224
  156.8 1.2 reshape.315
  159.3 10.3 %conditional.1 = (f32[64,64]{1,0:T(8,128)S(1)}) conditional(s32[]{:T(128)} %convert_element_type.101, (s32[64,64]{1,0:T(8,128)S(1)}, bf16[4096,1024]{1,0:T(8,128)(2,1)}, bf16[64,1024]{1,0:T(8,128)(2,1)S(1)}, pred[64,64]{1,0:T(8,128)(4,1)S(1)}) %tuple.14, (pred[64,64]{1,0:T(8,128)(4,1)S(1)}, s32[64,64]{1,0:T(8,128)S(1)}, ...), branch_computations={%region_12.14_spmd, %region_14.0_spmd} | conditional | flops 537702400 | bytes 12955656 | solution.py:397
  161.1 1.1 gather_fusion
  162.3 5.5 %gather_fusion.1 = bf16[128,1024]{1,0:T(8,128)(2,1)S(1)} fusion(bf16[4096,1024]{1,0:T(8,128)(2,1)} %get-tuple-element.25, s32[1024]{0:T(1024)S(1)} %pad_clamp_fusion.1), kind=kCustom, calls=%fused_computation.2 | custom fusion | bytes 524800 | tf_op jit(solution)/shard_map/cond/branch_1_fun/jit(_take)/gather | solution.py:380
  169.8 16.9 %all_to_all.5 = f32[128,2,16]{2,1,0:T(2,128)S(1)} all-to-all(f32[128,2,16]{2,1,0:T(2,128)S(1)} %copy.46), channel_id=1, replica_groups=mesh['req'=32,'tp'=4] {'req','tp'}, dimensions={0} | all-to-all | bytes 32768 | tf_op jit(solution)/shard_map/all_to_all | solution.py:403
  (73 shorter events, 10.6 us)
Async XLA Ops:
  0.6 90.1 %copy-start = (bf16[1024,1024]{1,0:T(8,128)(2,1)S(1)}, bf16[1024,1024]{1,0:T(8,128)(2,1)}, u32[]{:S(2)}) copy-start(bf16[1024,1024]{1,0:T(8,128)(2,1)} %param.26) | copy-start | bytes 6291460
  37.3 4.3 %copy-start.1 = (bf16[256,1024]{1,0:T(8,128)(2,1)S(1)}, bf16[256,1024]{1,0:T(8,128)(2,1)}, u32[]{:S(2)}) copy-start(bf16[256,1024]{1,0:T(8,128)(2,1)} %param.22) | copy-start | bytes 1572868
  41.6 24.8 %copy-start.4 = (f32[1024]{0:T(1024)S(1)}, f32[1024]{0:T(1024)}, u32[]{:S(2)}) copy-start(f32[1024]{0:T(1024)} %param.23) | copy-start | bytes 12292
  43.7 24.8 %copy-start.2 = (f32[1024]{0:T(1024)S(1)}, f32[1024]{0:T(1024)}, u32[]{:S(2)}) copy-start(f32[1024]{0:T(1024)} %param.25) | copy-start | bytes 12292
  43.7 24.8 %copy-start.3 = (f32[1024]{0:T(1024)S(1)}, f32[1024]{0:T(1024)}, u32[]{:S(2)}) copy-start(f32[1024]{0:T(1024)} %param.24) | copy-start | bytes 12292
  66.4 24.4 %copy-start.11 = (f32[1024]{0:T(1024)S(1)}, f32[1024]{0:T(1024)}, u32[]{:S(2)}) copy-start(f32[1024]{0:T(1024)} %param.27) | copy-start | bytes 12292
  90.8 12.7 %copy-start.10 = (bf16[1024,1024]{1,0:T(8,128)(2,1)S(1)}, bf16[1024,1024]{1,0:T(8,128)(2,1)}, u32[]{:S(2)}) copy-start(bf16[1024,1024]{1,0:T(8,128)(2,1)} %param.28) | copy-start | bytes 6291460
  107.2 22.5 %copy-start.5 = (f32[1024]{0:T(1024)S(1)}, f32[1024]{0:T(1024)}, u32[]{:S(2)}) copy-start(f32[1024]{0:T(1024)} %param.29) | copy-start | bytes 12292
  128.1 3.5 %copy-start.9 = (s32[2]{0:T(128)S(1)}, s32[2]{0:T(128)}, u32[]{:S(2)}) copy-start(s32[2]{0:T(128)} %param.19) | copy-start | bytes 28
  128.1 3.5 %copy-start.8 = (s32[2,16]{1,0:T(2,128)S(1)}, s32[2,16]{1,0:T(2,128)}, u32[]{:S(2)}) copy-start(s32[2,16]{1,0:T(2,128)} %param.33) | copy-start | bytes 388
  128.1 3.5 %copy-start.6 = (f32[1024]{0:T(1024)S(1)}, f32[1024]{0:T(1024)}, u32[]{:S(2)}) copy-start(f32[1024]{0:T(1024)} %param.31) | copy-start | bytes 12292
  128.1 3.5 %copy-start.7 = (f32[1024]{0:T(1024)S(1)}, f32[1024]{0:T(1024)}, u32[]{:S(2)}) copy-start(f32[1024]{0:T(1024)} %param.30) | copy-start | bytes 12292

commit v12 on v11

--- a/solution.py
+++ b/solution.py
@@ -236,8 +236,8 @@
 
 
 HEAD_DIM = 64
-RING_CHUNKS = 4
-SPARSE_PAIRS = 128
+RING_CHUNKS = 8
+SPARSE_PAIRS = 64
 WINDOW = 512
 
 

time: 188 us -> 188 us (level)
  no operation moved by 1% of the time
where the time goes in v12:
time: 188 us; the launch traced here: 187 us
  Pallas kernels  106 us (56%)
  matrix products  34.4 us (18%)
  other arithmetic  17.4 us (9%)
  blocking collectives  16.9 us (9%)
  local copies, waits for them, and re-layouts  10.5 us (6%)
    pallas_call x2, Pallas kernels, ring_all_gather(): pl.pallas_call(functools.partial(_gather_kernel, chunks), out_shape=jax.S...  43.6 us
    pallas_call x2, Pallas kernels, ring_reduce_scatter_add(): pl.pallas_call(functools.partial(_scatter_add_kernel, chunks), out_shape=...  41.6 us
    pallas_call x2, Pallas kernels, direct_exchange(): pl.pallas_call(functools.partial(_direct_kernel, axes, scatter), out_shap...  20.9 us
    all_to_all x1, blocking collectives, per_device(): lax.all_to_all(owner_terms, ('req', 'tp'), 0, 0, tiled=True)  16.9 us
    dot_general x1, matrix products, per_device(): jnp.einsum('tsd,df->tsf', normed_full, w_up, preferred_element_type=jnp.f...  12.7 us
    sub x1, matrix products, window_attention(): expo = jnp.exp(logits - top_val)  7.66 us
    gather x2, local copies, waits for them, and re-layouts, few_owned(): rows = jnp.take(index_rows, safe_ids.reshape(-1)[pair_at], axis=0)  6.03 us
    dot_general x1, matrix products, window_attention(): jnp.einsum('thqk,tkhe->tqhe', attn_weights, values_h, preferred_element_t...  4.29 us

profile of v12, /device:TPU:1, one launch (start us, length us, event | category | flops | bytes accessed | tf_op | source)
XLA Modules:
  0.0 187.2 jit_solution(7066166352045201878)
XLA Ops:
  0.8 0.8 iota_compare_fusion.1
  2.3 22.2 %shard_map.167 = bf16[2,512,1024]{2,1,0:T(8,128)(2,1)} custom-call(bf16[2,128,1024]{2,1,0:T(8,128)(2,1)} %x_ref.1), custom_call_target="tpu_custom_call" | custom-call | tf_op jit(solution)/shard_map/pallas_call | solution.py:74
  24.5 3.9 %add_convert_fusion = bf16[2,512,3,256]{1,3,2,0:T(8,128)(2,1)S(1)} fusion(f32[3,256]{1,0:T(4,128)} %param.21, bf16[1024,3,256]{2,0,1:T(8,128)(2,1)} %param.20, bf16[2,512,1024]{2,1,0:T(8,128)(2,1)} %shard_map.167), kind=kOutput, calls=%fused_computation.68 | convolution fusion | flops 1612185600 | bytes 5245952 | tf_op jit(solution)/shard_map/tsd,dce->tsce/dot_general | solution.py:310
  28.4 1.2 fusion.47
  29.9 7.7 %fusion.48 = (f32[2,4,512]{2,1,0:T(4,128)S(1)}, f32[2,4,512,512]{2,3,1,0:T(8,128)}) fusion(pred[2,512,512]{1,2,0:T(8,128)(4,1)S(1)} %broadcast_and_fusion, bf16[2,512,4,64]{1,3,2,0:T(8,128)(2,1)} %bitcast.73, bf16[2,512,4,64]{1,3,2,0:T(8,128)(2,1)} %bitcast.72), kind=kOutput, calls=%fused_computation.120 | convolution fusion | flops 276824576 | bytes 9977856 | tf_op jit(solution)/shard_map/sub | solution.py:267
  37.6 4.3 %fusion.36 = bf16[2,4,64,512]{3,2,1,0:T(8,128)(2,1)S(1)} fusion(bf16[2,512,4,64]{1,3,2,0:T(8,128)(2,1)S(1)} %bitcast.71, f32[2,4,512,512]{2,3,1,0:T(8,128)} %get-tuple-element.58, f32[2,4,512]{2,1,0:T(4,128)S(1)} %get-tuple-element.57, pred[2,512]{1,0:T(4,128)(4,1)S(1)} %iota_compare_fusion.1), kind=kOutput, calls=%fused_computation.81 | convolution fusion | flops 273154048 | bytes 9454592 | tf_op jit(solution)/shard_map/thqk,tkhe->tqhe/dot_general | solution.py:269
  41.9 2.1 %convolution_convert_fusion.p_ref = bf16[2,512,1024]{2,1,0:T(8,128)(2,1)} fusion(bf16[2,512,256]{1,2,0:T(8,128)(2,1)S(1)} %bitcast.74, bf16[256,1024]{1,0:T(8,128)(2,1)S(1)} %copy-done.1), kind=kOutput, calls=%fused_computation.78 | convolution fusion | flops 537919488 | bytes 3145728 | tf_op jit(solution)/shard_map/tsk,kd->tsd/dot_general | solution.py:317
  44.0 20.4 %shard_map.168 = bf16[2,2,128,1024]{3,2,1,0:T(8,128)(2,1)} custom-call(bf16[2,512,1024]{2,1,0:T(8,128)(2,1)} %convolution_convert_fusion.p_ref), custom_call_target="tpu_custom_call" | custom-call | tf_op jit(solution)/shard_map/pallas_call | solution.py:141
  64.4 2.5 %convert_reduce_fusion.1 = f32[2,128,1024]{2,1,0:T(8,128)} fusion(bf16[2,2,128,1024]{3,2,1,0:T(8,128)(2,1)} %shard_map.168), kind=kLoop, calls=%fused_computation.76 | loop fusion | flops 786432 | bytes 2097152 | tf_op jit(solution)/shard_map/reduce_sum | solution.py:322
  66.9 1.8 fusion.46
  69.0 1.0 add_convert_fusion.2.x_ref
  70.1 21.4 %shard_map.169 = bf16[2,512,1024]{2,1,0:T(8,128)(2,1)} custom-call(bf16[2,128,1024]{2,1,0:T(8,128)(2,1)} %add_convert_fusion.2.x_ref), custom_call_target="tpu_custom_call" | custom-call | tf_op jit(solution)/shard_map/pallas_call | solution.py:74
  91.5 12.7 %fusion.7 = bf16[2,512,1024]{2,1,0:T(8,128)(2,1)S(1)} fusion(f32[1024]{0:T(1024)S(1)} %copy-done.11, bf16[2,512,1024]{2,1,0:T(8,128)(2,1)} %shard_map.169, bf16[1024,1024]{1,0:T(8,128)(2,1)S(1)} %copy-done), kind=kOutput, calls=%fused_computation.48 | convolution fusion | flops 2216689664 | bytes 6295552 | tf_op jit(solution)/shard_map/tsd,df->tsf/dot_general | solution.py:328
  104.3 3.7 %fusion.25.p_ref = bf16[2,512,1024]{2,1,0:T(8,128)(2,1)} fusion(bf16[2,512,1024]{2,1,0:T(8,128)(2,1)S(1)} %fusion.7, bf16[1024,1024]{1,0:T(8,128)(2,1)S(1)} %copy-done.10), kind=kOutput, calls=%fused_computation.77 | convolution fusion | flops 2148532224 | bytes 6291456 | tf_op jit(solution)/shard_map/tsf,fd->tsd/dot_general | solution.py:332
  108.0 21.1 %shard_map.170 = bf16[2,2,128,1024]{3,2,1,0:T(8,128)(2,1)} custom-call(bf16[2,512,1024]{2,1,0:T(8,128)(2,1)} %fusion.25.p_ref), custom_call_target="tpu_custom_call" | custom-call | tf_op jit(solution)/shard_map/pallas_call | solution.py:141
  129.2 1.6 convert_reduce_fusion
  130.7 1.5 fusion.45
  132.7 1.2 select_reduce_fusion.3
  134.4 6.0 %shard_map.171 = f32[4,2,1040]{2,1,0:T(2,128)} custom-call(f32[2,1040]{1,0:T(2,128)} %pad_maximum_fusion.x_ref), custom_call_target="tpu_custom_call" | custom-call | tf_op jit(solution)/shard_map/pallas_call | solution.py:224
  142.9 14.9 %shard_map.172 = f32[32,2,1088]{2,1,0:T(2,128)} custom-call(f32[2,1088]{1,0:T(2,128)} %pad_maximum_fusion.1.x_ref), custom_call_target="tpu_custom_call" | custom-call | tf_op jit(solution)/shard_map/pallas_call | solution.py:224
  157.8 1.2 reshape.315
  160.3 9.0 %conditional.1 = (f32[64,64]{1,0:T(8,128)S(1)}) conditional(s32[]{:T(128)} %convert_element_type.101, (s32[64,64]{1,0:T(8,128)S(1)}, bf16[4096,1024]{1,0:T(8,128)(2,1)}, bf16[64,1024]{1,0:T(8,128)(2,1)S(1)}, pred[64,64]{1,0:T(8,128)(4,1)S(1)}) %tuple.14, (pred[64,64]{1,0:T(8,128)(4,1)S(1)}, s32[64,64]{1,0:T(8,128)S(1)}, ...), branch_computations={%region_12.14_spmd, %region_14.0_spmd} | conditional | flops 537702400 | bytes 12955656 | solution.py:397
  162.7 5.3 %gather_fusion.1 = bf16[64,1024]{1,0:T(8,128)(2,1)S(1)} fusion(bf16[4096,1024]{1,0:T(8,128)(2,1)} %get-tuple-element.25, s32[1024]{0:T(1024)S(1)} %pad_clamp_fusion.1), kind=kCustom, calls=%fused_computation.2 | custom fusion | bytes 262400 | tf_op jit(solution)/shard_map/cond/branch_1_fun/jit(_take)/gather | solution.py:380
  169.6 16.9 %all_to_all.5 = f32[128,2,16]{2,1,0:T(2,128)S(1)} all-to-all(f32[128,2,16]{2,1,0:T(2,128)S(1)} %copy.46), channel_id=1, replica_groups=mesh['req'=32,'tp'=4] {'req','tp'}, dimensions={0} | all-to-all | bytes 32768 | tf_op jit(solution)/shard_map/all_to_all | solution.py:403
  (73 shorter events, 9.9 us)
Async XLA Ops:
  0.6 90.9 %copy-start = (bf16[1024,1024]{1,0:T(8,128)(2,1)S(1)}, bf16[1024,1024]{1,0:T(8,128)(2,1)}, u32[]{:S(2)}) copy-start(bf16[1024,1024]{1,0:T(8,128)(2,1)} %param.26) | copy-start | bytes 6291460
  37.6 4.3 %copy-start.1 = (bf16[256,1024]{1,0:T(8,128)(2,1)S(1)}, bf16[256,1024]{1,0:T(8,128)(2,1)}, u32[]{:S(2)}) copy-start(bf16[256,1024]{1,0:T(8,128)(2,1)} %param.22) | copy-start | bytes 1572868
  41.9 25.1 %copy-start.4 = (f32[1024]{0:T(1024)S(1)}, f32[1024]{0:T(1024)}, u32[]{:S(2)}) copy-start(f32[1024]{0:T(1024)} %param.23) | copy-start | bytes 12292
  44.0 25.0 %copy-start.2 = (f32[1024]{0:T(1024)S(1)}, f32[1024]{0:T(1024)}, u32[]{:S(2)}) copy-start(f32[1024]{0:T(1024)} %param.25) | copy-start | bytes 12292
  44.0 25.1 %copy-start.3 = (f32[1024]{0:T(1024)S(1)}, f32[1024]{0:T(1024)}, u32[]{:S(2)}) copy-start(f32[1024]{0:T(1024)} %param.24) | copy-start | bytes 12292
  66.9 24.6 %copy-start.11 = (f32[1024]{0:T(1024)S(1)}, f32[1024]{0:T(1024)}, u32[]{:S(2)}) copy-start(f32[1024]{0:T(1024)} %param.27) | copy-start | bytes 12292
  91.5 12.7 %copy-start.10 = (bf16[1024,1024]{1,0:T(8,128)(2,1)S(1)}, bf16[1024,1024]{1,0:T(8,128)(2,1)}, u32[]{:S(2)}) copy-start(bf16[1024,1024]{1,0:T(8,128)(2,1)} %param.28) | copy-start | bytes 6291460
  108.0 22.8 %copy-start.5 = (f32[1024]{0:T(1024)S(1)}, f32[1024]{0:T(1024)}, u32[]{:S(2)}) copy-start(f32[1024]{0:T(1024)} %param.29) | copy-start | bytes 12292
  129.1 3.5 %copy-start.9 = (s32[2]{0:T(128)S(1)}, s32[2]{0:T(128)}, u32[]{:S(2)}) copy-start(s32[2]{0:T(128)} %param.19) | copy-start | bytes 28
  129.1 3.5 %copy-start.8 = (s32[2,16]{1,0:T(2,128)S(1)}, s32[2,16]{1,0:T(2,128)}, u32[]{:S(2)}) copy-start(s32[2,16]{1,0:T(2,128)} %param.33) | copy-start | bytes 388
  129.1 3.5 %copy-start.6 = (f32[1024]{0:T(1024)S(1)}, f32[1024]{0:T(1024)}, u32[]{:S(2)}) copy-start(f32[1024]{0:T(1024)} %param.31) | copy-start | bytes 12292
  129.1 3.5 %copy-start.7 = (f32[1024]{0:T(1024)S(1)}, f32[1024]{0:T(1024)}, u32[]{:S(2)}) copy-start(f32[1024]{0:T(1024)} %param.30) | copy-start | bytes 12292

commit v13 on v12

--- a/solution.py
+++ b/solution.py
@@ -236,7 +236,7 @@
 
 
 HEAD_DIM = 64
-RING_CHUNKS = 8
+RING_CHUNKS = 4
 SPARSE_PAIRS = 64
 WINDOW = 512
 
@@ -377,8 +377,14 @@
         chosen = flat_owned[None, :] & (running[None, :] == rank[:, None] + 1)
         pair_index = jnp.arange(flat_owned.shape[0], dtype=jnp.int32)
         pair_at = jnp.sum(jnp.where(chosen, pair_index[None, :], 0), axis=1)
-        rows = jnp.take(index_rows, safe_ids.reshape(-1)[pair_at], axis=0)
-        queries = jnp.take(all_queries, pair_at // all_ids.shape[1], axis=0)
+        row_of = jnp.sum(jnp.where(chosen, safe_ids.reshape(-1)[None, :], 0), axis=1)
+        row_pick = jnp.arange(rows_here, dtype=jnp.int32)[None, :] == row_of[:, None]
+        rows = jnp.dot(row_pick.astype(index_rows.dtype), index_rows, preferred_element_type=jnp.float32)
+        text_of = pair_at // all_ids.shape[1]
+        text_pick = jnp.arange(all_queries.shape[0], dtype=jnp.int32)[None, :] == text_of[:, None]
+        queries = jnp.dot(
+            text_pick.astype(all_queries.dtype), all_queries, preferred_element_type=jnp.float32
+        )
         values = jnp.sum(rows.astype(jnp.float32) * queries.astype(jnp.float32), axis=-1)
         return jnp.sum(
             jnp.where(chosen, values[:, None], jnp.float32(0.0)), axis=0

time: 188 us -> 185 us (0.984)
  local copies, waits for them, and re-layouts: 10.5 us -> 3.8 us
  matrix products: 34.4 us -> 39.7 us
    gather x3 -> x0, local copies, waits for them, and re-layouts: 6.74 us -> none  [the longest x2 6.03 us: few_owned(): rows = jnp.take(index_rows, safe_ids.reshape(-1)[pair_at], axis=0)]
    dot_general x0 -> x2, matrix products: none -> 5.33 us  [the longest x1 5 us: few_owned(): jnp.dot(row_pick.astype(index_rows.dtype), index_rows, preferred_element_...]
where the time goes in v13:
time: 185 us
  Pallas kernels  105 us (57%)
  matrix products  39.7 us (21%)
  other arithmetic  17.3 us (9%)
  blocking collectives  16.9 us (9%)
  local copies, waits for them, and re-layouts  3.8 us (2%)
    pallas_call x2, Pallas kernels, ring_all_gather(): pl.pallas_call(functools.partial(_gather_kernel, chunks), out_shape=jax.S...  43.1 us
    pallas_call x2, Pallas kernels, ring_reduce_scatter_add(): pl.pallas_call(functools.partial(_scatter_add_kernel, chunks), out_shape=...  41 us
    pallas_call x2, Pallas kernels, direct_exchange(): pl.pallas_call(functools.partial(_direct_kernel, axes, scatter), out_shap...  20.9 us
    all_to_all x1, blocking collectives, per_device(): lax.all_to_all(owner_terms, ('req', 'tp'), 0, 0, tiled=True)  16.9 us
    dot_general x1, matrix products, per_device(): jnp.einsum('tsd,df->tsf', normed_full, w_up, preferred_element_type=jnp.f...  12.7 us
    sub x1, matrix products, window_attention(): expo = jnp.exp(logits - top_val)  7.66 us
    dot_general x1, matrix products, few_owned(): jnp.dot(row_pick.astype(index_rows.dtype), index_rows, preferred_element_...  5 us
    dot_general x1, matrix products, window_attention(): jnp.einsum('thqk,tkhe->tqhe', attn_weights, values_h, preferred_element_t...  4.29 us

profile of v13, /device:TPU:1, one launch (start us, length us, event | category | flops | bytes accessed | tf_op | source)
XLA Modules:
  0.0 184.7 jit_solution(2878244244848573739)
XLA Ops:
  0.8 0.8 iota_compare_fusion.5
  2.3 21.9 %shard_map.167 = bf16[2,512,1024]{2,1,0:T(8,128)(2,1)} custom-call(bf16[2,128,1024]{2,1,0:T(8,128)(2,1)} %x_ref.1), custom_call_target="tpu_custom_call" | custom-call | tf_op jit(solution)/shard_map/pallas_call | solution.py:74
  24.3 3.9 %add_convert_fusion = bf16[2,512,3,256]{1,3,2,0:T(8,128)(2,1)S(1)} fusion(f32[3,256]{1,0:T(4,128)} %param.21, bf16[1024,3,256]{2,0,1:T(8,128)(2,1)} %param.20, bf16[2,512,1024]{2,1,0:T(8,128)(2,1)} %shard_map.167), kind=kOutput, calls=%fused_computation.54 | convolution fusion | flops 1612185600 | bytes 5245952 | tf_op jit(solution)/shard_map/tsd,dce->tsce/dot_general | solution.py:310
  28.2 1.2 fusion.48
  29.7 7.7 %fusion.49 = (f32[2,4,512]{2,1,0:T(4,128)S(1)}, f32[2,4,512,512]{2,3,1,0:T(8,128)}) fusion(pred[2,512,512]{1,2,0:T(8,128)(4,1)S(1)} %broadcast_and_fusion, bf16[2,512,4,64]{1,3,2,0:T(8,128)(2,1)} %bitcast.56, bf16[2,512,4,64]{1,3,2,0:T(8,128)(2,1)} %bitcast.55), kind=kOutput, calls=%fused_computation.106 | convolution fusion | flops 276824576 | bytes 9977856 | tf_op jit(solution)/shard_map/sub | solution.py:267
  37.3 4.3 %fusion.37 = bf16[2,4,64,512]{3,2,1,0:T(8,128)(2,1)S(1)} fusion(bf16[2,512,4,64]{1,3,2,0:T(8,128)(2,1)S(1)} %bitcast.54, f32[2,4,512,512]{2,3,1,0:T(8,128)} %get-tuple-element.56, f32[2,4,512]{2,1,0:T(4,128)S(1)} %get-tuple-element.55, pred[2,512]{1,0:T(4,128)(4,1)S(1)} %iota_compare_fusion.5), kind=kOutput, calls=%fused_computation.67 | convolution fusion | flops 273154048 | bytes 9454592 | tf_op jit(solution)/shard_map/thqk,tkhe->tqhe/dot_general | solution.py:269
  41.6 2.1 %convolution_convert_fusion.p_ref = bf16[2,512,1024]{2,1,0:T(8,128)(2,1)} fusion(bf16[2,512,256]{1,2,0:T(8,128)(2,1)S(1)} %bitcast.57, bf16[256,1024]{1,0:T(8,128)(2,1)S(1)} %copy-done.1), kind=kOutput, calls=%fused_computation.64 | convolution fusion | flops 537919488 | bytes 3145728 | tf_op jit(solution)/shard_map/tsk,kd->tsd/dot_general | solution.py:317
  43.7 20.2 %shard_map.168 = bf16[2,2,128,1024]{3,2,1,0:T(8,128)(2,1)} custom-call(bf16[2,512,1024]{2,1,0:T(8,128)(2,1)} %convolution_convert_fusion.p_ref), custom_call_target="tpu_custom_call" | custom-call | tf_op jit(solution)/shard_map/pallas_call | solution.py:141
  63.9 2.5 %convert_reduce_fusion.1 = f32[2,128,1024]{2,1,0:T(8,128)} fusion(bf16[2,2,128,1024]{3,2,1,0:T(8,128)(2,1)} %shard_map.168), kind=kLoop, calls=%fused_computation.62 | loop fusion | flops 786432 | bytes 2097152 | tf_op jit(solution)/shard_map/reduce_sum | solution.py:322
  66.4 1.8 fusion.47
  68.5 1.0 add_convert_fusion.2.x_ref
  69.6 21.2 %shard_map.169 = bf16[2,512,1024]{2,1,0:T(8,128)(2,1)} custom-call(bf16[2,128,1024]{2,1,0:T(8,128)(2,1)} %add_convert_fusion.2.x_ref), custom_call_target="tpu_custom_call" | custom-call | tf_op jit(solution)/shard_map/pallas_call | solution.py:74
  90.8 12.7 %fusion.8 = bf16[2,512,1024]{2,1,0:T(8,128)(2,1)S(1)} fusion(f32[1024]{0:T(1024)S(1)} %copy-done.11, bf16[2,512,1024]{2,1,0:T(8,128)(2,1)} %shard_map.169, bf16[1024,1024]{1,0:T(8,128)(2,1)S(1)} %copy-done), kind=kOutput, calls=%fused_computation.34 | convolution fusion | flops 2216689664 | bytes 6295552 | tf_op jit(solution)/shard_map/tsd,df->tsf/dot_general | solution.py:328
  103.5 3.7 %fusion.26.p_ref = bf16[2,512,1024]{2,1,0:T(8,128)(2,1)} fusion(bf16[2,512,1024]{2,1,0:T(8,128)(2,1)S(1)} %fusion.8, bf16[1024,1024]{1,0:T(8,128)(2,1)S(1)} %copy-done.10), kind=kOutput, calls=%fused_computation.63 | convolution fusion | flops 2148532224 | bytes 6291456 | tf_op jit(solution)/shard_map/tsf,fd->tsd/dot_general | solution.py:332
  107.2 20.9 %shard_map.170 = bf16[2,2,128,1024]{3,2,1,0:T(8,128)(2,1)} custom-call(bf16[2,512,1024]{2,1,0:T(8,128)(2,1)} %fusion.26.p_ref), custom_call_target="tpu_custom_call" | custom-call | tf_op jit(solution)/shard_map/pallas_call | solution.py:141
  128.2 1.6 convert_reduce_fusion
  129.7 1.5 fusion.46
  131.7 1.2 select_reduce_fusion.4
  133.4 6.0 %shard_map.171 = f32[4,2,1040]{2,1,0:T(2,128)} custom-call(f32[2,1040]{1,0:T(2,128)} %pad_maximum_fusion.x_ref), custom_call_target="tpu_custom_call" | custom-call | tf_op jit(solution)/shard_map/pallas_call | solution.py:224
  141.9 14.9 %shard_map.172 = f32[32,2,1088]{2,1,0:T(2,128)} custom-call(f32[2,1088]{1,0:T(2,128)} %pad_maximum_fusion.1.x_ref), custom_call_target="tpu_custom_call" | custom-call | tf_op jit(solution)/shard_map/pallas_call | solution.py:224
  156.8 1.2 reshape.241
  159.3 7.5 %conditional.1 = (f32[64,64]{1,0:T(8,128)S(1)}) conditional(s32[]{:T(128)} %convert_element_type.97, (s32[64,64]{1,0:T(8,128)S(1)}, bf16[4096,1024]{1,0:T(8,128)(2,1)}, bf16[64,1024]{1,0:T(8,128)(2,1)S(1)}, pred[64,64]{1,0:T(8,128)(4,1)S(1)}) %tuple.14, (pred[64,64]{1,0:T(8,128)(4,1)S(1)}, s32[64,64]{1,0:T(8,128)S(1)}, ...), branch_computations={%region_12.14_spmd, %region_14.21_spmd} | conditional | flops 548545344 | bytes 12955656 | solution.py:403
  161.0 5.0 %fusion.1 = f32[64,1024]{1,0:T(8,128)S(1)} fusion(bf16[4096,1024]{1,0:T(8,128)(2,1)} %get-tuple-element.25, s32[64]{0:T(128)S(1)} %get-tuple-element.38), kind=kOutput, calls=%fused_computation.14 | convolution fusion | flops 537133056 | bytes 8651008 | tf_op jit(solution)/shard_map/cond/branch_1_fun/dot_general | solution.py:382
  167.0 16.9 %all_to_all.5 = f32[128,2,16]{2,1,0:T(2,128)S(1)} all-to-all(f32[128,2,16]{2,1,0:T(2,128)S(1)} %copy.46), channel_id=1, replica_groups=mesh['req'=32,'tp'=4] {'req','tp'}, dimensions={0} | all-to-all | bytes 32768 | tf_op jit(solution)/shard_map/all_to_all | solution.py:409
  (66 shorter events, 8.6 us)
Async XLA Ops:
  0.6 90.1 %copy-start = (bf16[1024,1024]{1,0:T(8,128)(2,1)S(1)}, bf16[1024,1024]{1,0:T(8,128)(2,1)}, u32[]{:S(2)}) copy-start(bf16[1024,1024]{1,0:T(8,128)(2,1)} %param.26) | copy-start | bytes 6291460
  37.3 4.3 %copy-start.1 = (bf16[256,1024]{1,0:T(8,128)(2,1)S(1)}, bf16[256,1024]{1,0:T(8,128)(2,1)}, u32[]{:S(2)}) copy-start(bf16[256,1024]{1,0:T(8,128)(2,1)} %param.22) | copy-start | bytes 1572868
  41.6 24.8 %copy-start.4 = (f32[1024]{0:T(1024)S(1)}, f32[1024]{0:T(1024)}, u32[]{:S(2)}) copy-start(f32[1024]{0:T(1024)} %param.23) | copy-start | bytes 12292
  43.7 24.8 %copy-start.2 = (f32[1024]{0:T(1024)S(1)}, f32[1024]{0:T(1024)}, u32[]{:S(2)}) copy-start(f32[1024]{0:T(1024)} %param.25) | copy-start | bytes 12292
  43.7 24.8 %copy-start.3 = (f32[1024]{0:T(1024)S(1)}, f32[1024]{0:T(1024)}, u32[]{:S(2)}) copy-start(f32[1024]{0:T(1024)} %param.24) | copy-start | bytes 12292
  66.4 24.4 %copy-start.11 = (f32[1024]{0:T(1024)S(1)}, f32[1024]{0:T(1024)}, u32[]{:S(2)}) copy-start(f32[1024]{0:T(1024)} %param.27) | copy-start | bytes 12292
  90.8 12.7 %copy-start.10 = (bf16[1024,1024]{1,0:T(8,128)(2,1)S(1)}, bf16[1024,1024]{1,0:T(8,128)(2,1)}, u32[]{:S(2)}) copy-start(bf16[1024,1024]{1,0:T(8,128)(2,1)} %param.28) | copy-start | bytes 6291460
  107.2 22.5 %copy-start.5 = (f32[1024]{0:T(1024)S(1)}, f32[1024]{0:T(1024)}, u32[]{:S(2)}) copy-start(f32[1024]{0:T(1024)} %param.29) | copy-start | bytes 12292
  128.1 3.5 %copy-start.9 = (s32[2]{0:T(128)S(1)}, s32[2]{0:T(128)}, u32[]{:S(2)}) copy-start(s32[2]{0:T(128)} %param.19) | copy-start | bytes 28
  128.1 3.5 %copy-start.8 = (s32[2,16]{1,0:T(2,128)S(1)}, s32[2,16]{1,0:T(2,128)}, u32[]{:S(2)}) copy-start(s32[2,16]{1,0:T(2,128)} %param.33) | copy-start | bytes 388
  128.1 3.5 %copy-start.6 = (f32[1024]{0:T(1024)S(1)}, f32[1024]{0:T(1024)}, u32[]{:S(2)}) copy-start(f32[1024]{0:T(1024)} %param.31) | copy-start | bytes 12292
  128.1 3.5 %copy-start.7 = (f32[1024]{0:T(1024)S(1)}, f32[1024]{0:T(1024)}, u32[]{:S(2)}) copy-start(f32[1024]{0:T(1024)} %param.30) | copy-start | bytes 12292

commit v14 on v13

--- a/solution.py
+++ b/solution.py
@@ -26,7 +26,7 @@
     return me, rq, core, right, left, opp, relay_to, relay_from
 
 
-def _gather_kernel(chunks, x_ref, out_ref, send_sem, recv_sem, local_sem):
+def _gather_kernel(chunks, x_ref, out_ref, send_sem, recv_sem):
     me, rq, core, right, left, opp, relay_to, relay_from = _ring_peers()
     rows = x_ref.shape[1]
     step = rows // chunks
@@ -42,8 +42,6 @@
             src, dst, send, recv, device_id=(rq, peer), device_id_type=MESH_ID
         )
 
-    local = pltpu.make_async_copy(x_ref, out_ref.at[:, pl.ds(me * rows, rows), :], local_sem)
-    local.start()
     sends = []
     for k in range(chunks):
         to_right = copy(part(x_ref, k), slot(me, k), send_sem.at[0, k], recv_sem.at[0, k], right)
@@ -65,13 +63,12 @@
         copy(part(x_ref, k), slot(opp, k), send_sem.at[0, k], recv_sem.at[2, k], right).wait_recv()
     for c in sends:
         c.wait_send()
-    local.wait()
 
 
 def ring_all_gather(x, collective_id, chunks=1):
     texts, rows, width = x.shape
     n = lax.axis_size("tp")
-    return pl.pallas_call(
+    gathered = pl.pallas_call(
         functools.partial(_gather_kernel, chunks),
         out_shape=jax.ShapeDtypeStruct((texts, n * rows, width), x.dtype),
         in_specs=[pl.BlockSpec(memory_space=pl.ANY)],
@@ -79,10 +76,11 @@
         scratch_shapes=[
             pltpu.SemaphoreType.DMA((3, chunks)),
             pltpu.SemaphoreType.DMA((3, chunks)),
-            pltpu.SemaphoreType.DMA,
         ],
         compiler_params=pltpu.CompilerParams(collective_id=collective_id, has_side_effects=True),
     )(x)
+    me = lax.axis_index("tp")
+    return lax.dynamic_update_slice_in_dim(gathered, x, me * rows, 1)
 
 
 def _scatter_add_kernel(chunks, p_ref, recv_ref, send_sem, recv_sem, relay_sem, local_sem,

time: 185 us -> 187 us (1.011)
  local copies, waits for them, and re-layouts: 3.8 us -> 5.68 us
    dynamic_update_slice x0 -> x1, local copies, waits for them, and re-layouts: none -> 1.88 us  [ring_all_gather(): return lax.dynamic_update_slice_in_dim(gathered, x, me * rows, 1)]
where the time goes in v14:
time: 187 us; the launch traced here: 186 us
  Pallas kernels  105 us (56%)
  matrix products  39.7 us (21%)
  other arithmetic  17.1 us (9%)
  blocking collectives  16.9 us (9%)
  local copies, waits for them, and re-layouts  5.68 us (3%)
    pallas_call x2, Pallas kernels, ring_all_gather(): pl.pallas_call(functools.partial(_gather_kernel, chunks), out_shape=jax.S...  43.1 us
    pallas_call x2, Pallas kernels, ring_reduce_scatter_add(): pl.pallas_call(functools.partial(_scatter_add_kernel, chunks), out_shape=...  41 us
    pallas_call x2, Pallas kernels, direct_exchange(): pl.pallas_call(functools.partial(_direct_kernel, axes, scatter), out_shap...  20.9 us
    all_to_all x1, blocking collectives, per_device(): lax.all_to_all(owner_terms, ('req', 'tp'), 0, 0, tiled=True)  16.9 us
    dot_general x1, matrix products, per_device(): jnp.einsum('tsd,df->tsf', normed_full, w_up, preferred_element_type=jnp.f...  12.7 us
    sub x1, matrix products, window_attention(): expo = jnp.exp(logits - top_val)  7.67 us
    dot_general x1, matrix products, few_owned(): jnp.dot(row_pick.astype(index_rows.dtype), index_rows, preferred_element_...  5 us
    dot_general x1, matrix products, window_attention(): jnp.einsum('thqk,tkhe->tqhe', attn_weights, values_h, preferred_element_t...  4.29 us

profile of v14, /device:TPU:1, one launch (start us, length us, event | category | flops | bytes accessed | tf_op | source)
XLA Modules:
  0.0 186.4 jit_solution(8579695682463767099)
XLA Ops:
  2.4 21.9 %shard_map.167 = bf16[2,512,1024]{2,1,0:T(8,128)(2,1)} custom-call(bf16[2,128,1024]{2,1,0:T(8,128)(2,1)} %x_ref.1), custom_call_target="tpu_custom_call" | custom-call | tf_op jit(solution)/shard_map/pallas_call | solution.py:71
  24.3 1.9 %constant_dynamic-update-slice_fusion.1 = bf16[2,512,1024]{2,1,0:T(8,128)(2,1)} fusion(bf16[2,512,1024]{2,1,0:T(8,128)(2,1)} %shard_map.167, bf16[2,128,1024]{2,1,0:T(8,128)(2,1)} %x_ref.1, s32[]{:T(128)S(6)} %select_n.68), kind=kLoop, calls=%fused_computation.97 | loop fusion | bytes 1048580 | tf_op jit(solution)/shard_map/dynamic_update_slice | solution.py:83
  26.2 3.9 %add_convert_fusion = bf16[2,512,3,256]{1,3,2,0:T(8,128)(2,1)S(1)} fusion(f32[3,256]{1,0:T(4,128)} %param.21, bf16[1024,3,256]{2,0,1:T(8,128)(2,1)} %param.20, bf16[2,512,1024]{2,1,0:T(8,128)(2,1)} %constant_dynamic-update-slice_fusion.1), kind=kOutput, calls=%fused_computation.54 | convolution fusion | flops 1612185600 | bytes 5245952 | tf_op jit(solution)/shard_map/tsd,dce->tsce/dot_general | solution.py:308
  30.1 1.2 fusion.48
  31.6 7.7 %fusion.49 = (f32[2,4,512]{2,1,0:T(4,128)S(1)}, f32[2,4,512,512]{2,3,1,0:T(8,128)}) fusion(pred[2,512,512]{1,2,0:T(8,128)(4,1)S(1)} %broadcast_and_fusion, bf16[2,512,4,64]{1,3,2,0:T(8,128)(2,1)} %bitcast.56, bf16[2,512,4,64]{1,3,2,0:T(8,128)(2,1)} %bitcast.55), kind=kOutput, calls=%fused_computation.108 | convolution fusion | flops 276824576 | bytes 9977856 | tf_op jit(solution)/shard_map/sub | solution.py:265
  39.3 4.3 %fusion.37 = bf16[2,4,64,512]{3,2,1,0:T(8,128)(2,1)S(1)} fusion(bf16[2,512,4,64]{1,3,2,0:T(8,128)(2,1)S(1)} %bitcast.54, f32[2,4,512,512]{2,3,1,0:T(8,128)} %get-tuple-element.56, f32[2,4,512]{2,1,0:T(4,128)S(1)} %get-tuple-element.55, pred[2,512]{1,0:T(4,128)(4,1)S(1)} %iota_compare_fusion.5), kind=kOutput, calls=%fused_computation.67 | convolution fusion | flops 273154048 | bytes 9454592 | tf_op jit(solution)/shard_map/thqk,tkhe->tqhe/dot_general | solution.py:267
  43.6 2.1 %convolution_convert_fusion.p_ref = bf16[2,512,1024]{2,1,0:T(8,128)(2,1)} fusion(bf16[2,512,256]{1,2,0:T(8,128)(2,1)S(1)} %bitcast.57, bf16[256,1024]{1,0:T(8,128)(2,1)S(1)} %copy-done.1), kind=kOutput, calls=%fused_computation.64 | convolution fusion | flops 537919488 | bytes 3145728 | tf_op jit(solution)/shard_map/tsk,kd->tsd/dot_general | solution.py:315
  45.7 20.2 %shard_map.168 = bf16[2,2,128,1024]{3,2,1,0:T(8,128)(2,1)} custom-call(bf16[2,512,1024]{2,1,0:T(8,128)(2,1)} %convolution_convert_fusion.p_ref), custom_call_target="tpu_custom_call" | custom-call | tf_op jit(solution)/shard_map/pallas_call | solution.py:139
  65.9 1.6 convert_reduce_fusion.1
  67.4 1.5 fusion.47
  70.3 21.2 %shard_map.169 = bf16[2,512,1024]{2,1,0:T(8,128)(2,1)} custom-call(bf16[2,128,1024]{2,1,0:T(8,128)(2,1)} %add_convert_fusion.2.x_ref), custom_call_target="tpu_custom_call" | custom-call | tf_op jit(solution)/shard_map/pallas_call | solution.py:71
  91.5 1.1 constant_dynamic-update-slice_fusion
  92.6 12.7 %fusion.8 = bf16[2,512,1024]{2,1,0:T(8,128)(2,1)S(1)} fusion(f32[1024]{0:T(1024)S(1)} %copy-done.11, bf16[2,512,1024]{2,1,0:T(8,128)(2,1)} %constant_dynamic-update-slice_fusion, bf16[1024,1024]{1,0:T(8,128)(2,1)S(1)} %copy-done), kind=kOutput, calls=%fused_computation.34 | convolution fusion | flops 2216689664 | bytes 6295552 | tf_op jit(solution)/shard_map/tsd,df->tsf/dot_general | solution.py:326
  105.3 3.7 %fusion.26.p_ref = bf16[2,512,1024]{2,1,0:T(8,128)(2,1)} fusion(bf16[2,512,1024]{2,1,0:T(8,128)(2,1)S(1)} %fusion.8, bf16[1024,1024]{1,0:T(8,128)(2,1)S(1)} %copy-done.10), kind=kOutput, calls=%fused_computation.63 | convolution fusion | flops 2148532224 | bytes 6291456 | tf_op jit(solution)/shard_map/tsf,fd->tsd/dot_general | solution.py:330
  109.0 20.9 %shard_map.170 = bf16[2,2,128,1024]{3,2,1,0:T(8,128)(2,1)} custom-call(bf16[2,512,1024]{2,1,0:T(8,128)(2,1)} %fusion.26.p_ref), custom_call_target="tpu_custom_call" | custom-call | tf_op jit(solution)/shard_map/pallas_call | solution.py:139
  129.9 1.6 convert_reduce_fusion
  131.5 1.5 fusion.46
  133.3 1.2 select_reduce_fusion.4
  135.1 6.0 %shard_map.171 = f32[4,2,1040]{2,1,0:T(2,128)} custom-call(f32[2,1040]{1,0:T(2,128)} %pad_maximum_fusion.x_ref), custom_call_target="tpu_custom_call" | custom-call | tf_op jit(solution)/shard_map/pallas_call | solution.py:222
  143.6 14.9 %shard_map.172 = f32[32,2,1088]{2,1,0:T(2,128)} custom-call(f32[2,1088]{1,0:T(2,128)} %pad_maximum_fusion.1.x_ref), custom_call_target="tpu_custom_call" | custom-call | tf_op jit(solution)/shard_map/pallas_call | solution.py:222
  158.5 1.2 reshape.241
  161.0 7.5 %conditional.1 = (f32[64,64]{1,0:T(8,128)S(1)}) conditional(s32[]{:T(128)} %convert_element_type.97, (s32[64,64]{1,0:T(8,128)S(1)}, bf16[4096,1024]{1,0:T(8,128)(2,1)}, bf16[64,1024]{1,0:T(8,128)(2,1)S(1)}, pred[64,64]{1,0:T(8,128)(4,1)S(1)}) %tuple.14, (pred[64,64]{1,0:T(8,128)(4,1)S(1)}, s32[64,64]{1,0:T(8,128)S(1)}, ...), branch_computations={%region_12.14_spmd, %region_14.21_spmd} | conditional | flops 548545344 | bytes 12955656 | solution.py:401
  162.7 5.0 %fusion.1 = f32[64,1024]{1,0:T(8,128)S(1)} fusion(bf16[4096,1024]{1,0:T(8,128)(2,1)} %get-tuple-element.25, s32[64]{0:T(128)S(1)} %get-tuple-element.38), kind=kOutput, calls=%fused_computation.14 | convolution fusion | flops 537133056 | bytes 8651008 | tf_op jit(solution)/shard_map/cond/branch_1_fun/dot_general | solution.py:380
  168.7 16.9 %all_to_all.5 = f32[128,2,16]{2,1,0:T(2,128)S(1)} all-to-all(f32[128,2,16]{2,1,0:T(2,128)S(1)} %copy.46), channel_id=1, replica_groups=mesh['req'=32,'tp'=4] {'req','tp'}, dimensions={0} | all-to-all | bytes 32768 | tf_op jit(solution)/shard_map/all_to_all | solution.py:407
  (68 shorter events, 10.5 us)
Async XLA Ops:
  0.6 91.9 %copy-start = (bf16[1024,1024]{1,0:T(8,128)(2,1)S(1)}, bf16[1024,1024]{1,0:T(8,128)(2,1)}, u32[]{:S(2)}) copy-start(bf16[1024,1024]{1,0:T(8,128)(2,1)} %param.26) | copy-start | bytes 6291460
  39.3 4.3 %copy-start.1 = (bf16[256,1024]{1,0:T(8,128)(2,1)S(1)}, bf16[256,1024]{1,0:T(8,128)(2,1)}, u32[]{:S(2)}) copy-start(bf16[256,1024]{1,0:T(8,128)(2,1)} %param.22) | copy-start | bytes 1572868
  43.6 23.9 %copy-start.4 = (f32[1024]{0:T(1024)S(1)}, f32[1024]{0:T(1024)}, u32[]{:S(2)}) copy-start(f32[1024]{0:T(1024)} %param.23) | copy-start | bytes 12292
  45.7 23.6 %copy-start.2 = (f32[1024]{0:T(1024)S(1)}, f32[1024]{0:T(1024)}, u32[]{:S(2)}) copy-start(f32[1024]{0:T(1024)} %param.25) | copy-start | bytes 12292
  45.7 23.6 %copy-start.3 = (f32[1024]{0:T(1024)S(1)}, f32[1024]{0:T(1024)}, u32[]{:S(2)}) copy-start(f32[1024]{0:T(1024)} %param.24) | copy-start | bytes 12292
  69.0 23.6 %copy-start.11 = (f32[1024]{0:T(1024)S(1)}, f32[1024]{0:T(1024)}, u32[]{:S(2)}) copy-start(f32[1024]{0:T(1024)} %param.27) | copy-start | bytes 12292
  92.5 12.7 %copy-start.10 = (bf16[1024,1024]{1,0:T(8,128)(2,1)S(1)}, bf16[1024,1024]{1,0:T(8,128)(2,1)}, u32[]{:S(2)}) copy-start(bf16[1024,1024]{1,0:T(8,128)(2,1)} %param.28) | copy-start | bytes 6291460
  109.0 22.5 %copy-start.5 = (f32[1024]{0:T(1024)S(1)}, f32[1024]{0:T(1024)}, u32[]{:S(2)}) copy-start(f32[1024]{0:T(1024)} %param.29) | copy-start | bytes 12292
  129.9 3.5 %copy-start.8 = (s32[2,16]{1,0:T(2,128)S(1)}, s32[2,16]{1,0:T(2,128)}, u32[]{:S(2)}) copy-start(s32[2,16]{1,0:T(2,128)} %param.33) | copy-start | bytes 388
  129.9 3.5 %copy-start.6 = (f32[1024]{0:T(1024)S(1)}, f32[1024]{0:T(1024)}, u32[]{:S(2)}) copy-start(f32[1024]{0:T(1024)} %param.31) | copy-start | bytes 12292
  129.9 3.5 %copy-start.7 = (f32[1024]{0:T(1024)S(1)}, f32[1024]{0:T(1024)}, u32[]{:S(2)}) copy-start(f32[1024]{0:T(1024)} %param.30) | copy-start | bytes 12292
  129.9 12.7 %copy-start.9 = (s32[2]{0:T(128)S(1)}, s32[2]{0:T(128)}, u32[]{:S(2)}) copy-start(s32[2]{0:T(128)} %param.19) | copy-start | bytes 28

commit v15 on v13

--- a/solution.py
+++ b/solution.py
@@ -235,9 +235,42 @@
     )(x)
 
 
+def _row_pick_kernel(ids_ref, rows_hbm, out_hbm, sem):
+    count = ids_ref.shape[0]
+
+    def start(k, carry):
+        first = pl.multiple_of((ids_ref[k] // ROW_GROUP) * ROW_GROUP, ROW_GROUP)
+        pltpu.make_async_copy(
+            rows_hbm.at[pl.ds(first, ROW_GROUP)],
+            out_hbm.at[pl.ds(pl.multiple_of(k * ROW_GROUP, ROW_GROUP), ROW_GROUP)],
+            sem,
+        ).start()
+        return carry
+
+    lax.fori_loop(0, count, start, 0)
+    pltpu.make_async_copy(rows_hbm.at[pl.ds(0, count * ROW_GROUP)], out_hbm, sem).wait()
+
+
+def pick_rows(rows, ids):
+    groups = pl.pallas_call(
+        _row_pick_kernel,
+        out_shape=jax.ShapeDtypeStruct((ids.shape[0] * ROW_GROUP, rows.shape[1]), rows.dtype),
+        grid_spec=pltpu.PrefetchScalarGridSpec(
+            num_scalar_prefetch=1,
+            grid=(1,),
+            in_specs=[pl.BlockSpec(memory_space=pl.ANY)],
+            out_specs=pl.BlockSpec(memory_space=pl.ANY),
+            scratch_shapes=[pltpu.SemaphoreType.DMA],
+        ),
+    )(ids, rows).reshape(ids.shape[0], ROW_GROUP, rows.shape[1])
+    within = jnp.arange(ROW_GROUP, dtype=jnp.int32)[None, :, None] == (ids % ROW_GROUP)[:, None, None]
+    return jnp.sum(jnp.where(within, groups.astype(jnp.float32), jnp.float32(0.0)), axis=1)
+
+
 HEAD_DIM = 64
 RING_CHUNKS = 4
 SPARSE_PAIRS = 64
+ROW_GROUP = 8
 WINDOW = 512
 
 
@@ -378,8 +411,7 @@
         pair_index = jnp.arange(flat_owned.shape[0], dtype=jnp.int32)
         pair_at = jnp.sum(jnp.where(chosen, pair_index[None, :], 0), axis=1)
         row_of = jnp.sum(jnp.where(chosen, safe_ids.reshape(-1)[None, :], 0), axis=1)
-        row_pick = jnp.arange(rows_here, dtype=jnp.int32)[None, :] == row_of[:, None]
-        rows = jnp.dot(row_pick.astype(index_rows.dtype), index_rows, preferred_element_type=jnp.float32)
+        rows = pick_rows(index_rows, jnp.clip(row_of, 0, rows_here - 1))
         text_of = pair_at // all_ids.shape[1]
         text_pick = jnp.arange(all_queries.shape[0], dtype=jnp.int32)[None, :] == text_of[:, None]
         queries = jnp.dot(

time: 185 us -> 216 us (1.17)
  Pallas kernels: 105 us -> 139 us
  matrix products: 39.7 us -> 34.7 us
  other arithmetic: 17.3 us -> 19.9 us
    pallas_call x0 -> x1, Pallas kernels: none -> 33.5 us  [pick_rows(): pl.pallas_call(_row_pick_kernel, out_shape=jax.ShapeDtypeStruct((ids.shap...]
    dot_general x1 -> x0, matrix products: 5 us -> none  [few_owned(): jnp.dot(row_pick.astype(index_rows.dtype), index_rows, preferred_element_...]
where the time goes in v15:
time: 216 us
  Pallas kernels  139 us (64%)
  matrix products  34.7 us (16%)
  other arithmetic  19.9 us (9%)
  blocking collectives  16.9 us (8%)
  local copies, waits for them, and re-layouts  3.8 us (2%)
    pallas_call x2, Pallas kernels, ring_all_gather(): pl.pallas_call(functools.partial(_gather_kernel, chunks), out_shape=jax.S...  43.1 us
    pallas_call x2, Pallas kernels, ring_reduce_scatter_add(): pl.pallas_call(functools.partial(_scatter_add_kernel, chunks), out_shape=...  41 us
    pallas_call x1, Pallas kernels, pick_rows(): pl.pallas_call(_row_pick_kernel, out_shape=jax.ShapeDtypeStruct((ids.shap...  33.5 us
    pallas_call x2, Pallas kernels, direct_exchange(): pl.pallas_call(functools.partial(_direct_kernel, axes, scatter), out_shap...  20.9 us
    all_to_all x1, blocking collectives, per_device(): lax.all_to_all(owner_terms, ('req', 'tp'), 0, 0, tiled=True)  16.9 us
    dot_general x1, matrix products, per_device(): jnp.einsum('tsd,df->tsf', normed_full, w_up, preferred_element_type=jnp.f...  12.7 us
    sub x1, matrix products, window_attention(): expo = jnp.exp(logits - top_val)  7.66 us

profile of v15, /device:TPU:1, one launch (start us, length us, event | category | flops | bytes accessed | tf_op | source)
XLA Modules:
  0.0 215.8 jit_solution(10822311261944315819)
XLA Ops:
  2.3 21.9 %shard_map.167 = bf16[2,512,1024]{2,1,0:T(8,128)(2,1)} custom-call(bf16[2,128,1024]{2,1,0:T(8,128)(2,1)} %x_ref.1), custom_call_target="tpu_custom_call" | custom-call | tf_op jit(solution)/shard_map/pallas_call | solution.py:74
  24.3 3.9 %add_convert_fusion = bf16[2,512,3,256]{1,3,2,0:T(8,128)(2,1)S(1)} fusion(f32[3,256]{1,0:T(4,128)} %param.21, bf16[1024,3,256]{2,0,1:T(8,128)(2,1)} %param.20, bf16[2,512,1024]{2,1,0:T(8,128)(2,1)} %shard_map.167), kind=kOutput, calls=%fused_computation.59 | convolution fusion | flops 1612185600 | bytes 5245952 | tf_op jit(solution)/shard_map/tsd,dce->tsce/dot_general | solution.py:343
  28.2 1.2 fusion.48
  29.7 7.7 %fusion.49 = (f32[2,4,512]{2,1,0:T(4,128)S(1)}, f32[2,4,512,512]{2,3,1,0:T(8,128)}) fusion(pred[2,512,512]{1,2,0:T(8,128)(4,1)S(1)} %broadcast_and_fusion, bf16[2,512,4,64]{1,3,2,0:T(8,128)(2,1)} %bitcast.58, bf16[2,512,4,64]{1,3,2,0:T(8,128)(2,1)} %bitcast.57), kind=kOutput, calls=%fused_computation.111 | convolution fusion | flops 276824576 | bytes 9977856 | tf_op jit(solution)/shard_map/sub | solution.py:300
  37.3 4.3 %fusion.37 = bf16[2,4,64,512]{3,2,1,0:T(8,128)(2,1)S(1)} fusion(bf16[2,512,4,64]{1,3,2,0:T(8,128)(2,1)S(1)} %bitcast.56, f32[2,4,512,512]{2,3,1,0:T(8,128)} %get-tuple-element.59, f32[2,4,512]{2,1,0:T(4,128)S(1)} %get-tuple-element.58, pred[2,512]{1,0:T(4,128)(4,1)S(1)} %iota_compare_fusion.4), kind=kOutput, calls=%fused_computation.72 | convolution fusion | flops 273154048 | bytes 9454592 | tf_op jit(solution)/shard_map/thqk,tkhe->tqhe/dot_general | solution.py:302
  41.6 2.1 convolution_convert_fusion.p_ref
  43.7 20.2 %shard_map.168 = bf16[2,2,128,1024]{3,2,1,0:T(8,128)(2,1)} custom-call(bf16[2,512,1024]{2,1,0:T(8,128)(2,1)} %convolution_convert_fusion.p_ref), custom_call_target="tpu_custom_call" | custom-call | tf_op jit(solution)/shard_map/pallas_call | solution.py:141
  63.9 2.5 %convert_reduce_fusion.1 = f32[2,128,1024]{2,1,0:T(8,128)} fusion(bf16[2,2,128,1024]{3,2,1,0:T(8,128)(2,1)} %shard_map.168), kind=kLoop, calls=%fused_computation.67 | loop fusion | flops 786432 | bytes 2097152 | tf_op jit(solution)/shard_map/reduce_sum | solution.py:355
  66.4 1.8 fusion.47
  68.5 1.0 add_convert_fusion.2.x_ref
  69.6 21.2 %shard_map.169 = bf16[2,512,1024]{2,1,0:T(8,128)(2,1)} custom-call(bf16[2,128,1024]{2,1,0:T(8,128)(2,1)} %add_convert_fusion.2.x_ref), custom_call_target="tpu_custom_call" | custom-call | tf_op jit(solution)/shard_map/pallas_call | solution.py:74
  90.8 12.7 %fusion.8 = bf16[2,512,1024]{2,1,0:T(8,128)(2,1)S(1)} fusion(f32[1024]{0:T(1024)S(1)} %copy-done.11, bf16[2,512,1024]{2,1,0:T(8,128)(2,1)} %shard_map.169, bf16[1024,1024]{1,0:T(8,128)(2,1)S(1)} %copy-done), kind=kOutput, calls=%fused_computation.39 | convolution fusion | flops 2216689664 | bytes 6295552 | tf_op jit(solution)/shard_map/tsd,df->tsf/dot_general | solution.py:361
  103.5 3.7 %fusion.26.p_ref = bf16[2,512,1024]{2,1,0:T(8,128)(2,1)} fusion(bf16[2,512,1024]{2,1,0:T(8,128)(2,1)S(1)} %fusion.8, bf16[1024,1024]{1,0:T(8,128)(2,1)S(1)} %copy-done.10), kind=kOutput, calls=%fused_computation.68 | convolution fusion | flops 2148532224 | bytes 6291456 | tf_op jit(solution)/shard_map/tsf,fd->tsd/dot_general | solution.py:365
  107.2 20.9 %shard_map.170 = bf16[2,2,128,1024]{3,2,1,0:T(8,128)(2,1)} custom-call(bf16[2,512,1024]{2,1,0:T(8,128)(2,1)} %fusion.26.p_ref), custom_call_target="tpu_custom_call" | custom-call | tf_op jit(solution)/shard_map/pallas_call | solution.py:141
  128.2 1.6 convert_reduce_fusion
  129.7 1.5 fusion.46
  131.7 1.2 select_reduce_fusion.4
  133.4 6.0 %shard_map.171 = f32[4,2,1040]{2,1,0:T(2,128)} custom-call(f32[2,1040]{1,0:T(2,128)} %pad_maximum_fusion.x_ref), custom_call_target="tpu_custom_call" | custom-call | tf_op jit(solution)/shard_map/pallas_call | solution.py:224
  141.9 14.9 %shard_map.172 = f32[32,2,1088]{2,1,0:T(2,128)} custom-call(f32[2,1088]{1,0:T(2,128)} %pad_maximum_fusion.1.x_ref), custom_call_target="tpu_custom_call" | custom-call | tf_op jit(solution)/shard_map/pallas_call | solution.py:224
  156.8 1.2 reshape.281
  159.3 38.7 %conditional.1 = (f32[64,64]{1,0:T(8,128)S(1)}) conditional(s32[]{:T(128)} %convert_element_type.102, (s32[64,64]{1,0:T(8,128)S(1)}, bf16[4096,1024]{1,0:T(8,128)(2,1)}, bf16[64,1024]{1,0:T(8,128)(2,1)S(1)}, pred[64,64]{1,0:T(8,128)(4,1)S(1)}) %tuple.14, (pred[64,64]{1,0:T(8,128)(4,1)S(1)}, s32[64,64]{1,0:T(8,128)S(1)}, ...), branch_computations={%region_12.14_spmd, %region_14.22_spmd} | conditional | flops 537702400 | bytes 12955656 | solution.py:435
  161.6 33.5 %branch_1_fun.1 = bf16[512,1024]{1,0:T(8,128)(2,1)} custom-call(s32[64]{0:T(128)} %get-tuple-element.52.ids_ref, bf16[4096,1024]{1,0:T(8,128)(2,1)} %get-tuple-element.25.rows_hbm), custom_call_target="tpu_custom_call" | custom-call | tf_op jit(solution)/shard_map/cond/branch_1_fun/pallas_call | solution.py:255
  195.2 2.0 fusion
  198.2 16.9 %all_to_all.5 = f32[128,2,16]{2,1,0:T(2,128)S(1)} all-to-all(f32[128,2,16]{2,1,0:T(2,128)S(1)} %copy.46), channel_id=1, replica_groups=mesh['req'=32,'tp'=4] {'req','tp'}, dimensions={0} | all-to-all | bytes 32768 | tf_op jit(solution)/shard_map/all_to_all | solution.py:441
  (68 shorter events, 10.1 us)
Async XLA Ops:
  0.6 90.1 %copy-start = (bf16[1024,1024]{1,0:T(8,128)(2,1)S(1)}, bf16[1024,1024]{1,0:T(8,128)(2,1)}, u32[]{:S(2)}) copy-start(bf16[1024,1024]{1,0:T(8,128)(2,1)} %param.26) | copy-start | bytes 6291460
  37.3 4.3 %copy-start.1 = (bf16[256,1024]{1,0:T(8,128)(2,1)S(1)}, bf16[256,1024]{1,0:T(8,128)(2,1)}, u32[]{:S(2)}) copy-start(bf16[256,1024]{1,0:T(8,128)(2,1)} %param.22) | copy-start | bytes 1572868
  41.6 24.8 %copy-start.4 = (f32[1024]{0:T(1024)S(1)}, f32[1024]{0:T(1024)}, u32[]{:S(2)}) copy-start(f32[1024]{0:T(1024)} %param.23) | copy-start | bytes 12292
  43.7 24.8 %copy-start.2 = (f32[1024]{0:T(1024)S(1)}, f32[1024]{0:T(1024)}, u32[]{:S(2)}) copy-start(f32[1024]{0:T(1024)} %param.25) | copy-start | bytes 12292
  43.7 24.8 %copy-start.3 = (f32[1024]{0:T(1024)S(1)}, f32[1024]{0:T(1024)}, u32[]{:S(2)}) copy-start(f32[1024]{0:T(1024)} %param.24) | copy-start | bytes 12292
  66.4 24.4 %copy-start.11 = (f32[1024]{0:T(1024)S(1)}, f32[1024]{0:T(1024)}, u32[]{:S(2)}) copy-start(f32[1024]{0:T(1024)} %param.27) | copy-start | bytes 12292
  90.8 12.7 %copy-start.10 = (bf16[1024,1024]{1,0:T(8,128)(2,1)S(1)}, bf16[1024,1024]{1,0:T(8,128)(2,1)}, u32[]{:S(2)}) copy-start(bf16[1024,1024]{1,0:T(8,128)(2,1)} %param.28) | copy-start | bytes 6291460
  107.2 22.5 %copy-start.5 = (f32[1024]{0:T(1024)S(1)}, f32[1024]{0:T(1024)}, u32[]{:S(2)}) copy-start(f32[1024]{0:T(1024)} %param.29) | copy-start | bytes 12292
  128.1 3.5 %copy-start.9 = (s32[2]{0:T(128)S(1)}, s32[2]{0:T(128)}, u32[]{:S(2)}) copy-start(s32[2]{0:T(128)} %param.19) | copy-start | bytes 28
  128.1 3.5 %copy-start.8 = (s32[2,16]{1,0:T(2,128)S(1)}, s32[2,16]{1,0:T(2,128)}, u32[]{:S(2)}) copy-start(s32[2,16]{1,0:T(2,128)} %param.33) | copy-start | bytes 388
  128.1 3.5 %copy-start.6 = (f32[1024]{0:T(1024)S(1)}, f32[1024]{0:T(1024)}, u32[]{:S(2)}) copy-start(f32[1024]{0:T(1024)} %param.31) | copy-start | bytes 12292
  128.1 3.5 %copy-start.7 = (f32[1024]{0:T(1024)S(1)}, f32[1024]{0:T(1024)}, u32[]{:S(2)}) copy-start(f32[1024]{0:T(1024)} %param.30) | copy-start | bytes 12292

commit v16 on v15

--- a/solution.py
+++ b/solution.py
@@ -259,7 +259,7 @@
             num_scalar_prefetch=1,
             grid=(1,),
             in_specs=[pl.BlockSpec(memory_space=pl.ANY)],
-            out_specs=pl.BlockSpec(memory_space=pl.ANY),
+            out_specs=pl.BlockSpec((ids.shape[0] * ROW_GROUP, rows.shape[1]), lambda i, ids_ref: (0, 0)),
             scratch_shapes=[pltpu.SemaphoreType.DMA],
         ),
     )(ids, rows).reshape(ids.shape[0], ROW_GROUP, rows.shape[1])
@@ -270,7 +270,7 @@
 HEAD_DIM = 64
 RING_CHUNKS = 4
 SPARSE_PAIRS = 64
-ROW_GROUP = 8
+ROW_GROUP = 16
 WINDOW = 512
 
 

time: 216 us -> 188 us (0.87)
  Pallas kernels: 139 us -> 109 us
    pallas_call x1, Pallas kernels: 33.5 us -> 4.39 us  [pick_rows(): pl.pallas_call(_row_pick_kernel, out_shape=jax.ShapeDtypeStruct((ids.shap...]
where the time goes in v16:
time: 188 us; the launch traced here: 187 us
  Pallas kernels  109 us (58%)
  matrix products  34.7 us (18%)
  other arithmetic  20.6 us (11%)
  blocking collectives  17 us (9%)
  local copies, waits for them, and re-layouts  3.8 us (2%)
    pallas_call x2, Pallas kernels, ring_all_gather(): pl.pallas_call(functools.partial(_gather_kernel, chunks), out_shape=jax.S...  43.1 us
    pallas_call x2, Pallas kernels, ring_reduce_scatter_add(): pl.pallas_call(functools.partial(_scatter_add_kernel, chunks), out_shape=...  41 us
    pallas_call x2, Pallas kernels, direct_exchange(): pl.pallas_call(functools.partial(_direct_kernel, axes, scatter), out_shap...  20.9 us
    all_to_all x1, blocking collectives, per_device(): lax.all_to_all(owner_terms, ('req', 'tp'), 0, 0, tiled=True)  17 us
    dot_general x1, matrix products, per_device(): jnp.einsum('tsd,df->tsf', normed_full, w_up, preferred_element_type=jnp.f...  12.7 us
    sub x1, matrix products, window_attention(): expo = jnp.exp(logits - top_val)  7.66 us
    pallas_call x1, Pallas kernels, pick_rows(): pl.pallas_call(_row_pick_kernel, out_shape=jax.ShapeDtypeStruct((ids.shap...  4.39 us
    dot_general x1, matrix products, window_attention(): jnp.einsum('thqk,tkhe->tqhe', attn_weights, values_h, preferred_element_t...  4.29 us

profile of v16, /device:TPU:1, one launch (start us, length us, event | category | flops | bytes accessed | tf_op | source)
XLA Modules:
  0.0 187.3 jit_solution(1593134837108779740)
XLA Ops:
  2.3 21.9 %shard_map.167 = bf16[2,512,1024]{2,1,0:T(8,128)(2,1)} custom-call(bf16[2,128,1024]{2,1,0:T(8,128)(2,1)} %x_ref.1), custom_call_target="tpu_custom_call" | custom-call | tf_op jit(solution)/shard_map/pallas_call | solution.py:74
  24.3 3.9 %add_convert_fusion = bf16[2,512,3,256]{1,3,2,0:T(8,128)(2,1)S(1)} fusion(f32[3,256]{1,0:T(4,128)} %param.21, bf16[1024,3,256]{2,0,1:T(8,128)(2,1)} %param.20, bf16[2,512,1024]{2,1,0:T(8,128)(2,1)} %shard_map.167), kind=kOutput, calls=%fused_computation.59 | convolution fusion | flops 1612185600 | bytes 5245952 | tf_op jit(solution)/shard_map/tsd,dce->tsce/dot_general | solution.py:343
  28.2 1.2 fusion.48
  29.7 7.7 %fusion.49 = (f32[2,4,512]{2,1,0:T(4,128)S(1)}, f32[2,4,512,512]{2,3,1,0:T(8,128)}) fusion(pred[2,512,512]{1,2,0:T(8,128)(4,1)S(1)} %broadcast_and_fusion, bf16[2,512,4,64]{1,3,2,0:T(8,128)(2,1)} %bitcast.58, bf16[2,512,4,64]{1,3,2,0:T(8,128)(2,1)} %bitcast.57), kind=kOutput, calls=%fused_computation.111 | convolution fusion | flops 276824576 | bytes 9977856 | tf_op jit(solution)/shard_map/sub | solution.py:300
  37.3 4.3 %fusion.37 = bf16[2,4,64,512]{3,2,1,0:T(8,128)(2,1)S(1)} fusion(bf16[2,512,4,64]{1,3,2,0:T(8,128)(2,1)S(1)} %bitcast.56, f32[2,4,512,512]{2,3,1,0:T(8,128)} %get-tuple-element.59, f32[2,4,512]{2,1,0:T(4,128)S(1)} %get-tuple-element.58, pred[2,512]{1,0:T(4,128)(4,1)S(1)} %iota_compare_fusion.4), kind=kOutput, calls=%fused_computation.72 | convolution fusion | flops 273154048 | bytes 9454592 | tf_op jit(solution)/shard_map/thqk,tkhe->tqhe/dot_general | solution.py:302
  41.6 2.1 %convolution_convert_fusion.p_ref = bf16[2,512,1024]{2,1,0:T(8,128)(2,1)} fusion(bf16[2,512,256]{1,2,0:T(8,128)(2,1)S(1)} %bitcast.59, bf16[256,1024]{1,0:T(8,128)(2,1)S(1)} %copy-done.1), kind=kOutput, calls=%fused_computation.69 | convolution fusion | flops 537919488 | bytes 3145728 | tf_op jit(solution)/shard_map/tsk,kd->tsd/dot_general | solution.py:350
  43.7 20.2 %shard_map.168 = bf16[2,2,128,1024]{3,2,1,0:T(8,128)(2,1)} custom-call(bf16[2,512,1024]{2,1,0:T(8,128)(2,1)} %convolution_convert_fusion.p_ref), custom_call_target="tpu_custom_call" | custom-call | tf_op jit(solution)/shard_map/pallas_call | solution.py:141
  63.9 2.5 %convert_reduce_fusion.1 = f32[2,128,1024]{2,1,0:T(8,128)} fusion(bf16[2,2,128,1024]{3,2,1,0:T(8,128)(2,1)} %shard_map.168), kind=kLoop, calls=%fused_computation.67 | loop fusion | flops 786432 | bytes 2097152 | tf_op jit(solution)/shard_map/reduce_sum | solution.py:355
  66.4 1.8 fusion.47
  68.5 1.0 add_convert_fusion.2.x_ref
  69.6 21.2 %shard_map.169 = bf16[2,512,1024]{2,1,0:T(8,128)(2,1)} custom-call(bf16[2,128,1024]{2,1,0:T(8,128)(2,1)} %add_convert_fusion.2.x_ref), custom_call_target="tpu_custom_call" | custom-call | tf_op jit(solution)/shard_map/pallas_call | solution.py:74
  90.8 12.7 %fusion.8 = bf16[2,512,1024]{2,1,0:T(8,128)(2,1)S(1)} fusion(f32[1024]{0:T(1024)S(1)} %copy-done.11, bf16[2,512,1024]{2,1,0:T(8,128)(2,1)} %shard_map.169, bf16[1024,1024]{1,0:T(8,128)(2,1)S(1)} %copy-done), kind=kOutput, calls=%fused_computation.39 | convolution fusion | flops 2216689664 | bytes 6295552 | tf_op jit(solution)/shard_map/tsd,df->tsf/dot_general | solution.py:361
  103.5 3.7 %fusion.26.p_ref = bf16[2,512,1024]{2,1,0:T(8,128)(2,1)} fusion(bf16[2,512,1024]{2,1,0:T(8,128)(2,1)S(1)} %fusion.8, bf16[1024,1024]{1,0:T(8,128)(2,1)S(1)} %copy-done.10), kind=kOutput, calls=%fused_computation.68 | convolution fusion | flops 2148532224 | bytes 6291456 | tf_op jit(solution)/shard_map/tsf,fd->tsd/dot_general | solution.py:365
  107.2 20.9 %shard_map.170 = bf16[2,2,128,1024]{3,2,1,0:T(8,128)(2,1)} custom-call(bf16[2,512,1024]{2,1,0:T(8,128)(2,1)} %fusion.26.p_ref), custom_call_target="tpu_custom_call" | custom-call | tf_op jit(solution)/shard_map/pallas_call | solution.py:141
  128.2 1.6 convert_reduce_fusion
  129.7 1.5 fusion.46
  131.7 1.2 select_reduce_fusion.4
  133.4 6.0 %shard_map.171 = f32[4,2,1040]{2,1,0:T(2,128)} custom-call(f32[2,1040]{1,0:T(2,128)} %pad_maximum_fusion.x_ref), custom_call_target="tpu_custom_call" | custom-call | tf_op jit(solution)/shard_map/pallas_call | solution.py:224
  141.9 14.9 %shard_map.172 = f32[32,2,1088]{2,1,0:T(2,128)} custom-call(f32[2,1088]{1,0:T(2,128)} %pad_maximum_fusion.1.x_ref), custom_call_target="tpu_custom_call" | custom-call | tf_op jit(solution)/shard_map/pallas_call | solution.py:224
  156.8 1.2 reshape.281
  159.3 10.1 %conditional.1 = (f32[64,64]{1,0:T(8,128)S(1)}) conditional(s32[]{:T(128)} %convert_element_type.102, (s32[64,64]{1,0:T(8,128)S(1)}, bf16[4096,1024]{1,0:T(8,128)(2,1)}, bf16[64,1024]{1,0:T(8,128)(2,1)S(1)}, pred[64,64]{1,0:T(8,128)(4,1)S(1)}) %tuple.14, (pred[64,64]{1,0:T(8,128)(4,1)S(1)}, s32[64,64]{1,0:T(8,128)S(1)}, ...), branch_computations={%region_12.14_spmd, %region_14.22_spmd} | conditional | flops 537702400 | bytes 12955656 | solution.py:435
  161.5 4.4 %branch_1_fun.1 = bf16[1024,1024]{1,0:T(8,128)(2,1)} custom-call(s32[64]{0:T(128)} %get-tuple-element.51.ids_ref, bf16[4096,1024]{1,0:T(8,128)(2,1)} %get-tuple-element.25.rows_hbm), custom_call_target="tpu_custom_call" | custom-call | tf_op jit(solution)/shard_map/cond/branch_1_fun/pallas_call | solution.py:255
  166.0 2.6 %fusion = f32[64,1024]{1,0:T(8,128)S(1)} fusion(pred[64,16]{1,0:T(8,128)(4,1)S(1)} %iota_compare_fusion.2, bf16[1024,1024]{1,0:T(8,128)(2,1)} %branch_1_fun.1), kind=kLoop, calls=%fused_computation.9 | loop fusion | flops 3080192 | bytes 2360320 | tf_op jit(solution)/shard_map/cond/branch_1_fun/reduce_sum | solution.py:267
  169.6 17.0 %all_to_all.5 = f32[128,2,16]{2,1,0:T(2,128)S(1)} all-to-all(f32[128,2,16]{2,1,0:T(2,128)S(1)} %copy.46), channel_id=1, replica_groups=mesh['req'=32,'tp'=4] {'req','tp'}, dimensions={0} | all-to-all | bytes 32768 | tf_op jit(solution)/shard_map/all_to_all | solution.py:441
  (68 shorter events, 10.1 us)
Async XLA Ops:
  0.6 90.1 %copy-start = (bf16[1024,1024]{1,0:T(8,128)(2,1)S(1)}, bf16[1024,1024]{1,0:T(8,128)(2,1)}, u32[]{:S(2)}) copy-start(bf16[1024,1024]{1,0:T(8,128)(2,1)} %param.26) | copy-start | bytes 6291460
  37.3 4.3 %copy-start.1 = (bf16[256,1024]{1,0:T(8,128)(2,1)S(1)}, bf16[256,1024]{1,0:T(8,128)(2,1)}, u32[]{:S(2)}) copy-start(bf16[256,1024]{1,0:T(8,128)(2,1)} %param.22) | copy-start | bytes 1572868
  41.6 24.8 %copy-start.4 = (f32[1024]{0:T(1024)S(1)}, f32[1024]{0:T(1024)}, u32[]{:S(2)}) copy-start(f32[1024]{0:T(1024)} %param.23) | copy-start | bytes 12292
  43.7 24.8 %copy-start.2 = (f32[1024]{0:T(1024)S(1)}, f32[1024]{0:T(1024)}, u32[]{:S(2)}) copy-start(f32[1024]{0:T(1024)} %param.25) | copy-start | bytes 12292
  43.7 24.8 %copy-start.3 = (f32[1024]{0:T(1024)S(1)}, f32[1024]{0:T(1024)}, u32[]{:S(2)}) copy-start(f32[1024]{0:T(1024)} %param.24) | copy-start | bytes 12292
  66.4 24.4 %copy-start.11 = (f32[1024]{0:T(1024)S(1)}, f32[1024]{0:T(1024)}, u32[]{:S(2)}) copy-start(f32[1024]{0:T(1024)} %param.27) | copy-start | bytes 12292
  90.8 12.7 %copy-start.10 = (bf16[1024,1024]{1,0:T(8,128)(2,1)S(1)}, bf16[1024,1024]{1,0:T(8,128)(2,1)}, u32[]{:S(2)}) copy-start(bf16[1024,1024]{1,0:T(8,128)(2,1)} %param.28) | copy-start | bytes 6291460
  107.2 22.5 %copy-start.5 = (f32[1024]{0:T(1024)S(1)}, f32[1024]{0:T(1024)}, u32[]{:S(2)}) copy-start(f32[1024]{0:T(1024)} %param.29) | copy-start | bytes 12292
  128.1 3.5 %copy-start.9 = (s32[2]{0:T(128)S(1)}, s32[2]{0:T(128)}, u32[]{:S(2)}) copy-start(s32[2]{0:T(128)} %param.19) | copy-start | bytes 28
  128.1 3.5 %copy-start.8 = (s32[2,16]{1,0:T(2,128)S(1)}, s32[2,16]{1,0:T(2,128)}, u32[]{:S(2)}) copy-start(s32[2,16]{1,0:T(2,128)} %param.33) | copy-start | bytes 388
  128.1 3.5 %copy-start.6 = (f32[1024]{0:T(1024)S(1)}, f32[1024]{0:T(1024)}, u32[]{:S(2)}) copy-start(f32[1024]{0:T(1024)} %param.31) | copy-start | bytes 12292
  128.1 3.5 %copy-start.7 = (f32[1024]{0:T(1024)S(1)}, f32[1024]{0:T(1024)}, u32[]{:S(2)}) copy-start(f32[1024]{0:T(1024)} %param.30) | copy-start | bytes 12292

commit v17 on v13

--- a/solution.py
+++ b/solution.py
@@ -236,7 +236,7 @@
 
 
 HEAD_DIM = 64
-RING_CHUNKS = 4
+RING_CHUNKS = 2
 SPARSE_PAIRS = 64
 WINDOW = 512
 

time: 185 us -> 185 us (level)
  no operation moved by 1% of the time
where the time goes in v17:
time: 185 us; the launch traced here: 184 us
  Pallas kernels  105 us (57%)
  matrix products  39.7 us (21%)
  other arithmetic  17.3 us (9%)
  blocking collectives  17.1 us (9%)
  local copies, waits for them, and re-layouts  3.8 us (2%)
    pallas_call x2, Pallas kernels, ring_all_gather(): pl.pallas_call(functools.partial(_gather_kernel, chunks), out_shape=jax.S...  43.1 us
    pallas_call x2, Pallas kernels, ring_reduce_scatter_add(): pl.pallas_call(functools.partial(_scatter_add_kernel, chunks), out_shape=...  41.3 us
    pallas_call x2, Pallas kernels, direct_exchange(): pl.pallas_call(functools.partial(_direct_kernel, axes, scatter), out_shap...  20.1 us
    all_to_all x1, blocking collectives, per_device(): lax.all_to_all(owner_terms, ('req', 'tp'), 0, 0, tiled=True)  17.1 us
    dot_general x1, matrix products, per_device(): jnp.einsum('tsd,df->tsf', normed_full, w_up, preferred_element_type=jnp.f...  12.7 us
    sub x1, matrix products, window_attention(): expo = jnp.exp(logits - top_val)  7.66 us
    dot_general x1, matrix products, few_owned(): jnp.dot(row_pick.astype(index_rows.dtype), index_rows, preferred_element_...  5 us
    dot_general x1, matrix products, window_attention(): jnp.einsum('thqk,tkhe->tqhe', attn_weights, values_h, preferred_element_t...  4.29 us

profile of v17, /device:TPU:1, one launch (start us, length us, event | category | flops | bytes accessed | tf_op | source)
XLA Modules:
  0.0 184.3 jit_solution(9036169386843534045)
XLA Ops:
  0.8 0.8 iota_compare_fusion.5
  2.3 21.8 %shard_map.167 = bf16[2,512,1024]{2,1,0:T(8,128)(2,1)} custom-call(bf16[2,128,1024]{2,1,0:T(8,128)(2,1)} %x_ref.1), custom_call_target="tpu_custom_call" | custom-call | tf_op jit(solution)/shard_map/pallas_call | solution.py:74
  24.1 3.9 %add_convert_fusion = bf16[2,512,3,256]{1,3,2,0:T(8,128)(2,1)S(1)} fusion(f32[3,256]{1,0:T(4,128)} %param.21, bf16[1024,3,256]{2,0,1:T(8,128)(2,1)} %param.20, bf16[2,512,1024]{2,1,0:T(8,128)(2,1)} %shard_map.167), kind=kOutput, calls=%fused_computation.54 | convolution fusion | flops 1612185600 | bytes 5245952 | tf_op jit(solution)/shard_map/tsd,dce->tsce/dot_general | solution.py:310
  28.1 1.2 fusion.48
  29.5 7.7 %fusion.49 = (f32[2,4,512]{2,1,0:T(4,128)S(1)}, f32[2,4,512,512]{2,3,1,0:T(8,128)}) fusion(pred[2,512,512]{1,2,0:T(8,128)(4,1)S(1)} %broadcast_and_fusion, bf16[2,512,4,64]{1,3,2,0:T(8,128)(2,1)} %bitcast.56, bf16[2,512,4,64]{1,3,2,0:T(8,128)(2,1)} %bitcast.55), kind=kOutput, calls=%fused_computation.106 | convolution fusion | flops 276824576 | bytes 9977856 | tf_op jit(solution)/shard_map/sub | solution.py:267
  37.2 4.3 %fusion.37 = bf16[2,4,64,512]{3,2,1,0:T(8,128)(2,1)S(1)} fusion(bf16[2,512,4,64]{1,3,2,0:T(8,128)(2,1)S(1)} %bitcast.54, f32[2,4,512,512]{2,3,1,0:T(8,128)} %get-tuple-element.56, f32[2,4,512]{2,1,0:T(4,128)S(1)} %get-tuple-element.55, pred[2,512]{1,0:T(4,128)(4,1)S(1)} %iota_compare_fusion.5), kind=kOutput, calls=%fused_computation.67 | convolution fusion | flops 273154048 | bytes 9454592 | tf_op jit(solution)/shard_map/thqk,tkhe->tqhe/dot_general | solution.py:269
  41.5 2.1 %convolution_convert_fusion.p_ref = bf16[2,512,1024]{2,1,0:T(8,128)(2,1)} fusion(bf16[2,512,256]{1,2,0:T(8,128)(2,1)S(1)} %bitcast.57, bf16[256,1024]{1,0:T(8,128)(2,1)S(1)} %copy-done.1), kind=kOutput, calls=%fused_computation.64 | convolution fusion | flops 537919488 | bytes 3145728 | tf_op jit(solution)/shard_map/tsk,kd->tsd/dot_general | solution.py:317
  43.6 20.0 %shard_map.168 = bf16[2,2,128,1024]{3,2,1,0:T(8,128)(2,1)} custom-call(bf16[2,512,1024]{2,1,0:T(8,128)(2,1)} %convolution_convert_fusion.p_ref), custom_call_target="tpu_custom_call" | custom-call | tf_op jit(solution)/shard_map/pallas_call | solution.py:141
  63.7 2.5 %convert_reduce_fusion.1 = f32[2,128,1024]{2,1,0:T(8,128)} fusion(bf16[2,2,128,1024]{3,2,1,0:T(8,128)(2,1)} %shard_map.168), kind=kLoop, calls=%fused_computation.62 | loop fusion | flops 786432 | bytes 2097152 | tf_op jit(solution)/shard_map/reduce_sum | solution.py:322
  66.2 1.8 fusion.47
  68.3 1.0 add_convert_fusion.2.x_ref
  69.3 21.3 %shard_map.169 = bf16[2,512,1024]{2,1,0:T(8,128)(2,1)} custom-call(bf16[2,128,1024]{2,1,0:T(8,128)(2,1)} %add_convert_fusion.2.x_ref), custom_call_target="tpu_custom_call" | custom-call | tf_op jit(solution)/shard_map/pallas_call | solution.py:74
  90.7 12.7 %fusion.8 = bf16[2,512,1024]{2,1,0:T(8,128)(2,1)S(1)} fusion(f32[1024]{0:T(1024)S(1)} %copy-done.11, bf16[2,512,1024]{2,1,0:T(8,128)(2,1)} %shard_map.169, bf16[1024,1024]{1,0:T(8,128)(2,1)S(1)} %copy-done), kind=kOutput, calls=%fused_computation.34 | convolution fusion | flops 2216689664 | bytes 6295552 | tf_op jit(solution)/shard_map/tsd,df->tsf/dot_general | solution.py:328
  103.4 3.7 %fusion.26.p_ref = bf16[2,512,1024]{2,1,0:T(8,128)(2,1)} fusion(bf16[2,512,1024]{2,1,0:T(8,128)(2,1)S(1)} %fusion.8, bf16[1024,1024]{1,0:T(8,128)(2,1)S(1)} %copy-done.10), kind=kOutput, calls=%fused_computation.63 | convolution fusion | flops 2148532224 | bytes 6291456 | tf_op jit(solution)/shard_map/tsf,fd->tsd/dot_general | solution.py:332
  107.1 21.2 %shard_map.170 = bf16[2,2,128,1024]{3,2,1,0:T(8,128)(2,1)} custom-call(bf16[2,512,1024]{2,1,0:T(8,128)(2,1)} %fusion.26.p_ref), custom_call_target="tpu_custom_call" | custom-call | tf_op jit(solution)/shard_map/pallas_call | solution.py:141
  128.4 1.6 convert_reduce_fusion
  130.0 1.5 fusion.46
  131.9 1.2 select_reduce_fusion.4
  133.7 5.2 %shard_map.171 = f32[4,2,1040]{2,1,0:T(2,128)} custom-call(f32[2,1040]{1,0:T(2,128)} %pad_maximum_fusion.x_ref), custom_call_target="tpu_custom_call" | custom-call | tf_op jit(solution)/shard_map/pallas_call | solution.py:224
  141.4 14.9 %shard_map.172 = f32[32,2,1088]{2,1,0:T(2,128)} custom-call(f32[2,1088]{1,0:T(2,128)} %pad_maximum_fusion.1.x_ref), custom_call_target="tpu_custom_call" | custom-call | tf_op jit(solution)/shard_map/pallas_call | solution.py:224
  156.3 1.2 reshape.241
  158.8 7.5 %conditional.1 = (f32[64,64]{1,0:T(8,128)S(1)}) conditional(s32[]{:T(128)} %convert_element_type.97, (s32[64,64]{1,0:T(8,128)S(1)}, bf16[4096,1024]{1,0:T(8,128)(2,1)}, bf16[64,1024]{1,0:T(8,128)(2,1)S(1)}, pred[64,64]{1,0:T(8,128)(4,1)S(1)}) %tuple.14, (pred[64,64]{1,0:T(8,128)(4,1)S(1)}, s32[64,64]{1,0:T(8,128)S(1)}, ...), branch_computations={%region_12.14_spmd, %region_14.21_spmd} | conditional | flops 548545344 | bytes 12955656 | solution.py:403
  160.5 5.0 %fusion.1 = f32[64,1024]{1,0:T(8,128)S(1)} fusion(bf16[4096,1024]{1,0:T(8,128)(2,1)} %get-tuple-element.25, s32[64]{0:T(128)S(1)} %get-tuple-element.38), kind=kOutput, calls=%fused_computation.14 | convolution fusion | flops 537133056 | bytes 8651008 | tf_op jit(solution)/shard_map/cond/branch_1_fun/dot_general | solution.py:382
  166.5 17.1 %all_to_all.5 = f32[128,2,16]{2,1,0:T(2,128)S(1)} all-to-all(f32[128,2,16]{2,1,0:T(2,128)S(1)} %copy.46), channel_id=1, replica_groups=mesh['req'=32,'tp'=4] {'req','tp'}, dimensions={0} | all-to-all | bytes 32768 | tf_op jit(solution)/shard_map/all_to_all | solution.py:409
  (66 shorter events, 8.6 us)
Async XLA Ops:
  0.6 90.0 %copy-start = (bf16[1024,1024]{1,0:T(8,128)(2,1)S(1)}, bf16[1024,1024]{1,0:T(8,128)(2,1)}, u32[]{:S(2)}) copy-start(bf16[1024,1024]{1,0:T(8,128)(2,1)} %param.26) | copy-start | bytes 6291460
  37.2 4.3 %copy-start.1 = (bf16[256,1024]{1,0:T(8,128)(2,1)S(1)}, bf16[256,1024]{1,0:T(8,128)(2,1)}, u32[]{:S(2)}) copy-start(bf16[256,1024]{1,0:T(8,128)(2,1)} %param.22) | copy-start | bytes 1572868
  41.5 24.7 %copy-start.4 = (f32[1024]{0:T(1024)S(1)}, f32[1024]{0:T(1024)}, u32[]{:S(2)}) copy-start(f32[1024]{0:T(1024)} %param.23) | copy-start | bytes 12292
  43.6 24.7 %copy-start.2 = (f32[1024]{0:T(1024)S(1)}, f32[1024]{0:T(1024)}, u32[]{:S(2)}) copy-start(f32[1024]{0:T(1024)} %param.25) | copy-start | bytes 12292
  43.6 24.7 %copy-start.3 = (f32[1024]{0:T(1024)S(1)}, f32[1024]{0:T(1024)}, u32[]{:S(2)}) copy-start(f32[1024]{0:T(1024)} %param.24) | copy-start | bytes 12292
  66.2 24.5 %copy-start.11 = (f32[1024]{0:T(1024)S(1)}, f32[1024]{0:T(1024)}, u32[]{:S(2)}) copy-start(f32[1024]{0:T(1024)} %param.27) | copy-start | bytes 12292
  90.7 12.7 %copy-start.10 = (bf16[1024,1024]{1,0:T(8,128)(2,1)S(1)}, bf16[1024,1024]{1,0:T(8,128)(2,1)}, u32[]{:S(2)}) copy-start(bf16[1024,1024]{1,0:T(8,128)(2,1)} %param.28) | copy-start | bytes 6291460
  107.1 22.9 %copy-start.5 = (f32[1024]{0:T(1024)S(1)}, f32[1024]{0:T(1024)}, u32[]{:S(2)}) copy-start(f32[1024]{0:T(1024)} %param.29) | copy-start | bytes 12292
  128.4 3.5 %copy-start.9 = (s32[2]{0:T(128)S(1)}, s32[2]{0:T(128)}, u32[]{:S(2)}) copy-start(s32[2]{0:T(128)} %param.19) | copy-start | bytes 28
  128.4 3.5 %copy-start.8 = (s32[2,16]{1,0:T(2,128)S(1)}, s32[2,16]{1,0:T(2,128)}, u32[]{:S(2)}) copy-start(s32[2,16]{1,0:T(2,128)} %param.33) | copy-start | bytes 388
  128.4 3.5 %copy-start.6 = (f32[1024]{0:T(1024)S(1)}, f32[1024]{0:T(1024)}, u32[]{:S(2)}) copy-start(f32[1024]{0:T(1024)} %param.31) | copy-start | bytes 12292
  128.4 3.5 %copy-start.7 = (f32[1024]{0:T(1024)S(1)}, f32[1024]{0:T(1024)}, u32[]{:S(2)}) copy-start(f32[1024]{0:T(1024)} %param.30) | copy-start | bytes 12292

commit v18 on v17

--- a/solution.py
+++ b/solution.py
@@ -165,7 +165,7 @@
     return (peer // n_tp, peer % n_tp)
 
 
-def _direct_kernel(axes, scatter, x_ref, out_ref, send_sem, recv_sem, local_sem):
+def _direct_kernel(axes, scatter, x_ref, out_ref, send_sem, recv_sem):
     n = out_ref.shape[0]
     me = lax.axis_index(axes)
     barrier = pltpu.get_barrier_semaphore()
@@ -180,9 +180,6 @@
 
     def source(peer):
         return x_ref.at[peer] if scatter else x_ref
-
-    local = pltpu.make_async_copy(source(me), out_ref.at[me], local_sem)
-    local.start()
 
     def send(d, carry):
         peer = (me + d) % n
@@ -213,7 +210,6 @@
         return carry
 
     lax.fori_loop(1, n, sent, 0)
-    local.wait()
 
 
 def direct_exchange(x, axes, collective_id, scatter=False):
@@ -221,7 +217,7 @@
     for name in axes:
         n *= lax.axis_size(name)
     block = x.shape[1:] if scatter else x.shape
-    return pl.pallas_call(
+    received = pl.pallas_call(
         functools.partial(_direct_kernel, axes, scatter),
         out_shape=jax.ShapeDtypeStruct((n,) + block, x.dtype),
         in_specs=[pl.BlockSpec(memory_space=pl.ANY)],
@@ -229,10 +225,12 @@
         scratch_shapes=[
             pltpu.SemaphoreType.DMA((n,)),
             pltpu.SemaphoreType.DMA((n,)),
-            pltpu.SemaphoreType.DMA,
         ],
         compiler_params=pltpu.CompilerParams(collective_id=collective_id, has_side_effects=True),
     )(x)
+    own = x[lax.axis_index(axes)] if scatter else x
+    slot = jnp.arange(n, dtype=jnp.int32).reshape((n,) + (1,) * len(block))
+    return jnp.where(slot == lax.axis_index(axes), own[None], received)
 
 
 HEAD_DIM = 64

time: 185 us -> 184 us (level)
    select_n x0 -> x2, other arithmetic: none -> 1.98 us  [direct_exchange(): return jnp.where(slot == lax.axis_index(axes), own[None], received)]
where the time goes in v18:
time: 184 us
  Pallas kernels  104 us (57%)
  matrix products  39.7 us (22%)
  other arithmetic  18.5 us (10%)
  blocking collectives  17.1 us (9%)
  local copies, waits for them, and re-layouts  2.16 us (1%)
    pallas_call x2, Pallas kernels, ring_all_gather(): pl.pallas_call(functools.partial(_gather_kernel, chunks), out_shape=jax.S...  43.1 us
    pallas_call x2, Pallas kernels, ring_reduce_scatter_add(): pl.pallas_call(functools.partial(_scatter_add_kernel, chunks), out_shape=...  41.3 us
    pallas_call x2, Pallas kernels, direct_exchange(): pl.pallas_call(functools.partial(_direct_kernel, axes, scatter), out_shap...  20 us
    all_to_all x1, blocking collectives, per_device(): lax.all_to_all(owner_terms, ('req', 'tp'), 0, 0, tiled=True)  17.1 us
    dot_general x1, matrix products, per_device(): jnp.einsum('tsd,df->tsf', normed_full, w_up, preferred_element_type=jnp.f...  12.7 us
    sub x1, matrix products, window_attention(): expo = jnp.exp(logits - top_val)  7.67 us
    dot_general x1, matrix products, few_owned(): jnp.dot(row_pick.astype(index_rows.dtype), index_rows, preferred_element_...  5 us
    dot_general x1, matrix products, window_attention(): jnp.einsum('thqk,tkhe->tqhe', attn_weights, values_h, preferred_element_t...  4.29 us

profile of v18, /device:TPU:1, one launch (start us, length us, event | category | flops | bytes accessed | tf_op | source)
XLA Modules:
  0.0 183.9 jit_solution(16331159705548324271)
XLA Ops:
  2.4 21.8 %shard_map.167 = bf16[2,512,1024]{2,1,0:T(8,128)(2,1)} custom-call(bf16[2,128,1024]{2,1,0:T(8,128)(2,1)} %x_ref.1), custom_call_target="tpu_custom_call" | custom-call | tf_op jit(solution)/shard_map/pallas_call | solution.py:74
  24.2 3.9 %add_convert_fusion = bf16[2,512,3,256]{1,3,2,0:T(8,128)(2,1)S(1)} fusion(f32[3,256]{1,0:T(4,128)} %param.21, bf16[1024,3,256]{2,0,1:T(8,128)(2,1)} %param.20, bf16[2,512,1024]{2,1,0:T(8,128)(2,1)} %shard_map.167), kind=kOutput, calls=%fused_computation.54 | convolution fusion | flops 1612185600 | bytes 5245952 | tf_op jit(solution)/shard_map/tsd,dce->tsce/dot_general | solution.py:308
  28.2 1.2 fusion.48
  29.6 7.7 %fusion.49 = (f32[2,4,512]{2,1,0:T(4,128)S(1)}, f32[2,4,512,512]{2,3,1,0:T(8,128)}) fusion(pred[2,512,512]{1,2,0:T(8,128)(4,1)S(1)} %broadcast_and_fusion, bf16[2,512,4,64]{1,3,2,0:T(8,128)(2,1)} %bitcast.56, bf16[2,512,4,64]{1,3,2,0:T(8,128)(2,1)} %bitcast.55), kind=kOutput, calls=%fused_computation.110 | convolution fusion | flops 276824576 | bytes 9977856 | tf_op jit(solution)/shard_map/sub | solution.py:265
  37.3 4.3 %fusion.37 = bf16[2,4,64,512]{3,2,1,0:T(8,128)(2,1)S(1)} fusion(bf16[2,512,4,64]{1,3,2,0:T(8,128)(2,1)S(1)} %bitcast.54, f32[2,4,512,512]{2,3,1,0:T(8,128)} %get-tuple-element.56, f32[2,4,512]{2,1,0:T(4,128)S(1)} %get-tuple-element.55, pred[2,512]{1,0:T(4,128)(4,1)S(1)} %iota_compare_fusion.5), kind=kOutput, calls=%fused_computation.67 | convolution fusion | flops 273154048 | bytes 9454592 | tf_op jit(solution)/shard_map/thqk,tkhe->tqhe/dot_general | solution.py:267
  41.6 2.1 %convolution_convert_fusion.p_ref = bf16[2,512,1024]{2,1,0:T(8,128)(2,1)} fusion(bf16[2,512,256]{1,2,0:T(8,128)(2,1)S(1)} %bitcast.57, bf16[256,1024]{1,0:T(8,128)(2,1)S(1)} %copy-done.1), kind=kOutput, calls=%fused_computation.64 | convolution fusion | flops 537919488 | bytes 3145728 | tf_op jit(solution)/shard_map/tsk,kd->tsd/dot_general | solution.py:315
  43.7 20.0 %shard_map.168 = bf16[2,2,128,1024]{3,2,1,0:T(8,128)(2,1)} custom-call(bf16[2,512,1024]{2,1,0:T(8,128)(2,1)} %convolution_convert_fusion.p_ref), custom_call_target="tpu_custom_call" | custom-call | tf_op jit(solution)/shard_map/pallas_call | solution.py:141
  63.8 2.5 %convert_reduce_fusion.1 = f32[2,128,1024]{2,1,0:T(8,128)} fusion(bf16[2,2,128,1024]{3,2,1,0:T(8,128)(2,1)} %shard_map.168), kind=kLoop, calls=%fused_computation.62 | loop fusion | flops 786432 | bytes 2097152 | tf_op jit(solution)/shard_map/reduce_sum | solution.py:320
  66.3 1.8 fusion.47
  68.4 1.0 add_convert_fusion.2.x_ref
  69.4 21.3 %shard_map.169 = bf16[2,512,1024]{2,1,0:T(8,128)(2,1)} custom-call(bf16[2,128,1024]{2,1,0:T(8,128)(2,1)} %add_convert_fusion.2.x_ref), custom_call_target="tpu_custom_call" | custom-call | tf_op jit(solution)/shard_map/pallas_call | solution.py:74
  90.8 12.7 %fusion.8 = bf16[2,512,1024]{2,1,0:T(8,128)(2,1)S(1)} fusion(f32[1024]{0:T(1024)S(1)} %copy-done.11, bf16[2,512,1024]{2,1,0:T(8,128)(2,1)} %shard_map.169, bf16[1024,1024]{1,0:T(8,128)(2,1)S(1)} %copy-done), kind=kOutput, calls=%fused_computation.34 | convolution fusion | flops 2216689664 | bytes 6295552 | tf_op jit(solution)/shard_map/tsd,df->tsf/dot_general | solution.py:326
  103.6 3.7 %fusion.26.p_ref = bf16[2,512,1024]{2,1,0:T(8,128)(2,1)} fusion(bf16[2,512,1024]{2,1,0:T(8,128)(2,1)S(1)} %fusion.8, bf16[1024,1024]{1,0:T(8,128)(2,1)S(1)} %copy-done.10), kind=kOutput, calls=%fused_computation.63 | convolution fusion | flops 2148532224 | bytes 6291456 | tf_op jit(solution)/shard_map/tsf,fd->tsd/dot_general | solution.py:330
  107.3 21.2 %shard_map.170 = bf16[2,2,128,1024]{3,2,1,0:T(8,128)(2,1)} custom-call(bf16[2,512,1024]{2,1,0:T(8,128)(2,1)} %fusion.26.p_ref), custom_call_target="tpu_custom_call" | custom-call | tf_op jit(solution)/shard_map/pallas_call | solution.py:141
  128.5 1.6 convert_reduce_fusion
  130.1 1.5 fusion.46
  132.0 1.2 select_reduce_fusion.4
  133.7 5.2 %shard_map.171 = f32[4,2,1040]{2,1,0:T(2,128)} custom-call(f32[2,1040]{1,0:T(2,128)} %pad_maximum_fusion.x_ref), custom_call_target="tpu_custom_call" | custom-call | tf_op jit(solution)/shard_map/pallas_call | solution.py:220
  138.9 0.9 broadcast_select_fusion.1
  140.9 14.8 %shard_map.172 = f32[32,2,1088]{2,1,0:T(2,128)} custom-call(f32[2,1088]{1,0:T(2,128)} %pad_maximum_fusion.1.x_ref), custom_call_target="tpu_custom_call" | custom-call | tf_op jit(solution)/shard_map/pallas_call | solution.py:220
  155.7 1.1 broadcast_select_fusion
  158.4 7.5 %conditional.1 = (f32[64,64]{1,0:T(8,128)S(1)}) conditional(s32[]{:T(128)} %convert_element_type.97, (s32[64,64]{1,0:T(8,128)S(1)}, bf16[4096,1024]{1,0:T(8,128)(2,1)}, bf16[64,1024]{1,0:T(8,128)(2,1)S(1)}, pred[64,64]{1,0:T(8,128)(4,1)S(1)}) %tuple.14, (pred[64,64]{1,0:T(8,128)(4,1)S(1)}, s32[64,64]{1,0:T(8,128)S(1)}, ...), branch_computations={%region_12.14_spmd, %region_14.21_spmd} | conditional | flops 548545344 | bytes 12955656 | solution.py:401
  160.1 5.0 %fusion.1 = f32[64,1024]{1,0:T(8,128)S(1)} fusion(bf16[4096,1024]{1,0:T(8,128)(2,1)} %get-tuple-element.25, s32[64]{0:T(128)S(1)} %get-tuple-element.38), kind=kOutput, calls=%fused_computation.14 | convolution fusion | flops 537133056 | bytes 8651008 | tf_op jit(solution)/shard_map/cond/branch_1_fun/dot_general | solution.py:380
  166.1 17.1 %all_to_all.5 = f32[128,2,16]{2,1,0:T(2,128)S(1)} all-to-all(f32[128,2,16]{2,1,0:T(2,128)S(1)} %copy.46), channel_id=1, replica_groups=mesh['req'=32,'tp'=4] {'req','tp'}, dimensions={0} | all-to-all | bytes 32768 | tf_op jit(solution)/shard_map/all_to_all | solution.py:407
  (70 shorter events, 8.3 us)
Async XLA Ops:
  0.6 90.2 %copy-start = (bf16[1024,1024]{1,0:T(8,128)(2,1)S(1)}, bf16[1024,1024]{1,0:T(8,128)(2,1)}, u32[]{:S(2)}) copy-start(bf16[1024,1024]{1,0:T(8,128)(2,1)} %param.26) | copy-start | bytes 6291460
  37.3 4.3 %copy-start.1 = (bf16[256,1024]{1,0:T(8,128)(2,1)S(1)}, bf16[256,1024]{1,0:T(8,128)(2,1)}, u32[]{:S(2)}) copy-start(bf16[256,1024]{1,0:T(8,128)(2,1)} %param.22) | copy-start | bytes 1572868
  41.6 24.7 %copy-start.4 = (f32[1024]{0:T(1024)S(1)}, f32[1024]{0:T(1024)}, u32[]{:S(2)}) copy-start(f32[1024]{0:T(1024)} %param.23) | copy-start | bytes 12292
  43.7 24.7 %copy-start.2 = (f32[1024]{0:T(1024)S(1)}, f32[1024]{0:T(1024)}, u32[]{:S(2)}) copy-start(f32[1024]{0:T(1024)} %param.25) | copy-start | bytes 12292
  43.7 24.7 %copy-start.3 = (f32[1024]{0:T(1024)S(1)}, f32[1024]{0:T(1024)}, u32[]{:S(2)}) copy-start(f32[1024]{0:T(1024)} %param.24) | copy-start | bytes 12292
  66.3 24.5 %copy-start.11 = (f32[1024]{0:T(1024)S(1)}, f32[1024]{0:T(1024)}, u32[]{:S(2)}) copy-start(f32[1024]{0:T(1024)} %param.27) | copy-start | bytes 12292
  90.8 12.7 %copy-start.10 = (bf16[1024,1024]{1,0:T(8,128)(2,1)S(1)}, bf16[1024,1024]{1,0:T(8,128)(2,1)}, u32[]{:S(2)}) copy-start(bf16[1024,1024]{1,0:T(8,128)(2,1)} %param.28) | copy-start | bytes 6291460
  107.3 22.9 %copy-start.5 = (f32[1024]{0:T(1024)S(1)}, f32[1024]{0:T(1024)}, u32[]{:S(2)}) copy-start(f32[1024]{0:T(1024)} %param.29) | copy-start | bytes 12292
  128.5 3.5 %copy-start.8 = (s32[2,16]{1,0:T(2,128)S(1)}, s32[2,16]{1,0:T(2,128)}, u32[]{:S(2)}) copy-start(s32[2,16]{1,0:T(2,128)} %param.33) | copy-start | bytes 388
  128.5 3.5 %copy-start.6 = (f32[1024]{0:T(1024)S(1)}, f32[1024]{0:T(1024)}, u32[]{:S(2)}) copy-start(f32[1024]{0:T(1024)} %param.31) | copy-start | bytes 12292
  128.5 3.5 %copy-start.7 = (f32[1024]{0:T(1024)S(1)}, f32[1024]{0:T(1024)}, u32[]{:S(2)}) copy-start(f32[1024]{0:T(1024)} %param.30) | copy-start | bytes 12292
  128.5 11.3 %copy-start.9 = (s32[2]{0:T(128)S(1)}, s32[2]{0:T(128)}, u32[]{:S(2)}) copy-start(s32[2]{0:T(128)} %param.19) | copy-start | bytes 28

commit v19 on v18

--- a/solution.py
+++ b/solution.py
@@ -212,7 +212,7 @@
     lax.fori_loop(1, n, sent, 0)
 
 
-def direct_exchange(x, axes, collective_id, scatter=False):
+def direct_exchange(x, axes, collective_id, scatter=False, select=True):
     n = 1
     for name in axes:
         n *= lax.axis_size(name)
@@ -228,6 +228,8 @@
         ],
         compiler_params=pltpu.CompilerParams(collective_id=collective_id, has_side_effects=True),
     )(x)
+    if not select:
+        return received
     own = x[lax.axis_index(axes)] if scatter else x
     slot = jnp.arange(n, dtype=jnp.int32).reshape((n,) + (1,) * len(block))
     return jnp.where(slot == lax.axis_index(axes), own[None], received)
@@ -343,10 +345,15 @@
         jnp.where(is_valid[:, :, None], hidden_out.astype(jnp.float32), jnp.float32(0.0)), axis=1
     )
     pool_and_ids = direct_exchange(
-        jnp.concatenate([local_pool, cand_ids.astype(jnp.float32)], axis=1), ("tp",), 5
-    )
-    text_ids = jnp.swapaxes(pool_and_ids[:, :, model_width:], 0, 1)
-    pooled = jnp.sum(pool_and_ids[:, :, :model_width], axis=0) / lengths.astype(
+        jnp.concatenate([local_pool, cand_ids.astype(jnp.float32)], axis=1), ("tp",), 5, select=False
+    )
+    from_self = (jnp.arange(tp_count, dtype=jnp.int32) == tp_rank)[:, None, None]
+    text_ids = jnp.swapaxes(
+        jnp.where(from_self, cand_ids.astype(jnp.float32)[None], pool_and_ids[:, :, model_width:]), 0, 1
+    )
+    pooled = jnp.sum(
+        jnp.where(from_self, local_pool[None], pool_and_ids[:, :, :model_width]), axis=0
+    ) / lengths.astype(
         jnp.float32
     )[:, None]
     query_vec = (

time: 184 us -> 185 us (level)
  no operation moved by 1% of the time
where the time goes in v19:
time: 185 us
  Pallas kernels  104 us (56%)
  matrix products  39.7 us (21%)
  other arithmetic  19.3 us (10%)
  blocking collectives  17.1 us (9%)
  local copies, waits for them, and re-layouts  2.16 us (1%)
    pallas_call x2, Pallas kernels, ring_all_gather(): pl.pallas_call(functools.partial(_gather_kernel, chunks), out_shape=jax.S...  43.1 us
    pallas_call x2, Pallas kernels, ring_reduce_scatter_add(): pl.pallas_call(functools.partial(_scatter_add_kernel, chunks), out_shape=...  41.3 us
    pallas_call x2, Pallas kernels, direct_exchange(): pl.pallas_call(functools.partial(_direct_kernel, axes, scatter), out_shap...  20 us
    all_to_all x1, blocking collectives, per_device(): lax.all_to_all(owner_terms, ('req', 'tp'), 0, 0, tiled=True)  17.1 us
    dot_general x1, matrix products, per_device(): jnp.einsum('tsd,df->tsf', normed_full, w_up, preferred_element_type=jnp.f...  12.7 us
    sub x1, matrix products, window_attention(): expo = jnp.exp(logits - top_val)  7.67 us
    dot_general x1, matrix products, few_owned(): jnp.dot(row_pick.astype(index_rows.dtype), index_rows, preferred_element_...  5 us
    dot_general x1, matrix products, window_attention(): jnp.einsum('thqk,tkhe->tqhe', attn_weights, values_h, preferred_element_t...  4.29 us

profile of v19, /device:TPU:1, one launch (start us, length us, event | category | flops | bytes accessed | tf_op | source)
XLA Modules:
  0.0 184.6 jit_solution(5205815478857641311)
XLA Ops:
  2.4 21.8 %shard_map.167 = bf16[2,512,1024]{2,1,0:T(8,128)(2,1)} custom-call(bf16[2,128,1024]{2,1,0:T(8,128)(2,1)} %x_ref.1), custom_call_target="tpu_custom_call" | custom-call | tf_op jit(solution)/shard_map/pallas_call | solution.py:74
  24.2 3.9 %add_convert_fusion = bf16[2,512,3,256]{1,3,2,0:T(8,128)(2,1)S(1)} fusion(f32[3,256]{1,0:T(4,128)} %param.21, bf16[1024,3,256]{2,0,1:T(8,128)(2,1)} %param.20, bf16[2,512,1024]{2,1,0:T(8,128)(2,1)} %shard_map.167), kind=kOutput, calls=%fused_computation.54 | convolution fusion | flops 1612185600 | bytes 5245952 | tf_op jit(solution)/shard_map/tsd,dce->tsce/dot_general | solution.py:310
  28.2 1.2 fusion.48
  29.6 7.7 %fusion.49 = (f32[2,4,512]{2,1,0:T(4,128)S(1)}, f32[2,4,512,512]{2,3,1,0:T(8,128)}) fusion(pred[2,512,512]{1,2,0:T(8,128)(4,1)S(1)} %broadcast_and_fusion, bf16[2,512,4,64]{1,3,2,0:T(8,128)(2,1)} %bitcast.56, bf16[2,512,4,64]{1,3,2,0:T(8,128)(2,1)} %bitcast.55), kind=kOutput, calls=%fused_computation.109 | convolution fusion | flops 276824576 | bytes 9977856 | tf_op jit(solution)/shard_map/sub | solution.py:267
  37.3 4.3 %fusion.37 = bf16[2,4,64,512]{3,2,1,0:T(8,128)(2,1)S(1)} fusion(bf16[2,512,4,64]{1,3,2,0:T(8,128)(2,1)S(1)} %bitcast.54, f32[2,4,512,512]{2,3,1,0:T(8,128)} %get-tuple-element.56, f32[2,4,512]{2,1,0:T(4,128)S(1)} %get-tuple-element.55, pred[2,512]{1,0:T(4,128)(4,1)S(1)} %iota_compare_fusion.5), kind=kOutput, calls=%fused_computation.67 | convolution fusion | flops 273154048 | bytes 9454592 | tf_op jit(solution)/shard_map/thqk,tkhe->tqhe/dot_general | solution.py:269
  41.6 2.1 %convolution_convert_fusion.p_ref = bf16[2,512,1024]{2,1,0:T(8,128)(2,1)} fusion(bf16[2,512,256]{1,2,0:T(8,128)(2,1)S(1)} %bitcast.57, bf16[256,1024]{1,0:T(8,128)(2,1)S(1)} %copy-done.1), kind=kOutput, calls=%fused_computation.64 | convolution fusion | flops 537919488 | bytes 3145728 | tf_op jit(solution)/shard_map/tsk,kd->tsd/dot_general | solution.py:317
  43.7 20.0 %shard_map.168 = bf16[2,2,128,1024]{3,2,1,0:T(8,128)(2,1)} custom-call(bf16[2,512,1024]{2,1,0:T(8,128)(2,1)} %convolution_convert_fusion.p_ref), custom_call_target="tpu_custom_call" | custom-call | tf_op jit(solution)/shard_map/pallas_call | solution.py:141
  63.8 2.5 %convert_reduce_fusion.1 = f32[2,128,1024]{2,1,0:T(8,128)} fusion(bf16[2,2,128,1024]{3,2,1,0:T(8,128)(2,1)} %shard_map.168), kind=kLoop, calls=%fused_computation.62 | loop fusion | flops 786432 | bytes 2097152 | tf_op jit(solution)/shard_map/reduce_sum | solution.py:322
  66.3 1.8 fusion.47
  68.4 1.0 add_convert_fusion.2.x_ref
  69.4 21.3 %shard_map.169 = bf16[2,512,1024]{2,1,0:T(8,128)(2,1)} custom-call(bf16[2,128,1024]{2,1,0:T(8,128)(2,1)} %add_convert_fusion.2.x_ref), custom_call_target="tpu_custom_call" | custom-call | tf_op jit(solution)/shard_map/pallas_call | solution.py:74
  90.8 12.7 %fusion.8 = bf16[2,512,1024]{2,1,0:T(8,128)(2,1)S(1)} fusion(f32[1024]{0:T(1024)S(1)} %copy-done.11, bf16[2,512,1024]{2,1,0:T(8,128)(2,1)} %shard_map.169, bf16[1024,1024]{1,0:T(8,128)(2,1)S(1)} %copy-done), kind=kOutput, calls=%fused_computation.34 | convolution fusion | flops 2216689664 | bytes 6295552 | tf_op jit(solution)/shard_map/tsd,df->tsf/dot_general | solution.py:328
  103.6 3.7 %fusion.26.p_ref = bf16[2,512,1024]{2,1,0:T(8,128)(2,1)} fusion(bf16[2,512,1024]{2,1,0:T(8,128)(2,1)S(1)} %fusion.8, bf16[1024,1024]{1,0:T(8,128)(2,1)S(1)} %copy-done.10), kind=kOutput, calls=%fused_computation.63 | convolution fusion | flops 2148532224 | bytes 6291456 | tf_op jit(solution)/shard_map/tsf,fd->tsd/dot_general | solution.py:332
  107.3 21.2 %shard_map.170 = bf16[2,2,128,1024]{3,2,1,0:T(8,128)(2,1)} custom-call(bf16[2,512,1024]{2,1,0:T(8,128)(2,1)} %fusion.26.p_ref), custom_call_target="tpu_custom_call" | custom-call | tf_op jit(solution)/shard_map/pallas_call | solution.py:141
  128.5 1.6 convert_reduce_fusion
  130.1 1.5 fusion.46
  132.0 1.2 select_reduce_fusion.4
  133.7 5.2 %shard_map.171 = f32[4,2,1040]{2,1,0:T(2,128)} custom-call(f32[2,1040]{1,0:T(2,128)} %pad_maximum_fusion.x_ref), custom_call_target="tpu_custom_call" | custom-call | tf_op jit(solution)/shard_map/pallas_call | solution.py:220
  139.7 0.9 select_reduce_fusion.5
  141.6 14.8 %shard_map.172 = f32[32,2,1088]{2,1,0:T(2,128)} custom-call(f32[2,1088]{1,0:T(2,128)} %pad_maximum_fusion.1.x_ref), custom_call_target="tpu_custom_call" | custom-call | tf_op jit(solution)/shard_map/pallas_call | solution.py:220
  156.4 1.1 broadcast_select_fusion
  159.1 7.5 %conditional.1 = (f32[64,64]{1,0:T(8,128)S(1)}) conditional(s32[]{:T(128)} %convert_element_type.98, (s32[64,64]{1,0:T(8,128)S(1)}, bf16[4096,1024]{1,0:T(8,128)(2,1)}, bf16[64,1024]{1,0:T(8,128)(2,1)S(1)}, pred[64,64]{1,0:T(8,128)(4,1)S(1)}) %tuple.14, (pred[64,64]{1,0:T(8,128)(4,1)S(1)}, s32[64,64]{1,0:T(8,128)S(1)}, ...), branch_computations={%region_12.14_spmd, %region_14.21_spmd} | conditional | flops 548545344 | bytes 12955656 | solution.py:408
  160.8 5.0 %fusion.1 = f32[64,1024]{1,0:T(8,128)S(1)} fusion(bf16[4096,1024]{1,0:T(8,128)(2,1)} %get-tuple-element.25, s32[64]{0:T(128)S(1)} %get-tuple-element.38), kind=kOutput, calls=%fused_computation.14 | convolution fusion | flops 537133056 | bytes 8651008 | tf_op jit(solution)/shard_map/cond/branch_1_fun/dot_general | solution.py:387
  166.8 17.1 %all_to_all.5 = f32[128,2,16]{2,1,0:T(2,128)S(1)} all-to-all(f32[128,2,16]{2,1,0:T(2,128)S(1)} %copy.46), channel_id=1, replica_groups=mesh['req'=32,'tp'=4] {'req','tp'}, dimensions={0} | all-to-all | bytes 32768 | tf_op jit(solution)/shard_map/all_to_all | solution.py:414
  (69 shorter events, 9.0 us)
Async XLA Ops:
  0.6 90.2 %copy-start = (bf16[1024,1024]{1,0:T(8,128)(2,1)S(1)}, bf16[1024,1024]{1,0:T(8,128)(2,1)}, u32[]{:S(2)}) copy-start(bf16[1024,1024]{1,0:T(8,128)(2,1)} %param.26) | copy-start | bytes 6291460
  37.3 4.3 %copy-start.1 = (bf16[256,1024]{1,0:T(8,128)(2,1)S(1)}, bf16[256,1024]{1,0:T(8,128)(2,1)}, u32[]{:S(2)}) copy-start(bf16[256,1024]{1,0:T(8,128)(2,1)} %param.22) | copy-start | bytes 1572868
  41.6 24.7 %copy-start.4 = (f32[1024]{0:T(1024)S(1)}, f32[1024]{0:T(1024)}, u32[]{:S(2)}) copy-start(f32[1024]{0:T(1024)} %param.23) | copy-start | bytes 12292
  43.7 24.7 %copy-start.2 = (f32[1024]{0:T(1024)S(1)}, f32[1024]{0:T(1024)}, u32[]{:S(2)}) copy-start(f32[1024]{0:T(1024)} %param.25) | copy-start | bytes 12292
  43.7 24.7 %copy-start.3 = (f32[1024]{0:T(1024)S(1)}, f32[1024]{0:T(1024)}, u32[]{:S(2)}) copy-start(f32[1024]{0:T(1024)} %param.24) | copy-start | bytes 12292
  66.3 24.5 %copy-start.11 = (f32[1024]{0:T(1024)S(1)}, f32[1024]{0:T(1024)}, u32[]{:S(2)}) copy-start(f32[1024]{0:T(1024)} %param.27) | copy-start | bytes 12292
  90.8 12.7 %copy-start.10 = (bf16[1024,1024]{1,0:T(8,128)(2,1)S(1)}, bf16[1024,1024]{1,0:T(8,128)(2,1)}, u32[]{:S(2)}) copy-start(bf16[1024,1024]{1,0:T(8,128)(2,1)} %param.28) | copy-start | bytes 6291460
  107.3 22.9 %copy-start.5 = (f32[1024]{0:T(1024)S(1)}, f32[1024]{0:T(1024)}, u32[]{:S(2)}) copy-start(f32[1024]{0:T(1024)} %param.29) | copy-start | bytes 12292
  128.5 3.5 %copy-start.8 = (s32[2,16]{1,0:T(2,128)S(1)}, s32[2,16]{1,0:T(2,128)}, u32[]{:S(2)}) copy-start(s32[2,16]{1,0:T(2,128)} %param.33) | copy-start | bytes 388
  128.5 3.5 %copy-start.6 = (f32[1024]{0:T(1024)S(1)}, f32[1024]{0:T(1024)}, u32[]{:S(2)}) copy-start(f32[1024]{0:T(1024)} %param.31) | copy-start | bytes 12292
  128.5 3.5 %copy-start.7 = (f32[1024]{0:T(1024)S(1)}, f32[1024]{0:T(1024)}, u32[]{:S(2)}) copy-start(f32[1024]{0:T(1024)} %param.30) | copy-start | bytes 12292
  128.5 12.0 %copy-start.9 = (s32[2]{0:T(128)S(1)}, s32[2]{0:T(128)}, u32[]{:S(2)}) copy-start(s32[2]{0:T(128)} %param.19) | copy-start | bytes 28

commit v20 on v18

--- a/solution.py
+++ b/solution.py
@@ -234,7 +234,7 @@
 
 
 HEAD_DIM = 64
-RING_CHUNKS = 2
+RING_CHUNKS = 4
 SPARSE_PAIRS = 64
 WINDOW = 512
 

time: 184 us -> 185 us (level)
  no operation moved by 1% of the time
where the time goes in v20:
time: 185 us; the launch traced here: 184 us
  Pallas kernels  105 us (57%)
  matrix products  39.7 us (21%)
  other arithmetic  18.6 us (10%)
  blocking collectives  17 us (9%)
  local copies, waits for them, and re-layouts  2.16 us (1%)
    pallas_call x2, Pallas kernels, ring_all_gather(): pl.pallas_call(functools.partial(_gather_kernel, chunks), out_shape=jax.S...  43.1 us
    pallas_call x2, Pallas kernels, ring_reduce_scatter_add(): pl.pallas_call(functools.partial(_scatter_add_kernel, chunks), out_shape=...  41 us
    pallas_call x2, Pallas kernels, direct_exchange(): pl.pallas_call(functools.partial(_direct_kernel, axes, scatter), out_shap...  20.8 us
    all_to_all x1, blocking collectives, per_device(): lax.all_to_all(owner_terms, ('req', 'tp'), 0, 0, tiled=True)  17 us
    dot_general x1, matrix products, per_device(): jnp.einsum('tsd,df->tsf', normed_full, w_up, preferred_element_type=jnp.f...  12.7 us
    sub x1, matrix products, window_attention(): expo = jnp.exp(logits - top_val)  7.67 us
    dot_general x1, matrix products, few_owned(): jnp.dot(row_pick.astype(index_rows.dtype), index_rows, preferred_element_...  5 us
    dot_general x1, matrix products, window_attention(): jnp.einsum('thqk,tkhe->tqhe', attn_weights, values_h, preferred_element_t...  4.29 us

profile of v20, /device:TPU:1, one launch (start us, length us, event | category | flops | bytes accessed | tf_op | source)
XLA Modules:
  0.0 184.3 jit_solution(16953562421383845387)
XLA Ops:
  2.4 21.9 %shard_map.167 = bf16[2,512,1024]{2,1,0:T(8,128)(2,1)} custom-call(bf16[2,128,1024]{2,1,0:T(8,128)(2,1)} %x_ref.1), custom_call_target="tpu_custom_call" | custom-call | tf_op jit(solution)/shard_map/pallas_call | solution.py:74
  24.4 3.9 %add_convert_fusion = bf16[2,512,3,256]{1,3,2,0:T(8,128)(2,1)S(1)} fusion(f32[3,256]{1,0:T(4,128)} %param.21, bf16[1024,3,256]{2,0,1:T(8,128)(2,1)} %param.20, bf16[2,512,1024]{2,1,0:T(8,128)(2,1)} %shard_map.167), kind=kOutput, calls=%fused_computation.54 | convolution fusion | flops 1612185600 | bytes 5245952 | tf_op jit(solution)/shard_map/tsd,dce->tsce/dot_general | solution.py:308
  28.3 1.2 fusion.48
  29.8 7.7 %fusion.49 = (f32[2,4,512]{2,1,0:T(4,128)S(1)}, f32[2,4,512,512]{2,3,1,0:T(8,128)}) fusion(pred[2,512,512]{1,2,0:T(8,128)(4,1)S(1)} %broadcast_and_fusion, bf16[2,512,4,64]{1,3,2,0:T(8,128)(2,1)} %bitcast.56, bf16[2,512,4,64]{1,3,2,0:T(8,128)(2,1)} %bitcast.55), kind=kOutput, calls=%fused_computation.110 | convolution fusion | flops 276824576 | bytes 9977856 | tf_op jit(solution)/shard_map/sub | solution.py:265
  37.4 4.3 %fusion.37 = bf16[2,4,64,512]{3,2,1,0:T(8,128)(2,1)S(1)} fusion(bf16[2,512,4,64]{1,3,2,0:T(8,128)(2,1)S(1)} %bitcast.54, f32[2,4,512,512]{2,3,1,0:T(8,128)} %get-tuple-element.56, f32[2,4,512]{2,1,0:T(4,128)S(1)} %get-tuple-element.55, pred[2,512]{1,0:T(4,128)(4,1)S(1)} %iota_compare_fusion.5), kind=kOutput, calls=%fused_computation.67 | convolution fusion | flops 273154048 | bytes 9454592 | tf_op jit(solution)/shard_map/thqk,tkhe->tqhe/dot_general | solution.py:267
  41.7 2.1 %convolution_convert_fusion.p_ref = bf16[2,512,1024]{2,1,0:T(8,128)(2,1)} fusion(bf16[2,512,256]{1,2,0:T(8,128)(2,1)S(1)} %bitcast.57, bf16[256,1024]{1,0:T(8,128)(2,1)S(1)} %copy-done.1), kind=kOutput, calls=%fused_computation.64 | convolution fusion | flops 537919488 | bytes 3145728 | tf_op jit(solution)/shard_map/tsk,kd->tsd/dot_general | solution.py:315
  43.8 20.2 %shard_map.168 = bf16[2,2,128,1024]{3,2,1,0:T(8,128)(2,1)} custom-call(bf16[2,512,1024]{2,1,0:T(8,128)(2,1)} %convolution_convert_fusion.p_ref), custom_call_target="tpu_custom_call" | custom-call | tf_op jit(solution)/shard_map/pallas_call | solution.py:141
  64.0 2.5 %convert_reduce_fusion.1 = f32[2,128,1024]{2,1,0:T(8,128)} fusion(bf16[2,2,128,1024]{3,2,1,0:T(8,128)(2,1)} %shard_map.168), kind=kLoop, calls=%fused_computation.62 | loop fusion | flops 786432 | bytes 2097152 | tf_op jit(solution)/shard_map/reduce_sum | solution.py:320
  66.5 1.8 fusion.47
  68.6 1.0 add_convert_fusion.2.x_ref
  69.7 21.2 %shard_map.169 = bf16[2,512,1024]{2,1,0:T(8,128)(2,1)} custom-call(bf16[2,128,1024]{2,1,0:T(8,128)(2,1)} %add_convert_fusion.2.x_ref), custom_call_target="tpu_custom_call" | custom-call | tf_op jit(solution)/shard_map/pallas_call | solution.py:74
  90.9 12.7 %fusion.8 = bf16[2,512,1024]{2,1,0:T(8,128)(2,1)S(1)} fusion(f32[1024]{0:T(1024)S(1)} %copy-done.11, bf16[2,512,1024]{2,1,0:T(8,128)(2,1)} %shard_map.169, bf16[1024,1024]{1,0:T(8,128)(2,1)S(1)} %copy-done), kind=kOutput, calls=%fused_computation.34 | convolution fusion | flops 2216689664 | bytes 6295552 | tf_op jit(solution)/shard_map/tsd,df->tsf/dot_general | solution.py:326
  103.6 3.7 %fusion.26.p_ref = bf16[2,512,1024]{2,1,0:T(8,128)(2,1)} fusion(bf16[2,512,1024]{2,1,0:T(8,128)(2,1)S(1)} %fusion.8, bf16[1024,1024]{1,0:T(8,128)(2,1)S(1)} %copy-done.10), kind=kOutput, calls=%fused_computation.63 | convolution fusion | flops 2148532224 | bytes 6291456 | tf_op jit(solution)/shard_map/tsf,fd->tsd/dot_general | solution.py:330
  107.3 20.9 %shard_map.170 = bf16[2,2,128,1024]{3,2,1,0:T(8,128)(2,1)} custom-call(bf16[2,512,1024]{2,1,0:T(8,128)(2,1)} %fusion.26.p_ref), custom_call_target="tpu_custom_call" | custom-call | tf_op jit(solution)/shard_map/pallas_call | solution.py:141
  128.3 1.6 convert_reduce_fusion
  129.8 1.5 fusion.46
  131.7 1.2 select_reduce_fusion.4
  133.5 6.0 %shard_map.171 = f32[4,2,1040]{2,1,0:T(2,128)} custom-call(f32[2,1040]{1,0:T(2,128)} %pad_maximum_fusion.x_ref), custom_call_target="tpu_custom_call" | custom-call | tf_op jit(solution)/shard_map/pallas_call | solution.py:220
  139.4 0.9 broadcast_select_fusion.1
  141.4 14.8 %shard_map.172 = f32[32,2,1088]{2,1,0:T(2,128)} custom-call(f32[2,1088]{1,0:T(2,128)} %pad_maximum_fusion.1.x_ref), custom_call_target="tpu_custom_call" | custom-call | tf_op jit(solution)/shard_map/pallas_call | solution.py:220
  156.2 1.1 broadcast_select_fusion
  158.9 7.5 %conditional.1 = (f32[64,64]{1,0:T(8,128)S(1)}) conditional(s32[]{:T(128)} %convert_element_type.97, (s32[64,64]{1,0:T(8,128)S(1)}, bf16[4096,1024]{1,0:T(8,128)(2,1)}, bf16[64,1024]{1,0:T(8,128)(2,1)S(1)}, pred[64,64]{1,0:T(8,128)(4,1)S(1)}) %tuple.14, (pred[64,64]{1,0:T(8,128)(4,1)S(1)}, s32[64,64]{1,0:T(8,128)S(1)}, ...), branch_computations={%region_12.14_spmd, %region_14.21_spmd} | conditional | flops 548545344 | bytes 12955656 | solution.py:401
  160.6 5.0 %fusion.1 = f32[64,1024]{1,0:T(8,128)S(1)} fusion(bf16[4096,1024]{1,0:T(8,128)(2,1)} %get-tuple-element.25, s32[64]{0:T(128)S(1)} %get-tuple-element.38), kind=kOutput, calls=%fused_computation.14 | convolution fusion | flops 537133056 | bytes 8651008 | tf_op jit(solution)/shard_map/cond/branch_1_fun/dot_general | solution.py:380
  166.6 17.0 %all_to_all.5 = f32[128,2,16]{2,1,0:T(2,128)S(1)} all-to-all(f32[128,2,16]{2,1,0:T(2,128)S(1)} %copy.46), channel_id=1, replica_groups=mesh['req'=32,'tp'=4] {'req','tp'}, dimensions={0} | all-to-all | bytes 32768 | tf_op jit(solution)/shard_map/all_to_all | solution.py:407
  (70 shorter events, 8.3 us)
Async XLA Ops:
  0.6 90.2 %copy-start = (bf16[1024,1024]{1,0:T(8,128)(2,1)S(1)}, bf16[1024,1024]{1,0:T(8,128)(2,1)}, u32[]{:S(2)}) copy-start(bf16[1024,1024]{1,0:T(8,128)(2,1)} %param.26) | copy-start | bytes 6291460
  37.4 4.3 %copy-start.1 = (bf16[256,1024]{1,0:T(8,128)(2,1)S(1)}, bf16[256,1024]{1,0:T(8,128)(2,1)}, u32[]{:S(2)}) copy-start(bf16[256,1024]{1,0:T(8,128)(2,1)} %param.22) | copy-start | bytes 1572868
  41.7 24.8 %copy-start.4 = (f32[1024]{0:T(1024)S(1)}, f32[1024]{0:T(1024)}, u32[]{:S(2)}) copy-start(f32[1024]{0:T(1024)} %param.23) | copy-start | bytes 12292
  43.8 24.8 %copy-start.2 = (f32[1024]{0:T(1024)S(1)}, f32[1024]{0:T(1024)}, u32[]{:S(2)}) copy-start(f32[1024]{0:T(1024)} %param.25) | copy-start | bytes 12292
  43.8 24.8 %copy-start.3 = (f32[1024]{0:T(1024)S(1)}, f32[1024]{0:T(1024)}, u32[]{:S(2)}) copy-start(f32[1024]{0:T(1024)} %param.24) | copy-start | bytes 12292
  66.5 24.4 %copy-start.11 = (f32[1024]{0:T(1024)S(1)}, f32[1024]{0:T(1024)}, u32[]{:S(2)}) copy-start(f32[1024]{0:T(1024)} %param.27) | copy-start | bytes 12292
  90.9 12.7 %copy-start.10 = (bf16[1024,1024]{1,0:T(8,128)(2,1)S(1)}, bf16[1024,1024]{1,0:T(8,128)(2,1)}, u32[]{:S(2)}) copy-start(bf16[1024,1024]{1,0:T(8,128)(2,1)} %param.28) | copy-start | bytes 6291460
  107.3 22.5 %copy-start.5 = (f32[1024]{0:T(1024)S(1)}, f32[1024]{0:T(1024)}, u32[]{:S(2)}) copy-start(f32[1024]{0:T(1024)} %param.29) | copy-start | bytes 12292
  128.2 3.5 %copy-start.8 = (s32[2,16]{1,0:T(2,128)S(1)}, s32[2,16]{1,0:T(2,128)}, u32[]{:S(2)}) copy-start(s32[2,16]{1,0:T(2,128)} %param.33) | copy-start | bytes 388
  128.2 3.5 %copy-start.6 = (f32[1024]{0:T(1024)S(1)}, f32[1024]{0:T(1024)}, u32[]{:S(2)}) copy-start(f32[1024]{0:T(1024)} %param.31) | copy-start | bytes 12292
  128.2 3.5 %copy-start.7 = (f32[1024]{0:T(1024)S(1)}, f32[1024]{0:T(1024)}, u32[]{:S(2)}) copy-start(f32[1024]{0:T(1024)} %param.30) | copy-start | bytes 12292
  128.2 12.1 %copy-start.9 = (s32[2]{0:T(128)S(1)}, s32[2]{0:T(128)}, u32[]{:S(2)}) copy-start(s32[2]{0:T(128)} %param.19) | copy-start | bytes 28
